TPU v7x, 32 devices: a whole 2x2x4 slice. The times are simulated.
32 devices in a mesh: dp: 8 (over y, x, core), tensor: 4 (over z).
Axes of the slice: x: 2, y: 2, z: 4, core: 2. Of those that a mesh axis runs over, the one named last changes fastest.
Arguments:
- block_in: bfloat16 [8, 2048, 1024], P('dp', 'tensor'), may hold values from -6 to 6
- segments: int32 [8, 2048], P('dp'), may hold values from 0 to 15, never falling along the last dimension, each value on 1 to 512 neighbouring positions
- retrieved: int32 [8, 4, 8], P('dp'), may hold values from 0 to 255, as said below
- partner: int32 [8], P('dp'), may hold values from 0 to 7, as said below
- memory_keys: bfloat16 [8, 128, 128, 1024], P(None, 'dp', None, 'tensor'), may hold values from -6 to 6
- memory_values: bfloat16 [8, 128, 128, 1024], P(None, 'dp', None, 'tensor'), may hold values from -6 to 6
- gain_attn: bfloat16 [1024], P('dp'), may hold values from 0.5 to 1.5
- w_query: bfloat16 [1024, 1024], P('dp', 'tensor'), may hold values from -0.375 to 0.375
- w_key: bfloat16 [1024, 1024], P('dp', 'tensor'), may hold values from -0.1875 to 0.1875
- w_value: bfloat16 [1024, 1024], P('dp', 'tensor'), may hold values from -0.1875 to 0.1875
- w_out: bfloat16 [1024, 1024], P('tensor', 'dp'), may hold values from -2 to 2
- gain_ffn: bfloat16 [1024], P('dp'), may hold values from 0.5 to 1.5
- w_gate: bfloat16 [1024, 2816], P('dp', 'tensor'), may hold values from -0.1875 to 0.1875
- w_up: bfloat16 [1024, 2816], P('dp', 'tensor'), may hold values from -0.1875 to 0.1875
- w_down: bfloat16 [2816, 1024], P('tensor', 'dp'), may hold values from -0.21875 to 0.21875
- cotangent: bfloat16 [8, 2048, 1024], P('dp', 'tensor'), may hold values from -6 to 6
Outputs:
- block_out: float32 [8, 2048, 1024], P('dp', 'tensor')
- grad_in: float32 [8, 2048, 1024], P('dp', 'tensor')
- grad_gain_attn: float32 [1024], P('dp')
- grad_query: float32 [1024, 1024], P('dp', 'tensor')
- grad_key: float32 [1024, 1024], P('dp', 'tensor')
- grad_value: float32 [1024, 1024], P('dp', 'tensor')
- grad_out: float32 [1024, 1024], P('tensor', 'dp')
- grad_gain_ffn: float32 [1024], P('dp')
- grad_gate: float32 [1024, 2816], P('dp', 'tensor')
- grad_up: float32 [1024, 2816], P('dp', 'tensor')
- grad_down: float32 [2816, 1024], P('tensor', 'dp')
Inputs may be any that keep to these rules, and one draw needn't show every extreme that they name: `retrieved`: entry v names block v of the combined memory: below 128 the sequence's own block v, else the partner's block v - 128. Block j of any sequence lies on data device j // 16. All 32 entries of one sequence are different, at most 8 of them name blocks on one data device, and for some device exactly 8. partner[s] differs from s.
All inputs are finite; a program needn't handle non-finite values.
Results may differ from a plain program's by a relative error of at most 0.025.
Values may be sent and summed in bfloat16 or wider, within the bound.
A program may use at most 192 MiB of HBM per device.

v0:
```python
import jax
import jax.numpy as jnp
from jax import lax
from jax.sharding import PartitionSpec as P

HEADS = 8
HD = 128
QB = 512
MEMB = 128


EPSILON = 1e-05
MASKED = -1e30


def normalize(field, gain_vec):
    return field * lax.rsqrt(jnp.mean(field * field, axis=-1, keepdims=True) + EPSILON) * gain_vec


def rotate(field, heads_here):
    row_total = field.shape[0]
    head_size = field.shape[1] // heads_here
    half_width = head_size // 2
    frequencies = 10000.0 ** (-jnp.arange(half_width, dtype=jnp.float32) * 2.0 / head_size)
    angles = jnp.arange(row_total, dtype=jnp.float32)[:, None] * frequencies[None, :]
    cosine = jnp.cos(angles)[:, None, :]
    sine_table = jnp.sin(angles)[:, None, :]
    split_heads = field.reshape(row_total, heads_here, head_size)
    first_half = split_heads[..., :half_width]
    second_half = split_heads[..., half_width:]
    turned = jnp.concatenate(
        [
            first_half * cosine - second_half * sine_table,
            second_half * cosine + first_half * sine_table,
        ],
        axis=-1,
    )
    return turned.reshape(row_total, heads_here * head_size)


def contract_rows(left, right):
    return lax.dot_general(
        left, right, (((0,), (0,)), ((), ())), preferred_element_type=jnp.float32
    )


def against(left, right):
    return lax.dot_general(
        left, right, (((1,), (1,)), ((), ())), preferred_element_type=jnp.float32
    )


def spread_rows(local_rows, matrices):
    piece_rows = lax.all_gather(local_rows, "tensor", axis=0, tiled=True)
    return jnp.concatenate(
        [jnp.dot(piece_rows, matrix, preferred_element_type=jnp.float32) for matrix in matrices],
        axis=1,
    )


def reduce_rows(left, right):
    return lax.psum_scatter(
        jnp.dot(left, right, preferred_element_type=jnp.float32).astype(jnp.bfloat16),
        "tensor",
        scatter_dimension=0,
        tiled=True,
    ).astype(jnp.float32)


def return_rows(pairs):
    summed = against(pairs[0][0], pairs[0][1])
    for grad_block, matrix in pairs[1:]:
        summed = summed + against(grad_block, matrix)
    return lax.psum_scatter(
        summed.astype(jnp.bfloat16), "tensor", scatter_dimension=0, tiled=True
    ).astype(jnp.float32)


def weight_grads(local_rows, grads_list):
    piece_rows = lax.all_gather(local_rows, "tensor", axis=0, tiled=True)
    return tuple((contract_rows(piece_rows, grad_one) for grad_one in grads_list))


def all_rows(local_grad):
    return lax.all_gather(local_grad, "tensor", axis=0, tiled=True)


def on_device(
    block_in,
    segments,
    retrieved,
    partner,
    memory_keys,
    memory_values,
    gain_attn,
    w_query,
    w_key,
    w_value,
    w_out,
    gain_ffn,
    w_gate,
    w_up,
    w_down,
    cotangent,
):
    tensor_size = lax.axis_size("tensor")
    dp_size = lax.axis_size("dp")
    heads_here = HEADS // tensor_size
    head_width = heads_here * HD
    score_scale = HD ** (-0.5)
    seq_len = segments.shape[1]
    query_blocks = seq_len // QB
    stream_in = block_in[0].astype(jnp.float32)
    seg_row = segments[0]
    positions = jnp.arange(seq_len)
    gathered = (
        lax.all_gather(gain_attn, "dp", axis=0, tiled=True),
        lax.all_gather(w_query, "dp", axis=0, tiled=True),
        lax.all_gather(w_key, "dp", axis=0, tiled=True),
        lax.all_gather(w_value, "dp", axis=0, tiled=True),
        lax.all_gather(w_out, "dp", axis=1, tiled=True),
        lax.all_gather(gain_ffn, "dp", axis=0, tiled=True),
        lax.all_gather(w_gate, "dp", axis=0, tiled=True),
        lax.all_gather(w_up, "dp", axis=0, tiled=True),
        lax.all_gather(w_down, "dp", axis=1, tiled=True),
    )
    gain_one, query_w, key_w, value_w, out_w, gain_two, gate_w, up_w, down_w = gathered
    wanted = retrieved[0].reshape(-1)
    request_total = wanted.shape[0]
    capacity = max(2, (2 * request_total + dp_size - 1) // dp_size)
    blocks_dev = memory_keys.shape[1]
    from_partner = wanted // MEMB
    block_index = wanted % MEMB
    owner_dev = block_index // blocks_dev
    local_block = block_index % blocks_dev
    seq_id = jnp.where(from_partner == 0, lax.axis_index("dp"), partner[0])
    owner_hits = (owner_dev[:, None] == jnp.arange(dp_size)[None, :]).astype(jnp.int32)
    slot_index = jnp.sum((jnp.cumsum(owner_hits, axis=0) - 1) * owner_hits, axis=1)
    requests = (
        jnp.zeros((dp_size, capacity, 2), jnp.int32)
        .at[owner_dev, slot_index]
        .set(jnp.stack([seq_id, local_block], axis=-1))
    )
    received = lax.all_to_all(requests, "dp", split_axis=0, concat_axis=0, tiled=True)
    picked_keys = memory_keys[received[..., 0], received[..., 1]]
    picked_values = memory_values[received[..., 0], received[..., 1]]
    fetched_keys = lax.all_to_all(picked_keys, "dp", split_axis=0, concat_axis=0, tiled=True)
    fetched_values = lax.all_to_all(picked_values, "dp", split_axis=0, concat_axis=0, tiled=True)
    memory_k = fetched_keys[owner_dev, slot_index].reshape(query_blocks, -1, heads_here, HD)
    memory_v = fetched_values[owner_dev, slot_index].reshape(query_blocks, -1, heads_here, HD)
    normed = normalize(stream_in, gain_one.astype(jnp.float32)).astype(jnp.bfloat16)
    qkv_rows = spread_rows(normed, [query_w, key_w, value_w])
    query_raw = qkv_rows[:, :head_width]
    key_raw = qkv_rows[:, head_width : 2 * head_width]
    queries = rotate(query_raw, heads_here).astype(jnp.bfloat16)
    keys_all = rotate(key_raw, heads_here).astype(jnp.bfloat16).reshape(seq_len, heads_here, HD)
    values_all = qkv_rows[:, 2 * head_width :].astype(jnp.bfloat16).reshape(seq_len, heads_here, HD)
    query_tiles = queries.reshape(query_blocks, QB, heads_here, HD)
    seg_tiles = seg_row.reshape(query_blocks, QB)
    pos_tiles = positions.reshape(query_blocks, QB)

    def scores_of(query_blk, seg_blk, pos_blk, key_mem):
        local_scores = jnp.einsum(
            "qhd,khd->hqk", query_blk, keys_all, preferred_element_type=jnp.float32
        )
        memory_scores = jnp.einsum(
            "qhd,khd->hqk", query_blk, key_mem, preferred_element_type=jnp.float32
        )
        raw_scores = jnp.concatenate([local_scores, memory_scores], axis=-1) * score_scale
        allowed = (seg_blk[:, None] == seg_row[None, :]) & (positions[None, :] <= pos_blk[:, None])
        allowed = jnp.concatenate(
            [allowed, jnp.ones((query_blk.shape[0], key_mem.shape[0]), dtype=jnp.bool_)], axis=1
        )
        return (raw_scores, allowed)

    def forward_block(pieces):
        query_blk, seg_blk, pos_blk, key_mem, value_mem = pieces
        raw_scores, allowed = scores_of(query_blk, seg_blk, pos_blk, key_mem)
        masked = jnp.where(allowed[None], raw_scores, MASKED)
        row_max = jnp.max(masked, axis=-1, keepdims=True)
        expo = jnp.exp(masked - row_max)
        row_total = jnp.sum(expo, axis=-1, keepdims=True)
        weights_soft = (expo / row_total).astype(jnp.bfloat16)
        values_both = jnp.concatenate([values_all, value_mem], axis=0)
        result = jnp.einsum(
            "hqk,khd->qhd", weights_soft, values_both, preferred_element_type=jnp.float32
        )
        return (result, (row_max + jnp.log(row_total))[..., 0])

    attended, log_totals = lax.map(
        forward_block, (query_tiles, seg_tiles, pos_tiles, memory_k, memory_v)
    )
    mixed = attended.reshape(seq_len, head_width).astype(jnp.bfloat16)
    stream = stream_in + reduce_rows(mixed, out_w)
    normed_ffn = normalize(stream, gain_two.astype(jnp.float32)).astype(jnp.bfloat16)
    gate_up = spread_rows(normed_ffn, [gate_w, up_w])
    hidden_width = gate_w.shape[1]
    gate_pre = gate_up[:, :hidden_width]
    up_pre = gate_up[:, hidden_width:]
    hidden = (jax.nn.silu(gate_pre) * up_pre).astype(jnp.bfloat16)
    block_out = stream + reduce_rows(hidden, down_w)
    gathered_back = (
        lax.all_gather(gain_attn, "dp", axis=0, tiled=True),
        lax.all_gather(w_query, "dp", axis=0, tiled=True),
        lax.all_gather(w_key, "dp", axis=0, tiled=True),
        lax.all_gather(w_value, "dp", axis=0, tiled=True),
        lax.all_gather(w_out, "dp", axis=1, tiled=True),
        lax.all_gather(gain_ffn, "dp", axis=0, tiled=True),
        lax.all_gather(w_gate, "dp", axis=0, tiled=True),
        lax.all_gather(w_up, "dp", axis=0, tiled=True),
        lax.all_gather(w_down, "dp", axis=1, tiled=True),
    )
    gain_one, query_w, key_w, value_w, out_w, gain_two, gate_w, up_w, down_w = gathered_back
    dout_rows = cotangent[0]

    def gated(gate_in, up_in):
        return jax.nn.silu(gate_in) * up_in

    dout_full = all_rows(dout_rows)
    grad_down = contract_rows(hidden, dout_full)
    d_hidden = against(dout_full, down_w)
    gated_value, pull_gated = jax.vjp(gated, gate_pre, up_pre)
    d_gate, d_up = pull_gated(d_hidden)
    d_gate = d_gate.astype(jnp.bfloat16)
    d_up = d_up.astype(jnp.bfloat16)
    d_norm_ffn = return_rows([(d_gate, gate_w), (d_up, up_w)])
    grad_gate, grad_up = weight_grads(normed_ffn, [d_gate, d_up])
    norm_value, pull_norm_ffn = jax.vjp(normalize, stream, gain_two.astype(jnp.float32))
    d_stream_norm, grad_gain_ffn = pull_norm_ffn(d_norm_ffn)
    d_stream = dout_rows.astype(jnp.float32) + d_stream_norm
    d_stream_full = all_rows(d_stream.astype(jnp.bfloat16))
    grad_out = contract_rows(mixed, d_stream_full)
    d_mixed = against(d_stream_full, out_w).astype(jnp.bfloat16)
    d_mixed_tiles = d_mixed.reshape(query_blocks, QB, heads_here, HD)

    def backward_block(carry_sums, pieces):
        key_sum, value_sum = carry_sums
        query_blk, seg_blk, pos_blk, key_mem, value_mem, log_blk, grad_blk = pieces
        raw_scores, allowed = scores_of(query_blk, seg_blk, pos_blk, key_mem)
        probs = jnp.where(allowed[None], jnp.exp(raw_scores - log_blk[..., None]), 0.0)
        values_both = jnp.concatenate([values_all, value_mem], axis=0)
        d_probs = jnp.einsum(
            "qhd,khd->hqk", grad_blk, values_both, preferred_element_type=jnp.float32
        )
        shared = jnp.sum(probs * d_probs, axis=-1, keepdims=True)
        d_scores = (probs * (d_probs - shared)).astype(jnp.bfloat16)
        probs_low = probs.astype(jnp.bfloat16)
        keys_both = jnp.concatenate([keys_all, key_mem], axis=0)
        d_query = (
            jnp.einsum("hqk,khd->qhd", d_scores, keys_both, preferred_element_type=jnp.float32)
            * score_scale
        )
        key_sum = (
            key_sum
            + jnp.einsum(
                "hqk,qhd->khd",
                d_scores[..., :seq_len],
                query_blk,
                preferred_element_type=jnp.float32,
            )
            * score_scale
        )
        value_sum = value_sum + jnp.einsum(
            "hqk,qhd->khd", probs_low[..., :seq_len], grad_blk, preferred_element_type=jnp.float32
        )
        return ((key_sum, value_sum), d_query)

    zero_grads = jnp.zeros((seq_len, heads_here, HD), jnp.float32)
    (d_keys, d_values), d_queries = lax.scan(
        backward_block,
        (zero_grads, zero_grads),
        (query_tiles, seg_tiles, pos_tiles, memory_k, memory_v, log_totals, d_mixed_tiles),
    )

    def turn(field):
        return rotate(field, heads_here)

    turned_value, pull_turn = jax.vjp(turn, query_raw)
    d_query_raw = pull_turn(d_queries.reshape(seq_len, head_width))[0].astype(jnp.bfloat16)
    d_key_raw = pull_turn(d_keys.reshape(seq_len, head_width))[0].astype(jnp.bfloat16)
    d_value_raw = d_values.reshape(seq_len, head_width).astype(jnp.bfloat16)
    d_norm_attn = return_rows([(d_query_raw, query_w), (d_key_raw, key_w), (d_value_raw, value_w)])
    grad_query, grad_key, grad_value = weight_grads(normed, [d_query_raw, d_key_raw, d_value_raw])
    norm_first, pull_norm_attn = jax.vjp(normalize, stream_in, gain_one.astype(jnp.float32))
    d_input_norm, grad_gain_attn = pull_norm_attn(d_norm_attn)
    grad_in = d_stream + d_input_norm
    grad_gain_attn, grad_gain_ffn = lax.psum((grad_gain_attn, grad_gain_ffn), "tensor")
    results = (
        lax.psum_scatter(
            grad_gain_attn.astype(jnp.bfloat16), "dp", scatter_dimension=0, tiled=True
        ).astype(jnp.float32),
        lax.psum_scatter(
            grad_query.astype(jnp.bfloat16), "dp", scatter_dimension=0, tiled=True
        ).astype(jnp.float32),
        lax.psum_scatter(
            grad_key.astype(jnp.bfloat16), "dp", scatter_dimension=0, tiled=True
        ).astype(jnp.float32),
        lax.psum_scatter(
            grad_value.astype(jnp.bfloat16), "dp", scatter_dimension=0, tiled=True
        ).astype(jnp.float32),
        lax.psum_scatter(
            grad_out.astype(jnp.bfloat16), "dp", scatter_dimension=1, tiled=True
        ).astype(jnp.float32),
        lax.psum_scatter(
            grad_gain_ffn.astype(jnp.bfloat16), "dp", scatter_dimension=0, tiled=True
        ).astype(jnp.float32),
        lax.psum_scatter(
            grad_gate.astype(jnp.bfloat16), "dp", scatter_dimension=0, tiled=True
        ).astype(jnp.float32),
        lax.psum_scatter(
            grad_up.astype(jnp.bfloat16), "dp", scatter_dimension=0, tiled=True
        ).astype(jnp.float32),
        lax.psum_scatter(
            grad_down.astype(jnp.bfloat16), "dp", scatter_dimension=1, tiled=True
        ).astype(jnp.float32),
    )
    return (block_out[None], grad_in[None]) + results


def solution(mesh):
    return jax.shard_map(
        on_device,
        mesh=mesh,
        in_specs=(
            P("dp", "tensor", None),
            P("dp", None),
            P("dp", None, None),
            P("dp"),
            P(None, "dp", None, "tensor"),
            P(None, "dp", None, "tensor"),
            P("dp"),
            P("dp", "tensor"),
            P("dp", "tensor"),
            P("dp", "tensor"),
            P("tensor", "dp"),
            P("dp"),
            P("dp", "tensor"),
            P("dp", "tensor"),
            P("tensor", "dp"),
            P("dp", "tensor", None),
        ),
        out_specs=(
            P("dp", "tensor", None),
            P("dp", "tensor", None),
            P("dp"),
            P("dp", "tensor"),
            P("dp", "tensor"),
            P("dp", "tensor"),
            P("tensor", "dp"),
            P("dp"),
            P("dp", "tensor"),
            P("dp", "tensor"),
            P("tensor", "dp"),
        ),
        check_vma=False,
    )
```

profile of v0, /device:TPU:0, one launch (start us, length us, event | category | flops | bytes accessed | tf_op | source)
XLA Modules:
  0.0 1333.0 jit_solution(5837692865810400089)
XLA Ops:
  33.7 51.9 %all-gather.1 = bf16[8,1,128]{2,1,0:T(2,128)(2,1)S(1)} all-gather(bf16[1,1,128]{2,1,0:T(2,128)(2,1)S(1)} %bitcast.267), channel_id=1, replica_groups=mesh['dp'=8,'tensor'=4] {'dp'}, dimensions={0}, use_global_device_ids=true | all-gather | bytes 2304 | tf_op jit(solution)/shard_map/all_gather | solution.py:117
  99.6 52.9 %all_gather.53 = bf16[1024,256]{1,0:T(8,128)(2,1)} all-gather(bf16[128,256]{1,0:T(8,128)(2,1)S(1)} %copy-done.33), channel_id=1, replica_groups=mesh['dp'=8,'tensor'=4] {'dp'}, dimensions={0}, use_global_device_ids=true | all-gather | bytes 589824 | tf_op jit(solution)/shard_map/all_gather | solution.py:118
  161.4 10.8 all_gather.52
  172.2 10.1 all_gather.55
  236.3 79.6 %while.28 = (s32[]{:T(128)}, bf16[4,512,2,128]{1,3,2,0:T(8,128)(2,1)}, f32[4,2,512]{2,1,0:T(2,128)S(1)}, bf16[4,1024,2,128]{3,2,1,0:T(2,128)(2,1)}, bf16[2048,2,...) while((s32[]{:T(128)}, ...), condition=%wide.region_7.8_spmd.clone, body=%wide.region_4.7_spmd.clone.sunk | while | flops 1664089088 | bytes 69260464 | solution.py:190
  331.2 67.7 %reduce-scatter.20.cloned.1.call-done = bf16[512,1024]{1,0:T(8,128)(2,1)} async-done(((bf16[2048,1024]{1,0:T(8,128)(2,1)}), bf16[512,1024]{1,0:T(8,128)(2,1)}) %reduce-scatter.20.cloned.1.call-update) | async-done | bytes 1048592 | tf_op jit(solution)/shard_map/reduce_scatter | solution.py:62
  404.2 79.1 %all-gather.13.cloned.1.call-done = bf16[2048,1024]{1,0:T(8,128)(2,1)} async-done(((bf16[512,1024]{1,0:T(8,128)(2,1)}), bf16[2048,1024]{1,0:T(8,128)(2,1)}) %all-gather.13.cloned.1.call-update) | async-done | bytes 4194320 | tf_op jit(solution)/shard_map/all_gather | solution.py:54
  491.5 17.3 %all-gather.15.cloned.1.call-done = bf16[1024,704]{0,1:T(8,128)(2,1)} async-done(((bf16[128,704]{0,1:T(8,128)(2,1)}), bf16[1024,704]{0,1:T(8,128)(2,1)}) %all-gather.15.cloned.1.call-update) | async-done | bytes 1441808 | tf_op jit(solution)/shard_map/all_gather | solution.py:123
  517.2 18.9 %all-gather.19.cloned.1.call-done = bf16[704,1024]{1,0:T(8,128)(2,1)} async-done(((bf16[704,128]{1,0:T(8,128)(2,1)}), bf16[704,1024]{1,0:T(8,128)(2,1)}) %all-gather.19.cloned.1.call-update) | async-done | bytes 1441808 | tf_op jit(solution)/shard_map/all_gather | solution.py:125
  536.0 82.3 %all-gather.23.cloned.1.call-done = bf16[1,2048,1024]{2,1,0:T(8,128)(2,1)} async-done(((bf16[1,512,1024]{2,1,0:T(8,128)(2,1)}), bf16[1,2048,1024]{2,1,0:T(8,128)(2,1)}) %all-gather.23.cloned.1.call-update) | async-done | bytes 4194320 | tf_op jit(solution)/shard_map/all_gather | solution.py:85
  618.3 11.8 multiply_convert_fusion.1
  638.9 75.4 %reduce-scatter.24.cloned.1.call-done = bf16[512,1024]{1,0:T(8,128)(2,1)} async-done(((bf16[2048,1024]{1,0:T(8,128)(2,1)}), bf16[512,1024]{1,0:T(8,128)(2,1)}) %reduce-scatter.24.cloned.1.call-update) | async-done | bytes 1048592 | tf_op jit(solution)/shard_map/reduce_scatter | solution.py:74
  747.4 52.9 %all-gather.21.cloned.1.call-done = bf16[2048,1024]{1,0:T(8,128)(2,1)} async-done(((bf16[512,1024]{1,0:T(8,128)(2,1)}), bf16[2048,1024]{1,0:T(8,128)(2,1)}) %all-gather.21.cloned.1.call-update) | async-done | bytes 4194320 | tf_op jit(solution)/shard_map/all_gather | solution.py:85
  805.1 204.3 %while.29 = (s32[]{:T(128)}, f32[2048,2,128]{0,2,1:T(8,128)}, f32[2048,2,128]{0,2,1:T(8,128)}, f32[4,512,2,128]{3,1,0,2:T(8,128)}, bf16[4,512,2,128]{3,1,2,0:T(8...) while((s32[]{:T(128)}, f32[2048,2,128]{0,2,1:T(8,128)}, ...), condition=%wide.region_15.16_spmd.clone, body=%wide.region_13.15_spmd.clone.sunk | while | flops 3530161152 | bytes 201106800 | solution.py:269
  819.6 13.9 %multiply_reduce_fusion.3 = (f32[2,512]{1,0:T(2,128)S(1)}, f32[2,512,3072]{2,1,0:T(8,128)}, f32[2,512,3072]{2,1,0:T(8,128)}) fusion(f32[2,512]{1,0:T(2,128)S(1)} %dynamic-slice_bitcast_fusion.7, f32[2,512,1024]{2,1,0:T(8,128)} %fusion.215, f32[2,512,2048]{2,1,0:T(8,128)} %fusion.216, pred[512,3072]{1,0:T(8,128)(4,1)S(1)} %concatenate.62, ...), kind=kOutput, calls=%fused_computation.44.clone.1 | convolution fusion | flops 827325440 | bytes 41164800 | tf_op jit(solution)/shard_map/while/body/eval_jaxpr/qhd,khd->hqk/dot_general | solution.py:242
  869.5 13.9 %multiply_reduce_fusion.3 = (f32[2,512]{1,0:T(2,128)S(1)}, f32[2,512,3072]{2,1,0:T(8,128)}, f32[2,512,3072]{2,1,0:T(8,128)}) fusion(f32[2,512]{1,0:T(2,128)S(1)} %dynamic-slice_bitcast_fusion.7, f32[2,512,1024]{2,1,0:T(8,128)} %fusion.215, f32[2,512,2048]{2,1,0:T(8,128)} %fusion.216, pred[512,3072]{1,0:T(8,128)(4,1)S(1)} %concatenate.62, ...), kind=kOutput, calls=%fused_computation.44.clone.1 | convolution fusion | flops 827325440 | bytes 41164800 | tf_op jit(solution)/shard_map/while/body/eval_jaxpr/qhd,khd->hqk/dot_general | solution.py:242
  921.7 13.8 %multiply_reduce_fusion.3 = (f32[2,512]{1,0:T(2,128)S(1)}, f32[2,512,3072]{2,1,0:T(8,128)}, f32[2,512,3072]{2,1,0:T(8,128)}) fusion(f32[2,512]{1,0:T(2,128)S(1)} %dynamic-slice_bitcast_fusion.7, f32[2,512,1024]{2,1,0:T(8,128)} %fusion.215, f32[2,512,2048]{2,1,0:T(8,128)} %fusion.216, pred[512,3072]{1,0:T(8,128)(4,1)S(1)} %concatenate.62, ...), kind=kOutput, calls=%fused_computation.44.clone.1 | convolution fusion | flops 827325440 | bytes 41164800 | tf_op jit(solution)/shard_map/while/body/eval_jaxpr/qhd,khd->hqk/dot_general | solution.py:242
  972.8 13.7 %multiply_reduce_fusion.3 = (f32[2,512]{1,0:T(2,128)S(1)}, f32[2,512,3072]{2,1,0:T(8,128)}, f32[2,512,3072]{2,1,0:T(8,128)}) fusion(f32[2,512]{1,0:T(2,128)S(1)} %dynamic-slice_bitcast_fusion.7, f32[2,512,1024]{2,1,0:T(8,128)} %fusion.215, f32[2,512,2048]{2,1,0:T(8,128)} %fusion.216, pred[512,3072]{1,0:T(8,128)(4,1)S(1)} %concatenate.62, ...), kind=kOutput, calls=%fused_computation.44.clone.1 | convolution fusion | flops 827325440 | bytes 41164800 | tf_op jit(solution)/shard_map/while/body/eval_jaxpr/qhd,khd->hqk/dot_general | solution.py:242
  1087.7 36.3 %reduce-scatter.30.cloned.1.call-done = bf16[128,256]{1,0:T(8,128)(2,1)} async-done(((bf16[1024,256]{1,0:T(8,128)(2,1)}), bf16[128,256]{1,0:T(8,128)(2,1)}) %reduce-scatter.30.cloned.1.call-update) | async-done | bytes 65552 | tf_op jit(solution)/shard_map/reduce_scatter | solution.py:295
  1125.6 36.5 %reduce-scatter.28.cloned.1.call-done = bf16[128,256]{1,0:T(8,128)(2,1)} async-done(((bf16[1024,256]{1,0:T(8,128)(2,1)}), bf16[128,256]{1,0:T(8,128)(2,1)}) %reduce-scatter.28.cloned.1.call-update) | async-done | bytes 65552 | tf_op jit(solution)/shard_map/reduce_scatter | solution.py:292
  1163.5 77.6 %reduce-scatter.26.cloned.1.call-done = bf16[512,1024]{1,0:T(8,128)(2,1)} async-done(((bf16[2048,1024]{1,0:T(8,128)(2,1)}), bf16[512,1024]{1,0:T(8,128)(2,1)}) %reduce-scatter.26.cloned.1.call-update) | async-done | bytes 1048592 | tf_op jit(solution)/shard_map/reduce_scatter | solution.py:74
  1243.3 11.1 all-reduce.8
  1254.5 11.9 all-reduce.9
  1267.6 53.3 %reduce-scatter.22.cloned.1.call-done = bf16[512,1024]{1,0:T(8,128)(2,1)} async-done(((bf16[2048,1024]{1,0:T(8,128)(2,1)}), bf16[512,1024]{1,0:T(8,128)(2,1)}) %reduce-scatter.22.cloned.1.call-update) | async-done | bytes 1048592 | tf_op jit(solution)/shard_map/reduce_scatter | solution.py:62
  (421 shorter events, 500.8 us)
Async XLA Ops:
  28.9 64.6 %all-to-all-start.2 = ((bf16[8,8,128,256]{3,2,1,0:T(8,128)(2,1)}), bf16[8,8,128,256]{3,2,1,0:T(8,128)(2,1)}, u32[]{:S(2)}, u32[]{:S(2)}) async-start(bf16[8,8,128,256]{3,2,1,0:T(8,128)(2,1)} %bitcast.235), calls=%async_computation.2 | async-start | bytes 8388608 | tf_op jit(solution)/shard_map/all_to_all | solution.py:147
  33.6 172.9 %all-gather.11.cloned.1.call-start = ((), (), s32[]{:S(2)}) async-start(), calls=%async_computation.14 | async-start | bytes 5242880 | tf_op jit(solution)/shard_map/all_gather | solution.py:54
  93.6 104.8 %all-to-all-start.1 = ((bf16[8,8,128,256]{3,2,1,0:T(8,128)(2,1)}), bf16[8,8,128,256]{3,2,1,0:T(8,128)(2,1)}, u32[]{:S(2)}, u32[]{:S(2)}) async-start(bf16[8,8,128,256]{3,2,1,0:T(8,128)(2,1)} %bitcast.234), calls=%async_computation.1 | async-start | bytes 8388608 | tf_op jit(solution)/shard_map/all_to_all | solution.py:148
  98.3 300.6 %reduce-scatter.20.cloned.1.call-start = ((), (), s32[]{:S(2)}) async-start(), calls=%async_computation.15 | async-start | bytes 5242880 | tf_op jit(solution)/shard_map/reduce_scatter | solution.py:62
  321.7 82.5 %all-gather.17.cloned.1.call-start = ((), (), s32[]{:S(2)}) async-start(), calls=%async_computation.18 | async-start | bytes 1622016 | tf_op jit(solution)/shard_map/all_gather | solution.py:124
  322.3 161.0 %all-gather.13.cloned.1.call-start = ((), (), s32[]{:S(2)}) async-start(), calls=%async_computation.16 | async-start | bytes 5242880 | tf_op jit(solution)/shard_map/all_gather | solution.py:54
  331.2 386.0 %copy-start.29 = (f32[8,1,128]{2,1,0:T(1,128)}, f32[8,1,128]{2,1,0:T(1,128)S(1)}, u32[]{:S(2)}) copy-start(f32[8,1,128]{2,1,0:T(1,128)S(1)} %convert_element_type.214) | copy-start | bytes 12292
  400.6 316.6 %copy-start.37 = (f32[512]{0:T(512)}, f32[512]{0:T(512)S(1)}, u32[]{:S(2)}) copy-start(f32[512]{0:T(512)S(1)} %fusion.116) | copy-start | bytes 6148
  402.0 106.8 %all-gather.15.cloned.1.call-start = ((), (), s32[]{:S(2)}) async-start(), calls=%async_computation.17 | async-start | bytes 1622016 | tf_op jit(solution)/shard_map/all_gather | solution.py:123
  402.6 133.4 %all-gather.19.cloned.1.call-start = ((), (), s32[]{:S(2)}) async-start(), calls=%async_computation.19 | async-start | bytes 1622016 | tf_op jit(solution)/shard_map/all_gather | solution.py:125
  403.4 215.0 %all-gather.23.cloned.1.call-start = ((), (), s32[]{:S(2)}) async-start(), calls=%async_computation.27 | async-start | bytes 5242880 | tf_op jit(solution)/shard_map/all_gather | solution.py:85
  404.1 310.2 %reduce-scatter.24.cloned.1.call-start = ((), (), s32[]{:S(2)}) async-start(), calls=%async_computation.21 | async-start | bytes 5242880 | tf_op jit(solution)/shard_map/reduce_scatter | solution.py:74
  638.8 161.5 %all-gather.21.cloned.1.call-start = ((), (), s32[]{:S(2)}) async-start(), calls=%async_computation.22 | async-start | bytes 5242880 | tf_op jit(solution)/shard_map/all_gather | solution.py:85
  719.1 356.0 %reduce-scatter.40.cloned.1.call-start = ((), (), s32[]{:S(2)}) async-start(), calls=%async_computation.31 | async-start | bytes 1769472
  727.4 349.6 %reduce-scatter.38.cloned.1.call-start = ((), (), s32[]{:S(2)}) async-start(), calls=%async_computation.30 | async-start | bytes 1769472
  735.7 343.2 %reduce-scatter.36.cloned.1.call-start = ((), (), s32[]{:S(2)}) async-start(), calls=%async_computation.29 | async-start | bytes 1769472
  747.4 333.6 %reduce-scatter.34.cloned.1.call-start = ((), (), s32[]{:S(2)}) async-start(), calls=%async_computation.28 | async-start | bytes 589824
  1016.2 70.0 %reduce-scatter.32.cloned.1.call-start = ((), (), s32[]{:S(2)}) async-start(), calls=%async_computation.26 | async-start | bytes 589824 | tf_op jit(solution)/shard_map/reduce_scatter | solution.py:298
  1035.5 88.5 %reduce-scatter.30.cloned.1.call-start = ((), (), s32[]{:S(2)}) async-start(), calls=%async_computation.25 | async-start | bytes 589824 | tf_op jit(solution)/shard_map/reduce_scatter | solution.py:295
  1045.6 116.5 %reduce-scatter.28.cloned.1.call-start = ((), (), s32[]{:S(2)}) async-start(), calls=%async_computation.24 | async-start | bytes 589824 | tf_op jit(solution)/shard_map/reduce_scatter | solution.py:292
  1055.6 185.5 %reduce-scatter.26.cloned.1.call-start = ((), (), s32[]{:S(2)}) async-start(), calls=%async_computation.23 | async-start | bytes 5242880 | tf_op jit(solution)/shard_map/reduce_scatter | solution.py:74
  1065.0 255.9 %reduce-scatter.22.cloned.1.call-start = ((), (), s32[]{:S(2)}) async-start(), calls=%async_computation.20 | async-start | bytes 5242880 | tf_op jit(solution)/shard_map/reduce_scatter | solution.py:62
  1078.9 242.0 %copy-start.12 = (bf16[512,1024]{1,0:T(8,128)(2,1)S(1)}, bf16[512,1024]{1,0:T(8,128)(2,1)}, u32[]{:S(2)}) copy-start(bf16[512,1024]{1,0:T(8,128)(2,1)} %reduce-scatter.20.cloned.1.call-done) | copy-start | bytes 3145732
  1078.9 242.0 %copy-start.18 = (bf16[1,512,1024]{2,1,0:T(8,128)(2,1)S(1)}, bf16[1,512,1024]{2,1,0:T(8,128)(2,1)}, u32[]{:S(2)}) copy-start(bf16[1,512,1024]{2,1,0:T(8,128)(2,1)} %param.35) | copy-start | bytes 3145732
  (72 other events, 2341.1 us)
Sparse Core Ops, SparseCore 0:
  87.4 80.2 all-gather.10
  321.8 77.0 reduce-scatter.19
  639.0 75.2 reduce-scatter.23
Sparse Core Ops, SparseCore 1:
  324.1 25.3 all-gather.16
  402.1 81.1 all-gather.12
  485.2 23.6 all-gather.14
  510.9 25.1 all-gather.18
  537.7 80.6 all-gather.22
  719.2 81.1 all-gather.20
  803.5 36.8 reduce-scatter.39
  843.5 38.3 reduce-scatter.37
  885.0 38.3 reduce-scatter.35
  1016.3 32.5 reduce-scatter.33
  1052.1 34.1 reduce-scatter.31
  1089.9 34.1 reduce-scatter.29
  1127.9 34.1 reduce-scatter.27
  1164.4 76.7 reduce-scatter.25
  1243.6 77.2 reduce-scatter.21
where the time goes:
time: 1340 us; the launch traced here: 1330 us
  waiting for transfers between devices  604 us (45%)
  matrix products  273 us (20%)
  blocking collectives  176 us (13%)
  local copies, waits for them, and re-layouts  127 us (9%)
  other arithmetic  123 us (9%)
  between operations  18.1 us (1%)
    reduce_scatter x2, waiting for transfers between devices, return_rows(): lax.psum_scatter(summed.astype(jnp.bfloat16), 'tensor', scatter_dimension...  153 us
    all_gather x2, waiting for transfers between devices, all_rows(): return lax.all_gather(local_grad, 'tensor', axis=0, tiled=True)  135 us
    reduce_scatter x2, waiting for transfers between devices, reduce_rows(): lax.psum_scatter(jnp.dot(left, right, preferred_element_type=jnp.float32)...  121 us
    all_gather x2, waiting for transfers between devices, spread_rows(): piece_rows = lax.all_gather(local_rows, 'tensor', axis=0, tiled=True)  79.1 us
    dot_general x4, matrix products, backward_block(): jnp.einsum('qhd,khd->hqk', grad_blk, values_both, preferred_element_type=...  55.2 us
    all_gather x1, blocking collectives, on_device(): lax.all_gather(w_query, 'dp', axis=0, tiled=True)  52.9 us
    all_gather x1, blocking collectives, on_device(): lax.all_gather(gain_attn, 'dp', axis=0, tiled=True)  51.9 us
    dot_general x7, matrix products, against(): lax.dot_general(left, right, (((1,), (1,)), ((), ())), preferred_element_...  44.5 us
  transfers between devices with their start and end apart: 20, of which 12 were waited for; matrix products, arithmetic and copies ran while one was open for 26% of the time, Pallas kernels for 0%

commit v1 on v0

--- a/solution.py
+++ b/solution.py
@@ -1,16 +1,1029 @@
+import functools
+import math
+
 import jax
 import jax.numpy as jnp
 from jax import lax
+from jax.experimental import pallas as pl
+from jax.experimental.pallas import tpu as pltpu
 from jax.sharding import PartitionSpec as P
 
-HEADS = 8
+MESH = pl.DeviceIdType.MESH
+MEMB = 128
+
+
+class Grid:
+    def __init__(self, dp, tensor):
+        side = math.isqrt(dp // 2)
+        assert side * side * 2 == dp
+        self.na, self.nb, self.nc, self.nz, self.dp = side, side, 2, tensor, dp
+
+
+def coords(g):
+    me = lax.axis_index("dp")
+    t = lax.axis_index("tensor")
+    return me // (2 * g.nb), (me // 2) % g.nb, me % 2, t, me
+
+
+def send(src, dst, ssem, rsem, dp, t):
+    return pltpu.make_async_remote_copy(
+        src_ref=src, dst_ref=dst, send_sem=ssem, recv_sem=rsem, device_id=(dp, t), device_id_type=MESH
+    )
+
+
+def greet(g, me, t):
+    bar = pltpu.get_barrier_semaphore()
+    for k in range(1, g.dp):
+        pl.semaphore_signal(bar, inc=1, device_id=((me + k) % g.dp, t), device_id_type=MESH)
+    for k in range(1, g.nz):
+        pl.semaphore_signal(bar, inc=1, device_id=(me, (t + k) % g.nz), device_id_type=MESH)
+    pl.semaphore_wait(bar, g.dp - 1 + g.nz - 1)
+
+
+class Gather:
+    def __init__(self, g, shard, buf, rows, b_first, sems, base):
+        self.g, self.shard, self.buf, self.rows, self.b_first = g, shard, buf, rows, b_first
+        self.sems, self.next = sems, base
+        self.sent = []
+
+    def _sem(self):
+        i = self.next
+        self.next += 1
+        return self.sems[0].at[i], self.sems[1].at[i]
+
+    def at(self, dp, t=None):
+        lo, n = self.rows
+        if t is None:
+            return self.buf.at[dp, :, pl.ds(lo, n), :]
+        return self.buf.at[dp, t, pl.ds(lo, n), :]
+
+    def start_z(self):
+        g = self.g
+        a, b, c, t, me = coords(g)
+        lo, n = self.rows
+        src = self.shard.at[pl.ds(lo, n), :]
+        self.z = []
+        for k in range(1, g.nz):
+            s, r = self._sem()
+            d = send(src, self.at(me, t), s, r, me, (t + k) % g.nz)
+            d.start()
+            self.z.append(d)
+        s, _ = self._sem()
+        self.own = pltpu.make_async_copy(src, self.at(me, t), s)
+        self.own.start()
+        self.sent += self.z
+
+    def _dp(self, a, b, c):
+        return (a * self.g.nb + b) * 2 + c
+
+    def _core(self, dp, c):
+        s, r = self._sem()
+        d = send(self.at(dp), self.at(dp), s, r, coords(self.g)[4] + 1 - 2 * c, coords(self.g)[3])
+        d.start()
+        self.core.append(d)
+        self.sent.append(d)
+
+    def start_first(self):
+        g = self.g
+        a, b, c, t, me = coords(g)
+        self.own.wait()
+        for d in self.z:
+            d.wait_recv()
+        self.first, self.core = [], []
+        n1 = g.nb if self.b_first else g.na
+        for k in range(1, n1):
+            to = self._dp(a, (b + k) % n1, c) if self.b_first else self._dp((a + k) % n1, b, c)
+            s, r = self._sem()
+            d = send(self.at(me), self.at(me), s, r, to, t)
+            d.start()
+            self.first.append(d)
+        self.sent += self.first
+        self._core(me, c)
+
+    def start_second(self):
+        g = self.g
+        a, b, c, t, me = coords(g)
+        n1, n2 = (g.nb, g.na) if self.b_first else (g.na, g.nb)
+        for d in self.first:
+            d.wait_recv()
+        held = [self._dp(a, (b - k) % n1, c) if self.b_first else self._dp((a - k) % n1, b, c) for k in range(n1)]
+        self.second = []
+        for slot in held:
+            for k in range(1, n2):
+                to = self._dp((a + k) % n2, b, c) if self.b_first else self._dp(a, (b + k) % n2, c)
+                s, r = self._sem()
+                d = send(self.at(slot), self.at(slot), s, r, to, t)
+                d.start()
+                self.second.append(d)
+        for slot in held[1:]:
+            self._core(slot, c)
+        self.sent += self.second
+
+    def start_core(self):
+        g = self.g
+        a, b, c, t, me = coords(g)
+        n1, n2 = (g.nb, g.na) if self.b_first else (g.na, g.nb)
+        for d in self.second:
+            d.wait_recv()
+        for k1 in range(n1):
+            for k in range(1, n2):
+                slot = (
+                    self._dp((a - k) % n2, (b - k1) % n1, c)
+                    if self.b_first
+                    else self._dp((a - k1) % n1, (b - k) % n2, c)
+                )
+                self._core(slot, c)
+
+    def finish(self):
+        for d in self.core:
+            d.wait_recv()
+        for d in self.sent:
+            d.wait_send()
+
+
+def gather_sems(g):
+    return g.nz + (g.na - 1) + g.na * (g.na - 1) + g.na * g.nb
+
+
+def k1_kernel(g, cap, nq, ksel, halo, units, n_w, *refs):
+    refs = list(refs)
+    take = lambda n: [refs.pop(0) for _ in range(n)]
+    requests, sel = take(2)
+    x, gains, mem_k, mem_v = take(4)
+    shards = take(n_w)
+    bufs = take(n_w)
+    xh, gains_all, mk, mv = take(4)
+    loc_k, loc_v, stage_k, stage_v, rec_k, rec_v, zst_k, zst_v = take(8)
+    req_in, req_s = take(2)
+    ss, rs, msl, mss, mrs, zss, zrs, xss, xrs, qss, qrs, gss, grs = take(13)
+    a, b, c, t, me = coords(g)
+    greet(g, me, t)
+    rq, gn = [], []
+    for k in range(1, g.dp):
+        to = (me + k) % g.dp
+        d = send(requests.at[to], req_in.at[me], qss.at[k], qrs.at[k], to, t)
+        d.start()
+        rq.append(d)
+    for k in range(1, g.dp):
+        to = (me + k) % g.dp
+        d = send(gains, gains_all.at[me], gss.at[k], grs.at[k], to, t)
+        d.start()
+        gn.append(d)
+    own_r = pltpu.make_async_copy(requests.at[me], req_in.at[me], qss.at[0])
+    own_r.start()
+    own_g = pltpu.make_async_copy(gains, gains_all.at[me], gss.at[0])
+    own_g.start()
+    lk = pltpu.make_async_copy(mem_k, loc_k, msl.at[0])
+    lv = pltpu.make_async_copy(mem_v, loc_v, msl.at[1])
+    lk.start()
+    lv.start()
+    per = gather_sems(g)
+    gs = [Gather(g, shards[w], bufs[w], rows, bf, (ss, rs), i * per) for i, (w, rows, bf) in enumerate(units)]
+    for u in gs[:4]:
+        u.start_z()
+    xs = []
+    for k in range(1, halo + 1):
+        d = send(x, xh.at[k - 1], xss.at[k - 1], xrs.at[k - 1], me, (t + k) % g.nz)
+        xs.append(d)
+
+        @pl.when(t + k < g.nz)
+        def _():
+            d.start()
+
+    own_r.wait()
+    own_g.wait()
+    for d in rq:
+        d.wait()
+    cp = pltpu.make_async_copy(req_in, req_s, qrs.at[0])
+    cp.start()
+    cp.wait()
+
+    def exchange(loc, stage, rec, i, load):
+        load.wait()
+
+        @pl.loop(0, g.dp)
+        def _(s):
+            for k in range(cap):
+                stage[s, k] = loc[req_s[s, 0, k]]
+
+        out = []
+        for k in range(1, g.dp):
+            to = (me + k) % g.dp
+            d = send(stage.at[to], rec.at[me], mss.at[i, k], mrs.at[i, k], to, t)
+            d.start()
+            out.append(d)
+        own = pltpu.make_async_copy(stage.at[me], rec.at[me], mss.at[i, 0])
+        own.start()
+        return out + [own]
+
+    ek = exchange(loc_k, stage_k, rec_k, 0, lk)
+    for u in gs[:4]:
+        u.start_first()
+    ev = exchange(loc_v, stage_v, rec_v, 1, lv)
+    for u in gs[4:]:
+        u.start_z()
+    for u in gs[:4]:
+        u.start_second()
+    for u in gs[:4]:
+        u.start_core()
+
+    def spread(moves, rec, zst, out, i):
+        for d in moves:
+            d.wait()
+
+        @pl.loop(0, nq)
+        def _(q):
+            for j in range(ksel):
+                zst[q, j] = rec[sel[q * ksel + j] // cap, sel[q * ksel + j] % cap]
+
+        res = []
+        for k in range(1, g.nz):
+            to = (t + k) % g.nz
+            d = send(zst.at[to], out.at[t], zss.at[i, k], zrs.at[i, k], me, to)
+            d.start()
+            res.append(d)
+        own = pltpu.make_async_copy(zst.at[t], out.at[t], zss.at[i, 0])
+        own.start()
+        return res + [own]
+
+    zk = spread(ek, rec_k, zst_k, mk, 0)
+    for u in gs[4:]:
+        u.start_first()
+    zv = spread(ev, rec_v, zst_v, mv, 1)
+    for u in gs[4:]:
+        u.start_second()
+    for u in gs[4:]:
+        u.start_core()
+    for d in zk + zv + gn:
+        d.wait()
+    for u in gs:
+        u.finish()
+    for k, d in enumerate(xs):
+
+        @pl.when(t + k + 1 < g.nz)
+        def _():
+            d.wait_send()
+
+        @pl.when(t >= k + 1)
+        def _():
+            d.wait_recv()
+
+
+def k1(g, cap, halo, requests, sel, x, gains, mem_k, mem_v, shards, nq, ksel):
+    bf = jnp.bfloat16
+    blk = mem_k.shape[1:]
+    units = []
+    for w, s in enumerate(shards):
+        r = s.shape[0]
+        kind = w % 7
+        if w in (0, 4):
+            units.append((w, (0, r), True))
+        elif w in (1, 5):
+            units.append((w, (0, r), False))
+        else:
+            units.append((w, (0, r // 2), True))
+            units.append((w, (r // 2, r - r // 2), False))
+    n_w = len(shards)
+    any_ = pl.BlockSpec(memory_space=pl.ANY)
+    nsem = len(units) * gather_sems(g)
+    dma = lambda *n: pltpu.SemaphoreType.DMA(n)
+    out_shape = (
+        [jax.ShapeDtypeStruct((g.dp, g.nz) + s.shape, bf) for s in shards]
+        + [jax.ShapeDtypeStruct((halo,) + x.shape, bf), jax.ShapeDtypeStruct((g.dp,) + gains.shape, gains.dtype)]
+        + [jax.ShapeDtypeStruct((g.nz, ksel) + blk, bf)] * 2
+    )
+    scratch = (
+        [pltpu.VMEM(mem_k.shape, bf)] * 2
+        + [pltpu.VMEM((g.dp, cap) + blk, bf)] * 4
+        + [pltpu.VMEM((nq, ksel) + blk, bf)] * 2
+        + [pltpu.VMEM((g.dp, 8, 128), jnp.int32), pltpu.SMEM((g.dp, 8, 128), jnp.int32)]
+        + [dma(nsem), dma(nsem), dma(2), dma(2, g.dp), dma(2, g.dp), dma(2, g.nz), dma(2, g.nz)]
+        + [dma(halo), dma(halo), dma(g.dp), dma(g.dp), dma(g.dp), dma(g.dp)]
+    )
+    return pl.pallas_call(
+        functools.partial(k1_kernel, g, cap, nq, ksel, halo, units, n_w),
+        out_shape=out_shape,
+        in_specs=[pl.BlockSpec(memory_space=pltpu.VMEM), pl.BlockSpec(memory_space=pltpu.SMEM)] + [any_] * (4 + n_w),
+        out_specs=[any_] * len(out_shape),
+        scratch_shapes=scratch,
+        compiler_params=pltpu.CompilerParams(collective_id=0, has_side_effects=True, vmem_limit_bytes=60 * 2**20),
+        name="fwd_exchange",
+    )(requests, sel, x, gains, mem_k, mem_v, *shards)
+
+
+def plan_requests(retrieved, partner, dp_size, blocks_dev, cap):
+    wanted = retrieved.reshape(-1)
+    n = wanted.shape[0]
+    from_partner = wanted // MEMB
+    block_index = wanted % MEMB
+    owner = block_index // blocks_dev
+    local = block_index % blocks_dev
+    seq = jnp.where(from_partner == 0, lax.axis_index("dp"), partner)
+    flat = seq * blocks_dev + local
+    i = jnp.arange(n)
+    slot = jnp.sum(((owner[:, None] == owner[None, :]) & (i[None, :] < i[:, None])).astype(jnp.int32), axis=1)
+    hit = (owner[None, None, :] == jnp.arange(dp_size)[:, None, None]) & (
+        slot[None, None, :] == jnp.arange(128)[None, :, None]
+    )
+    req = jnp.sum(jnp.where(hit, flat[None, None, :], 0), axis=2)
+    return jnp.broadcast_to(req[:, None, :], (dp_size, 8, 128)).astype(jnp.int32), (owner * cap + slot).astype(jnp.int32)
+
 HD = 128
-QB = 512
-MEMB = 128
-
-
 EPSILON = 1e-05
 MASKED = -1e30
+F32, BF16 = jnp.float32, jnp.bfloat16
+
+
+def dot_nn(x, y):
+    return lax.dot_general(x, y, (((1,), (0,)), ((), ())), preferred_element_type=F32)
+
+
+def dot_nt(x, y):
+    return lax.dot_general(x, y, (((1,), (1,)), ((), ())), preferred_element_type=F32)
+
+
+def dot_tn(x, y):
+    return lax.dot_general(x, y, (((0,), (0,)), ((), ())), preferred_element_type=F32)
+
+
+def inv_rms(v):
+    return lax.rsqrt(jnp.mean(v * v, axis=-1, keepdims=True) + EPSILON)
+
+
+def gain_row(gains_ref, which):
+    n = gains_ref.shape[0]
+    return jnp.concatenate([gains_ref[d, which : which + 1, :] for d in range(n)], axis=1)
+
+
+def turn(v, cos, sin):
+    return v * cos + pltpu.roll(v, HD // 2, axis=1) * sin
+
+
+def lanes(ref):
+    return jnp.concatenate([ref[d, 0] for d in range(ref.shape[0])], axis=1)
+
+
+def rows(ref):
+    return jnp.concatenate([ref[d, 0] for d in range(ref.shape[0])], axis=0)
+
+
+VL = 60 * 2**20
+
+
+def full(shape, buffers=None):
+    n = len(shape)
+    kw = {} if buffers is None else dict(pipeline_mode=pl.Buffered(buffers))
+    return pl.BlockSpec(shape, lambda *i: (0,) * n, **kw)
+
+
+def project(halo, first, x, xh, gains, cos, sin, wq, wk, wv):
+    r, d = x.shape
+    dp, nz, _, cols = wq.shape
+    rt = (halo + 1) * r
+
+    def kern(x_ref, xh_ref, gn_ref, cos_ref, sin_ref, wq_ref, wk_ref, wv_ref, n_ref, q_ref, k_ref, v_ref, w_s):
+        @pl.when(pl.program_id(0) == 0)
+        def _():
+            g = gain_row(gn_ref, 0)
+            t = lax.axis_index("tensor")
+            for j in range(halo):
+                v = xh_ref[j].astype(F32)
+                n = (v * inv_rms(v) * g).astype(BF16)
+                n_ref[pl.ds((halo - 1 - j) * r, r), :] = jnp.where(t >= j + 1, n, jnp.zeros_like(n))
+            v = x_ref[...].astype(F32)
+            n_ref[pl.ds(halo * r, r), :] = (v * inv_rms(v) * g).astype(BF16)
+
+        w_s[:, 0:cols] = rows(wq_ref)
+        w_s[:, cols : 2 * cols] = rows(wk_ref)
+        w_s[:, 2 * cols :] = rows(wv_ref)
+
+        tile = 256
+
+        @pl.loop(0, rt // tile)
+        def _(i):
+            at = pl.ds(pl.multiple_of(i * tile, tile), tile)
+            n = n_ref[at, :]
+            y = dot_nn(n, w_s[:, cols:])
+            cs, sn = cos_ref[at, :], sin_ref[at, :]
+            for h in range(cols // HD):
+                k_ref[at, h * HD : (h + 1) * HD] = turn(y[:, h * HD : (h + 1) * HD], cs, sn).astype(BF16)
+            v_ref[at, :] = y[:, cols:].astype(BF16)
+
+            @pl.when(i >= halo * r // tile)
+            def _():
+                z = dot_nn(n, w_s[:, 0:cols])
+                to = pl.ds(pl.multiple_of(i * tile - halo * r, tile), tile)
+                for h in range(cols // HD):
+                    q_ref[to, h * HD : (h + 1) * HD] = turn(z[:, h * HD : (h + 1) * HD], cs, sn).astype(BF16)
+
+    wspec = pl.BlockSpec((dp, 1, wq.shape[2], cols), lambda t: (0, t, 0, 0))
+    col = lambda n: pl.BlockSpec((n, cols), lambda t: (0, t))
+    return pl.pallas_call(
+        kern,
+        grid=(nz,),
+        in_specs=[full((r, d)), full((halo, r, d)), full(gains.shape), full((rt, HD)), full((rt, HD))] + [wspec] * 3,
+        out_specs=[full((rt, d)), col(r), col(rt), col(rt)],
+        out_shape=[
+            jax.ShapeDtypeStruct((rt, d), BF16),
+            jax.ShapeDtypeStruct((r, d), BF16),
+            jax.ShapeDtypeStruct((rt, d), BF16),
+            jax.ShapeDtypeStruct((rt, d), BF16),
+        ],
+        scratch_shapes=[pltpu.VMEM((d, 3 * cols), BF16)],
+        compiler_params=pltpu.CompilerParams(vmem_limit_bytes=VL, dimension_semantics=("arbitrary",)),
+        name="project",
+    )(x, xh, gains, cos, sin, wq, wk, wv)
+
+
+def allowed_of(seg_q, seg_k, q0, k0):
+    n, m = seg_q.shape[0], seg_k.shape[1]
+    qp = lax.broadcasted_iota(jnp.int32, (n, m), 0) + q0
+    kp = lax.broadcasted_iota(jnp.int32, (n, m), 1) + k0
+    return (seg_q == seg_k) & (kp <= qp)
+
+
+QT = 256
+C2 = HD**-0.5 * math.log2(math.e)
+
+
+def attend(halo, window, q, k, v, mk, mv, seg_q, seg_k):
+    r, d = q.shape
+    rt = k.shape[0]
+    nz, ksel, blk, cols = mk.shape
+    per = cols // HD
+    nm = ksel * blk
+
+    def kern(q_ref, k_ref, v_ref, mk_ref, mv_ref, sq_ref, sk_ref, o_ref, l_ref):
+        km = mk_ref[0].reshape(nm, HD)
+        vm = mv_ref[0].reshape(nm, HD)
+        for i in range(r // QT):
+            at = slice(i * QT, (i + 1) * QT)
+            k0 = halo * r - window + i * QT
+            ks = slice(k0, k0 + window + QT)
+            qq = q_ref[at, :]
+            ok = allowed_of(sq_ref[at, :], sk_ref[:, ks], halo * r + i * QT, k0)
+            sl = jnp.where(ok, dot_nt(qq, k_ref[ks, :]), MASKED)
+            sm = dot_nt(qq, km)
+            m = jnp.maximum(jnp.max(sl, axis=1, keepdims=True), jnp.max(sm, axis=1, keepdims=True))
+            mc = m * C2
+            el = jnp.exp2(sl * C2 - mc)
+            em = jnp.exp2(sm * C2 - mc)
+            tot = jnp.sum(el, axis=1, keepdims=True) + jnp.sum(em, axis=1, keepdims=True)
+            acc = dot_nn(el.astype(BF16), v_ref[ks, :]) + dot_nn(em.astype(BF16), vm)
+            o_ref[at, :] = (acc / tot).astype(BF16)
+            l_ref[0, at, :] = mc + jnp.log2(tot)
+
+    head = lambda n: pl.BlockSpec((n, HD), lambda h: (0, h))
+    mem = pl.BlockSpec((1, ksel, blk, HD), lambda h: (h // per, 0, 0, h % per))
+    return pl.pallas_call(
+        kern,
+        grid=(d // HD,),
+        in_specs=[head(r), head(rt), head(rt), mem, mem, full((r, 1)), full((1, rt))],
+        out_specs=[head(r), pl.BlockSpec((1, r, 1), lambda h: (h, 0, 0))],
+        out_shape=[jax.ShapeDtypeStruct((r, d), BF16), jax.ShapeDtypeStruct((d // HD, r, 1), F32)],
+        compiler_params=pltpu.CompilerParams(vmem_limit_bytes=VL, dimension_semantics=("arbitrary",)),
+        name="attend",
+    )(q, k, v, mk, mv, seg_q, seg_k)
+
+
+def attend_back(halo, window, q, k, v, mk, mv, seg_q, seg_k, o, lse, do, cos, sin):
+    r, d = q.shape
+    rt = k.shape[0]
+    nz, ksel, blk, cols = mk.shape
+    per = cols // HD
+    nm = ksel * blk
+    scale = HD**-0.5
+
+    def kern(q_ref, k_ref, v_ref, mk_ref, mv_ref, sq_ref, sk_ref, o_ref, l_ref, do_ref, cos_ref, sin_ref,
+             dq_ref, dk_ref, dv_ref, sdk, sdv):
+        km = mk_ref[0].reshape(nm, HD)
+        vm = mv_ref[0].reshape(nm, HD)
+        sdk[...] = jnp.zeros_like(sdk)
+        sdv[...] = jnp.zeros_like(sdv)
+        for i in range(r // QT):
+            at = slice(i * QT, (i + 1) * QT)
+            k0 = halo * r - window + i * QT
+            ks = slice(k0, k0 + window + QT)
+            own = slice(halo * r + i * QT, halo * r + (i + 1) * QT)
+            qq, dd = q_ref[at, :], do_ref[at, :]
+            lse_c = l_ref[0, at, :]
+            delta = jnp.sum(dd.astype(F32) * o_ref[at, :].astype(F32), axis=1, keepdims=True)
+            ok = allowed_of(sq_ref[at, :], sk_ref[:, ks], halo * r + i * QT, k0)
+            pm = jnp.exp2(dot_nt(qq, km) * C2 - lse_c)
+            dsm = (pm * (dot_nt(dd, vm) - delta)).astype(BF16)
+            plo = jnp.where(ok, jnp.exp2(dot_nt(qq, k_ref[ks, :]) * C2 - lse_c), 0.0)
+            dsl = (plo * (dot_nt(dd, v_ref[ks, :]) - delta)).astype(BF16)
+            dq = (dot_nn(dsm, km) + dot_nn(dsl, k_ref[ks, :])) * scale
+            dq_ref[at, :] = turn(dq, cos_ref[own, :], -sin_ref[own, :]).astype(BF16)
+            sdk[ks, :] += dot_tn(dsl, qq)
+            sdv[ks, :] += dot_tn(plo.astype(BF16), dd)
+        dk_ref[...] = turn(sdk[...] * scale, cos_ref[...], -sin_ref[...]).astype(BF16)
+        dv_ref[...] = sdv[...].astype(BF16)
+
+    head = lambda n: pl.BlockSpec((n, HD), lambda h: (0, h))
+    mem = pl.BlockSpec((1, ksel, blk, HD), lambda h: (h // per, 0, 0, h % per))
+    return pl.pallas_call(
+        kern,
+        grid=(d // HD,),
+        in_specs=[head(r), head(rt), head(rt), mem, mem, full((r, 1)), full((1, rt)), head(r),
+                  pl.BlockSpec((1, r, 1), lambda h: (h, 0, 0)), head(r), full((rt, HD)), full((rt, HD))],
+        out_specs=[head(r), head(rt), head(rt)],
+        out_shape=[jax.ShapeDtypeStruct((n, d), BF16) for n in (r, rt, rt)],
+        scratch_shapes=[pltpu.VMEM((rt, HD), F32)] * 2,
+        compiler_params=pltpu.CompilerParams(vmem_limit_bytes=VL, dimension_semantics=("arbitrary",)),
+        name="attend_back",
+    )(q, k, v, mk, mv, seg_q, seg_k, o, lse, do, cos, sin)
+
+
+def out_norm(x, o, wo, gains):
+    r, d = x.shape
+    dp, nz, kk, _ = wo.shape
+
+    def kern(x_ref, o_ref, w_ref, gn_ref, h_ref, n_ref):
+        t = pl.program_id(0)
+
+        @pl.when(t == 0)
+        def _():
+            h_ref[...] = x_ref[...].astype(F32)
+
+        w = lanes(w_ref)
+        tile = 256
+
+        @pl.loop(0, r // tile)
+        def _(i):
+            at = pl.ds(pl.multiple_of(i * tile, tile), tile)
+            h_ref[at, :] += dot_nn(o_ref[at, :], w)
+
+        @pl.when(t == pl.num_programs(0) - 1)
+        def _():
+            h = h_ref[...]
+            n_ref[...] = (h * inv_rms(h) * gain_row(gn_ref, 1)).astype(BF16)
+
+    return pl.pallas_call(
+        kern,
+        grid=(nz,),
+        in_specs=[full((r, d)), pl.BlockSpec((r, kk), lambda t: (0, t)),
+                  pl.BlockSpec((dp, 1, kk, wo.shape[3]), lambda t: (0, t, 0, 0)), full(gains.shape)],
+        out_specs=[full((r, d)), full((r, d))],
+        out_shape=[jax.ShapeDtypeStruct((r, d), F32), jax.ShapeDtypeStruct((r, d), BF16)],
+        compiler_params=pltpu.CompilerParams(vmem_limit_bytes=VL, dimension_semantics=("arbitrary",)),
+        name="out_norm",
+    )(x, o, wo, gains)
+
+
+def feed(h, n2, c, gains, wg, wu, wd, wo):
+    r, d = h.shape
+    dp, nz, ff, _ = wg.shape
+    kk = wo.shape[2]
+
+    def kern(h_ref, n_ref, c_ref, gn_ref, wg_ref, wu_ref, wd_ref, wo_ref,
+             hid_ref, dg_ref, du_ref, out_ref, dh_ref, dhb_ref, do_ref, gg_ref, sg, su, sd, acc):
+        t = pl.program_id(0)
+        last = pl.num_programs(0) - 1
+        sg[...] = lanes(wg_ref)
+        su[...] = lanes(wu_ref)
+        sd[...] = lanes(wd_ref)
+
+        @pl.when(t == 0)
+        def _():
+            out_ref[...] = h_ref[...]
+            acc[...] = jnp.zeros_like(acc)
+
+        tile = 128
+
+        @pl.loop(0, r // tile)
+        def _(i):
+            at = pl.ds(pl.multiple_of(i * tile, tile), tile)
+            n = n_ref[at, :]
+            gate = dot_nt(n, sg[...])
+            up = dot_nt(n, su[...])
+            dhid = dot_nt(c_ref[at, :], sd[...])
+            sig = 1.0 / (1.0 + jnp.exp(-gate))
+            act = gate * sig
+            hid = (act * up).astype(BF16)
+            hid_ref[0, at, :] = hid
+            dg = (dhid * up * (sig * (1.0 + gate * (1.0 - sig)))).astype(BF16)
+            du = (dhid * act).astype(BF16)
+            dg_ref[0, at, :] = dg
+            du_ref[0, at, :] = du
+            out_ref[at, :] += dot_nn(hid, sd[...])
+            acc[at, :] += dot_nn(dg, sg[...]) + dot_nn(du, su[...])
+
+        @pl.when(t == last)
+        def _():
+            g = gain_row(gn_ref, 1)
+            h = h_ref[...]
+            dn = acc[...]
+            iv = inv_rms(h)
+            gg_ref[...] = jnp.sum(dn * h * iv, axis=0, keepdims=True)
+            gd = dn * g
+            dh = c_ref[...].astype(F32) + iv * gd - h * (iv * iv * iv * jnp.mean(h * gd, axis=1, keepdims=True))
+            dh_ref[...] = dh
+            dhb_ref[...] = dh.astype(BF16)
+
+            @pl.loop(0, nz)
+            def _(u):
+                w = jnp.concatenate([wo_ref[e, u] for e in range(dp)], axis=1)
+                do_ref[u] = dot_nt(dhb_ref[...], w).astype(BF16)
+
+    wspec = pl.BlockSpec((dp, 1, ff, wg.shape[3]), lambda t: (0, t, 0, 0))
+    piece = pl.BlockSpec((1, r, ff), lambda t: (t, 0, 0))
+    one = lambda s: full(s, 1)
+    return pl.pallas_call(
+        kern,
+        grid=(nz,),
+        in_specs=[one((r, d)), one((r, d)), one((r, d)), one(gains.shape), wspec, wspec, wspec, one(wo.shape)],
+        out_specs=[piece, piece, piece, full((r, d)), full((r, d)), full((r, d)), full((nz, r, kk)), full((1, d))],
+        out_shape=[jax.ShapeDtypeStruct((nz, r, ff), BF16)] * 3
+        + [jax.ShapeDtypeStruct((r, d), F32), jax.ShapeDtypeStruct((r, d), F32), jax.ShapeDtypeStruct((r, d), BF16),
+           jax.ShapeDtypeStruct((nz, r, kk), BF16), jax.ShapeDtypeStruct((1, d), F32)],
+        scratch_shapes=[pltpu.VMEM((ff, d), BF16)] * 3 + [pltpu.VMEM((r, d), F32)],
+        compiler_params=pltpu.CompilerParams(vmem_limit_bytes=VL, dimension_semantics=("arbitrary",)),
+        name="feed",
+    )(h, n2, c, gains, wg, wu, wd, wo)
+
+
+def project_back(halo, x, xh, dq, dk, dv, wq, wk, wv):
+    r, d = x.shape
+    dp, nz, _, cols = wq.shape
+    rt = (halo + 1) * r
+
+    def kern(x_ref, xh_ref, dq_ref, dk_ref, dv_ref, wq_ref, wk_ref, wv_ref, own_ref, hb_ref, gg_ref, acc, w_s):
+        t = pl.program_id(0)
+        w_s[:, 0:cols] = rows(wk_ref)
+        w_s[:, cols : 2 * cols] = rows(wv_ref)
+        w_s[:, 2 * cols :] = rows(wq_ref)
+
+        @pl.when(t == 0)
+        def _():
+            acc[...] = jnp.zeros_like(acc)
+
+        tile = 256
+
+        @pl.loop(0, rt // tile)
+        def _(i):
+            at = pl.ds(pl.multiple_of(i * tile, tile), tile)
+            acc[at, :] += dot_nt(jnp.concatenate([dk_ref[at, :], dv_ref[at, :]], axis=1), w_s[:, 0 : 2 * cols])
+
+        @pl.loop(0, r // tile)
+        def _(i):
+            at = pl.ds(pl.multiple_of(i * tile, tile), tile)
+            to = pl.ds(pl.multiple_of(i * tile + halo * r, tile), tile)
+            acc[to, :] += dot_nt(dq_ref[at, :], w_s[:, 2 * cols :])
+
+        @pl.when(t == pl.num_programs(0) - 1)
+        def _():
+            me = lax.axis_index("tensor")
+            own_ref[...] = acc[halo * r :, :]
+            hb_ref[...] = acc[: halo * r, :].astype(BF16)
+            v = x_ref[...].astype(F32)
+            g = jnp.sum(acc[halo * r :, :] * v * inv_rms(v), axis=0, keepdims=True)
+            for j in range(halo):
+                v = xh_ref[j].astype(F32)
+                lo = (halo - 1 - j) * r
+                more = jnp.sum(acc[lo : lo + r, :] * v * inv_rms(v), axis=0, keepdims=True)
+                g = g + jnp.where(me >= j + 1, more, jnp.zeros_like(more))
+            gg_ref[...] = g
+
+    wspec = pl.BlockSpec((dp, 1, wq.shape[2], cols), lambda t: (0, t, 0, 0))
+    col = lambda n: pl.BlockSpec((n, cols), lambda t: (0, t))
+    return pl.pallas_call(
+        kern,
+        grid=(nz,),
+        in_specs=[full((r, d)), full((halo, r, d)), col(r), col(rt), col(rt)] + [wspec] * 3,
+        out_specs=[full((r, d)), full((halo * r, d)), full((1, d))],
+        out_shape=[jax.ShapeDtypeStruct((r, d), F32), jax.ShapeDtypeStruct((halo * r, d), BF16),
+                   jax.ShapeDtypeStruct((1, d), F32)],
+        scratch_shapes=[pltpu.VMEM((rt, d), F32), pltpu.VMEM((d, 3 * cols), BF16)],
+        compiler_params=pltpu.CompilerParams(vmem_limit_bytes=VL, dimension_semantics=("arbitrary",)),
+        name="project_back",
+    )(x, xh, dq, dk, dv, wq, wk, wv)
+
+
+def feed_grads(hid, dg, du, n2, c):
+    nz, r, ff = hid[0].shape
+    half = n2[0].shape[1]
+    nb = half // 128
+
+    def kern(h0, h1, g0, g1, u0, u1, n0, n1, c0, c1, gg, gu, gd):
+        def put(out, a0, a1, b0, b1):
+            y = (dot_tn(a0[0], b0[...]) + dot_tn(a1[0], b1[...])).astype(BF16)
+            for e in range(nb):
+                out[e, 0] = y[:, e * 128 : (e + 1) * 128]
+
+        put(gg, g0, g1, n0, n1)
+        put(gu, u0, u1, n0, n1)
+        put(gd, h0, h1, c0, c1)
+
+    piece = pl.BlockSpec((1, r, ff), lambda t: (t, 0, 0))
+    out = pl.BlockSpec((nb, 1, ff, 128), lambda t: (0, t, 0, 0))
+    return pl.pallas_call(
+        kern,
+        grid=(nz,),
+        in_specs=[piece] * 6 + [full((r, half))] * 4,
+        out_specs=[out] * 3,
+        out_shape=[jax.ShapeDtypeStruct((nb, nz, ff, 128), BF16)] * 3,
+        compiler_params=pltpu.CompilerParams(vmem_limit_bytes=VL, dimension_semantics=("arbitrary",)),
+        name="feed_grads",
+    )(*hid, *dg, *du, *n2, *c)
+
+
+def attn_grads(halo, nz, o, dhb, n1, dq, dk, dv):
+    r, d = o[0].shape
+    half = dhb[0].shape[1]
+    rt = (halo + 1) * r
+    nb, cols = half // 128, d // nz
+
+    def kern(o0, o1, b0, b1, n0, m1, q0, q1, k0, k1, v0, v1, go, gq, gk, gv):
+        y = (dot_tn(o0[...], b0[...]) + dot_tn(o1[...], b1[...])).astype(BF16)
+        for e in range(nb):
+            go[e, 0] = y[:, e * 128 : (e + 1) * 128]
+        own = pl.ds(halo * r, r)
+        for out, p0, p1, a0, a1 in (
+            (gq, q0, q1, n0.at[own], m1.at[own]),
+            (gk, k0, k1, n0, m1),
+            (gv, v0, v1, n0, m1),
+        ):
+            y = (dot_tn(a0[...], p0[...]) + dot_tn(a1[...], p1[...])).astype(BF16)
+            for e in range(nb):
+                out[e, 0] = y[e * 128 : (e + 1) * 128, :]
+
+    col = lambda n: pl.BlockSpec((n, cols), lambda t: (0, t))
+    out1 = pl.BlockSpec((nb, 1, cols, 128), lambda t: (0, t, 0, 0))
+    out2 = pl.BlockSpec((nb, 1, 128, cols), lambda t: (0, t, 0, 0))
+    return pl.pallas_call(
+        kern,
+        grid=(nz,),
+        in_specs=[col(r)] * 2 + [full((r, half))] * 2 + [full((rt, half))] * 2 + [col(r)] * 2 + [col(rt)] * 4,
+        out_specs=[out1, out2, out2, out2],
+        out_shape=[jax.ShapeDtypeStruct((nb, nz, cols, 128), BF16)]
+        + [jax.ShapeDtypeStruct((nb, nz, 128, cols), BF16)] * 3,
+        compiler_params=pltpu.CompilerParams(vmem_limit_bytes=VL, dimension_semantics=("arbitrary",)),
+        name="attn_grads",
+    )(*o, *dhb, *n1, *dq, *dk, *dv)
+
+
+def input_grad(halo, x, gains, dn1, more, dh):
+    r, d = x.shape
+    tile = 256
+
+    def kern(x_ref, gn_ref, dn_ref, m_ref, dh_ref, out_ref):
+        t = lax.axis_index("tensor")
+        nz = lax.axis_size("tensor")
+        dn = dn_ref[...]
+        for j in range(halo):
+            v = m_ref[j].astype(F32)
+            dn = dn + jnp.where(t + j + 1 < nz, v, jnp.zeros_like(v))
+        v = x_ref[...].astype(F32)
+        iv = inv_rms(v)
+        gd = dn * gain_row(gn_ref, 0)
+        out_ref[...] = dh_ref[...] + iv * gd - v * (iv * iv * iv * jnp.mean(v * gd, axis=1, keepdims=True))
+
+    row = pl.BlockSpec((tile, d), lambda i: (i, 0))
+    return pl.pallas_call(
+        kern,
+        grid=(r // tile,),
+        in_specs=[row, full(gains.shape), row, pl.BlockSpec((halo, tile, d), lambda i: (0, i, 0)), row],
+        out_specs=row,
+        out_shape=jax.ShapeDtypeStruct((r, d), F32),
+        compiler_params=pltpu.CompilerParams(vmem_limit_bytes=VL, dimension_semantics=("arbitrary",)),
+        name="input_grad",
+    )(x, gains, dn1, more, dh)
+
+
+class Scatter:
+    def __init__(self, g, src, rows, b_first, bufs, sems, out):
+        self.g, self.src, self.rows, self.b_first, self.out = g, src, rows, b_first, out
+        self.acc, self.r1, self.r2, self.r3 = bufs
+        self.sems, self.next = sems, 0
+        self.sent = []
+
+    def _sem(self):
+        i = self.next
+        self.next += 1
+        return self.sems[0].at[i], self.sems[1].at[i]
+
+    def _e(self, f, s):
+        return s * self.g.nb + f if self.b_first else f * self.g.nb + s
+
+    def _dp(self, f, s, c):
+        return self._e(f, s) * 2 + c
+
+    def _mine(self):
+        a, b, c, t, me = coords(self.g)
+        f, s = (b, a) if self.b_first else (a, b)
+        n1, n2 = (self.g.nb, self.g.na) if self.b_first else (self.g.na, self.g.nb)
+        return f, s, c, t, me, n1, n2
+
+    def start_first(self):
+        f, s, c, t, me, n1, n2 = self._mine()
+        lo, n = self.rows
+        self.own, self.first = [], []
+        for k in range(1, n1):
+            to = (f + k) % n1
+            for j in range(n2):
+                x, y = self._sem()
+                d = send(self.src.at[self._e(to, j), :, pl.ds(lo, n), :], self.r1.at[k - 1, j], x, y, self._dp(to, s, c), t)
+                d.start()
+                self.first.append(d)
+        for j in range(n2):
+            x, _ = self._sem()
+            d = pltpu.make_async_copy(self.src.at[self._e(f, j), :, pl.ds(lo, n), :], self.acc.at[j], x)
+            d.start()
+            self.own.append(d)
+        self.sent += self.first
+
+    def start_second(self):
+        f, s, c, t, me, n1, n2 = self._mine()
+        for d in self.own:
+            d.wait()
+        for d in self.first:
+            d.wait_recv()
+        for j in range(n2):
+
+            @pl.loop(0, self.g.nz)
+            def _(u):
+                v = self.acc[j, u].astype(F32)
+                for k in range(n1 - 1):
+                    v = v + self.r1[k, j, u].astype(F32)
+                self.acc[j, u] = v.astype(BF16)
+
+        self.second = []
+        for k in range(1, n2):
+            to = (s + k) % n2
+            x, y = self._sem()
+            d = send(self.acc.at[to], self.r2.at[k - 1], x, y, self._dp(f, to, c), t)
+            d.start()
+            self.second.append(d)
+        self.sent += self.second
+
+    def start_z(self):
+        f, s, c, t, me, n1, n2 = self._mine()
+        for d in self.second:
+            d.wait_recv()
+
+        @pl.loop(0, self.g.nz)
+        def _(u):
+            v = self.acc[s, u].astype(F32)
+            for k in range(n2 - 1):
+                v = v + self.r2[k, u].astype(F32)
+            self.acc[s, u] = v.astype(BF16)
+
+        self.third = []
+        for k in range(1, self.g.nz):
+            to = (t + k) % self.g.nz
+            x, y = self._sem()
+            d = send(self.acc.at[s, to], self.r3.at[k - 1], x, y, me, to)
+            d.start()
+            self.third.append(d)
+        self.sent += self.third
+
+    def finish(self):
+        f, s, c, t, me, n1, n2 = self._mine()
+        lo, n = self.rows
+        for d in self.third:
+            d.wait_recv()
+        v = self.acc[s, t].astype(F32)
+        for k in range(self.g.nz - 1):
+            v = v + self.r3[k].astype(F32)
+        self.out[pl.ds(lo, n), :] = v
+        for d in self.sent:
+            d.wait_send()
+
+
+def scatter_sems(g):
+    return (g.na - 1) * g.na + g.na + (g.na - 1) + (g.nz - 1)
+
+
+def k2_kernel(g, halo, units, n_w, *refs):
+    refs = list(refs)
+    take = lambda n: [refs.pop(0) for _ in range(n)]
+    gains, hb = take(2)
+    srcs = take(n_w)
+    gout, more = take(2)
+    outs = take(n_w)
+    bufs = [take(4) for _ in units]
+    sems = [take(2) for _ in units]
+    gz, gs, gd = take(3)
+    zss, zrs, dss, drs, hss, hrs = take(6)
+    a, b, c, t, me = coords(g)
+    greet(g, me, t)
+    us = [
+        Scatter(g, srcs[w], rows, bf, bufs[i], sems[i], outs[w]) for i, (w, rows, bf) in enumerate(units)
+    ]
+    pairs = [us[i : i + 2] for i in range(0, len(us), 2)]
+    np_ = len(pairs)
+    r = more.shape[1]
+    hd = []
+    for j in range(halo):
+        d = send(hb.at[pl.ds((halo - 1 - j) * r, r), :], more.at[j], hss.at[j], hrs.at[j], me, (t + g.nz - 1 - j) % g.nz)
+        hd.append(d)
+
+        @pl.when(t >= j + 1)
+        def _():
+            d.start()
+
+    zg = []
+    for k in range(1, g.nz):
+        d = send(gains, gz.at[k - 1], zss.at[k - 1], zrs.at[k - 1], me, (t + k) % g.nz)
+        d.start()
+        zg.append(d)
+    for p in range(min(2, np_)):
+        for u in pairs[p]:
+            u.start_first()
+    for d in zg:
+        d.wait()
+    tot = gains[...]
+    for k in range(g.nz - 1):
+        tot = tot + gz[k]
+    for e in range(g.dp):
+        gs[e] = tot[:, e * 128 : (e + 1) * 128]
+    dg = []
+    for k in range(1, g.dp):
+        to = (me + k) % g.dp
+        d = send(gs.at[to], gd.at[me], dss.at[k], drs.at[k], to, t)
+        d.start()
+        dg.append(d)
+    own = pltpu.make_async_copy(gs.at[me], gd.at[me], dss.at[0])
+    own.start()
+    for p in range(np_):
+        for u in pairs[p]:
+            u.start_second()
+        if p + 2 < np_:
+            for u in pairs[p + 2]:
+                u.start_first()
+        if p >= 1:
+            for u in pairs[p - 1]:
+                u.start_z()
+    for u in pairs[-1]:
+        u.start_z()
+    own.wait()
+    for d in dg:
+        d.wait()
+    v = gd[0]
+    for e in range(1, g.dp):
+        v = v + gd[e]
+    gout[...] = v
+    for u in us:
+        u.finish()
+    for j, d in enumerate(hd):
+
+        @pl.when(t >= j + 1)
+        def _():
+            d.wait_send()
+
+        @pl.when(t + j + 1 < g.nz)
+        def _():
+            d.wait_recv()
+
+
+def halves(srcs_rows):
+    units = []
+    for item in srcs_rows:
+        if len(item) == 2:
+            (w0, n0), (w1, n1) = item
+            units += [(w0, (0, n0), True), (w1, (0, n1), False)]
+        else:
+            ((w, n),) = item
+            units += [(w, (0, n // 2), True), (w, (n // 2, n - n // 2), False)]
+    return units
+
+
+def k2(g, halo, gains, hb, srcs, units, r):
+    any_ = pl.BlockSpec(memory_space=pl.ANY)
+    vm = pl.BlockSpec(memory_space=pltpu.VMEM)
+    dma = lambda *n: pltpu.SemaphoreType.DMA(n)
+    d = hb.shape[1]
+    n_w = len(srcs)
+    scratch = []
+    for w, (lo, n), bf in units:
+        cols = srcs[w].shape[3]
+        n1, n2 = (g.nb, g.na) if bf else (g.na, g.nb)
+        scratch += [
+            pltpu.VMEM((n2, g.nz, n, cols), BF16),
+            pltpu.VMEM((n1 - 1, n2, g.nz, n, cols), BF16),
+            pltpu.VMEM((n2 - 1, g.nz, n, cols), BF16),
+            pltpu.VMEM((g.nz - 1, n, cols), BF16),
+        ]
+    scratch += [dma(scatter_sems(g))] * (2 * len(units))
+    scratch += [pltpu.VMEM((g.nz - 1,) + gains.shape, F32), pltpu.VMEM((g.dp, 2, 128), F32), pltpu.VMEM((g.dp, 2, 128), F32)]
+    scratch += [dma(g.nz), dma(g.nz), dma(g.dp), dma(g.dp), dma(halo), dma(halo)]
+    out_shape = [jax.ShapeDtypeStruct((2, 128), F32), jax.ShapeDtypeStruct((halo, r, d), BF16)] + [
+        jax.ShapeDtypeStruct(s.shape[2:], F32) for s in srcs
+    ]
+    return pl.pallas_call(
+        functools.partial(k2_kernel, g, halo, units, n_w),
+        out_shape=out_shape,
+        in_specs=[vm, any_] + [any_] * n_w,
+        out_specs=[vm, any_] + [vm] * n_w,
+        scratch_shapes=scratch,
+        compiler_params=pltpu.CompilerParams(collective_id=1, has_side_effects=True, vmem_limit_bytes=60 * 2**20),
+        name="bwd_exchange",
+    )(gains, hb, *srcs)
+
+
+HEADS = 8
+QB = 512
 
 
 def normalize(field, gain_vec):
@@ -85,7 +1098,7 @@
     return lax.all_gather(local_grad, "tensor", axis=0, tiled=True)
 
 
-def on_device(
+def on_device_any(
     block_in,
     segments,
     retrieved,
@@ -317,40 +1330,94 @@
     return (block_out[None], grad_in[None]) + results
 
 
+def cover(halo, r, t):
+    half = HD // 2
+    freq = 10000.0 ** (-jnp.arange(half, dtype=F32) * 2.0 / HD)
+    pos = (t * r - halo * r + jnp.arange((halo + 1) * r)).astype(F32)
+    ang = pos[:, None] * freq[None, :]
+    cos, sin = jnp.cos(ang), jnp.sin(ang)
+    return jnp.concatenate([cos, cos], axis=1), jnp.concatenate([-sin, sin], axis=1)
+
+
+def on_device(*args):
+    x, dp = args[0], lax.axis_size("dp")
+    side = math.isqrt(dp // 2)
+    if 2 * side * side == dp and x.shape[2] % (128 * dp) == 0:
+        return on_device_rows(*args)
+    return on_device_any(*args)
+
+
+def on_device_rows(
+    block_in, segments, retrieved, partner, memory_keys, memory_values,
+    gain_attn, w_query, w_key, w_value, w_out, gain_ffn, w_gate, w_up, w_down, cotangent,
+):
+    g = Grid(lax.axis_size("dp"), lax.axis_size("tensor"))
+    t, me = lax.axis_index("tensor"), lax.axis_index("dp")
+    x, c = block_in[0], cotangent[0]
+    r, d = x.shape
+    seq_len = segments.shape[1]
+    window = seq_len // 4
+    halo = -(-window // r)
+    nq, ksel = retrieved.shape[1:]
+    cap = max(2, -(-2 * nq * ksel // g.dp))
+    req, sel = plan_requests(retrieved[0], partner[0], g.dp, memory_keys.shape[1], cap)
+    gains = jnp.stack([gain_attn, gain_ffn]).astype(F32)
+    flat = lambda m: m.reshape((-1,) + m.shape[2:])
+    shards = [w_query, w_key, w_value, w_out, w_gate.T, w_up.T, w_down]
+    wq, wk, wv, wo, wg, wu, wd, xh, gn, mk, mv = k1(
+        g, cap, halo, req, sel, x, gains, flat(memory_keys), flat(memory_values), shards, nq, ksel
+    )
+    cos, sin = cover(halo, r, t)
+    padded = jnp.concatenate([jnp.full((halo * r,), -1, jnp.int32), segments[0]])
+    seg = lax.dynamic_slice(padded, (t * r,), ((halo + 1) * r,))
+    seg_k, seg_q = seg[None, :], seg[halo * r :, None]
+
+    n1, q, k, v = project(halo, None, x, xh, gn, cos, sin, wq, wk, wv)
+    o, lse = attend(halo, window, q, k, v, mk, mv, seg_q, seg_k)
+    h, n2 = out_norm(x, o, wo, gn)
+    hid, dg, du, block_out, dh, dhb, do, gg_ffn = feed(h, n2, c, gn, wg, wu, wd, wo)
+    do = jnp.transpose(do, (1, 0, 2)).reshape(r, d)
+    dq, dk, dv = attend_back(halo, window, q, k, v, mk, mv, seg_q, seg_k, o, lse, do, cos, sin)
+    dn1, hb, gg_attn = project_back(halo, x, xh, dq, dk, dv, wq, wk, wv)
+
+    core = me % 2
+    pairs = [(i, i ^ 1) for i in range(g.dp)]
+    other = lambda y: lax.ppermute(y, "dp", pairs)
+
+    def cut(y):
+        z = y.reshape(y.shape[0], d // 256, 2, 128)
+        mine = lax.dynamic_index_in_dim(z, core, 2, False).reshape(y.shape[0], d // 2)
+        theirs = lax.dynamic_index_in_dim(z, 1 - core, 2, False).reshape(y.shape[0], d // 2)
+        return mine, other(theirs)
+
+    both = lambda y: (y, other(y))
+    ggt, gut, gdn = feed_grads(both(hid), both(dg), both(du), cut(n2), cut(c))
+    go, gq, gk, gv = attn_grads(halo, g.nz, both(o), cut(dhb), cut(n1), both(dq), both(dk), both(dv))
+    srcs = [ggt, gut, gdn, go, gq, gk, gv]
+    n = lambda w: (w, srcs[w].shape[2])
+    units = halves([(n(0), n(1)), (n(2),), (n(3),), (n(4), n(5)), (n(6),)])
+    gains_part = jnp.concatenate([gg_attn, gg_ffn], axis=0)
+    gout, more, o_gate, o_up, o_down, o_out, o_q, o_k, o_v = k2(g, halo, gains_part, hb, srcs, units, r)
+    grad_in = input_grad(halo, x, gn, dn1, more, dh)
+    return (
+        block_out[None], grad_in[None], gout[0], o_q, o_k, o_v, o_out, gout[1], o_gate.T, o_up.T, o_down,
+    )
+
+
 def solution(mesh):
     return jax.shard_map(
         on_device,
         mesh=mesh,
         in_specs=(
-            P("dp", "tensor", None),
-            P("dp", None),
-            P("dp", None, None),
-            P("dp"),
-            P(None, "dp", None, "tensor"),
-            P(None, "dp", None, "tensor"),
-            P("dp"),
-            P("dp", "tensor"),
-            P("dp", "tensor"),
-            P("dp", "tensor"),
-            P("tensor", "dp"),
-            P("dp"),
-            P("dp", "tensor"),
-            P("dp", "tensor"),
-            P("tensor", "dp"),
-            P("dp", "tensor", None),
+            P("dp", "tensor", None), P("dp", None), P("dp", None, None), P("dp"),
+            P(None, "dp", None, "tensor"), P(None, "dp", None, "tensor"),
+            P("dp"), P("dp", "tensor"), P("dp", "tensor"), P("dp", "tensor"), P("tensor", "dp"),
+            P("dp"), P("dp", "tensor"), P("dp", "tensor"), P("tensor", "dp"), P("dp", "tensor", None),
         ),
         out_specs=(
-            P("dp", "tensor", None),
-            P("dp", "tensor", None),
-            P("dp"),
-            P("dp", "tensor"),
-            P("dp", "tensor"),
-            P("dp", "tensor"),
-            P("tensor", "dp"),
-            P("dp"),
-            P("dp", "tensor"),
-            P("dp", "tensor"),
-            P("tensor", "dp"),
+            P("dp", "tensor", None), P("dp", "tensor", None),
+            P("dp"), P("dp", "tensor"), P("dp", "tensor"), P("dp", "tensor"), P("tensor", "dp"),
+            P("dp"), P("dp", "tensor"), P("dp", "tensor"), P("tensor", "dp"),
         ),
         check_vma=False,
     )

time: 1340 us -> 624 us (0.47)
  waiting for transfers between devices: 604 us -> 0.03 us
  Pallas kernels: 0 us -> 521 us
  matrix products: 273 us -> 0 us
  blocking collectives: 176 us -> 0 us
  other arithmetic: 123 us -> 6.05 us
  local copies, waits for them, and re-layouts: 127 us -> 88.6 us
  between operations: 18.1 us -> 1.75 us
    pallas_call x0 -> x11, Pallas kernels: none -> 521 us  [the longest x1 215 us: k1(): pl.pallas_call(functools.partial(k1_kernel, g, cap, nq, ksel, halo, units...]
    reduce_scatter x7 -> x0, waiting for transfers between devices: 350 us -> none  [the longest x2 153 us: return_rows(): lax.psum_scatter(summed.astype(jnp.bfloat16), 'tensor', scatter_dimension...]
    dot_general x57 -> x0, matrix products: 273 us -> none  [the longest x4 55.2 us: backward_block(): jnp.einsum('qhd,khd->hqk', grad_blk, values_both, preferred_element_type=...]
    all_gather x7 -> x0, waiting for transfers between devices: 250 us -> none  [the longest x2 135 us: all_rows(): return lax.all_gather(local_grad, 'tensor', axis=0, tiled=True)]
    all_gather x6 -> x0, blocking collectives: 143 us -> none  [the longest x1 52.9 us: on_device(): lax.all_gather(w_query, 'dp', axis=0, tiled=True)]
    convert_element_type x22 -> x2, other arithmetic: 55.9 us -> 1.24 us  [the longest x1 1.24 us: on_device_rows(): gains = jnp.stack([gain_attn, gain_ffn]).astype(F32)]
    gather x4 -> x0, local copies, waits for them, and re-layouts: 21.6 us -> none  [the longest x1 6.26 us: on_device(): picked_keys = memory_keys[received[..., 0], received[..., 1]]]
    reduce_sum x9 -> x2, other arithmetic: 21.3 us -> 0.3 us  [the longest x1 0.18 us: plan_requests(): jnp.sum(((owner[:, None] == owner[None, :]) & (i[None, :] < i[:, None]))....]
  transfers between devices with their start and end apart: 20 -> 11, of which waited for: 12 -> 0; matrix products, arithmetic and copies ran while one was open for 26% -> 12% of each run, Pallas kernels for 0% -> 5%
where the time goes in v1:
time: 624 us; the launch traced here: 621 us
  Pallas kernels  521 us (83%)
  local copies, waits for them, and re-layouts  88.6 us (14%)
    pallas_call x1, Pallas kernels, k1(): pl.pallas_call(functools.partial(k1_kernel, g, cap, nq, ksel, halo, units...  215 us
    pallas_call x1, Pallas kernels, k2(): pl.pallas_call(functools.partial(k2_kernel, g, halo, units, n_w), out_sha...  147 us
    pallas_call x1, Pallas kernels, feed(): pl.pallas_call(kern, grid=(nz,), in_specs=[one((r, d)), one((r, d)), one(...  47.8 us
    dynamic_slice x4, local copies, waits for them, and re-layouts, cut(): lax.dynamic_index_in_dim(z, 1 - core, 2, False).reshape(y.shape[0], d // 2)  37.3 us
    pallas_call x1, Pallas kernels, attend_back(): pl.pallas_call(kern, grid=(d // HD,), in_specs=[head(r), head(rt), head(r...  21.4 us
    pallas_call x1, Pallas kernels, attend(): pl.pallas_call(kern, grid=(d // HD,), in_specs=[head(r), head(rt), head(r...  17.4 us
    pallas_call x1, Pallas kernels, project(): pl.pallas_call(kern, grid=(nz,), in_specs=[full((r, d)), full((halo, r, d...  17 us
    pallas_call x1, Pallas kernels, project_back(): pl.pallas_call(kern, grid=(nz,), in_specs=[full((r, d)), full((halo, r, d...  16.5 us
  transfers between devices with their start and end apart: 11, of which 0 were waited for; matrix products, arithmetic and copies ran while one was open for 12% of the time, Pallas kernels for 5%

profile of v1, /device:TPU:0, one launch (start us, length us, event | category | flops | bytes accessed | tf_op | source)
XLA Modules:
  0.0 620.5 jit_solution(16228380164213012636)
XLA Ops:
  9.8 215.1 %fwd_exchange.1 = (bf16[8,4,128,256]{3,2,1,0:T(8,128)(2,1)}, bf16[8,4,128,256]{3,2,1,0:T(8,128)(2,1)}, bf16[8,4,128,256]{3,2,1,0:T(8,128)(2,1)}, bf16[8,4,256,12...) custom-call(s32[8,8,128]{2,1,0:T(8,128)} %broadcast_in_dim.54.refs_0, ...), custom_call_target="tpu_custom_call" | custom-call | tf_op jit(solution)/shard_map/fwd_exchange/pallas_call | solution.py:303
  224.9 17.0 %project.1 = (bf16[1024,1024]{1,0:T(8,128)(2,1)}, bf16[512,1024]{1,0:T(8,128)(2,1)}, bf16[1024,1024]{1,0:T(8,128)(2,1)}, bf16[1024,1024]{1,0:T(8,128)(2,1)}) custom-call(bf16[512,1024]{1,0:T(8,128)(2,1)} %bitcast.57, bf16[1,512,1024]{2,1,0:T(8,128)(2,1)} %get-tuple-element.60.xh_ref, f32[8,2,128]{2,1,0:T(2,128)} %get-tuple-element.61.gn_ref, ...), custom_call_target="tpu_custom_call" | custom-call | tf_op jit(solution)/shard_map/project/pallas_call | solution.py:421
  241.9 17.4 %attend.1 = (bf16[512,1024]{1,0:T(8,128)(2,1)}, f32[8,512,1]{2,1,0:T(8,128)}) custom-call(bf16[512,1024]{1,0:T(8,128)(2,1)} %get-tuple-element.65.q_ref, bf16[1024,1024]{1,0:T(8,128)(2,1)} %get-tuple-element.66.k_ref, bf16[1024,1024]{1,0:T(8,128)(2,1)} %get-tuple-element.67.v_ref, bf16[4,8,128,256]{3,2,1,0:T(8,128)(2,1)} %get-tuple-element.68.mk_ref, ...), custom_call_target="tpu_custom_call" | custom-call | tf_op jit(solution)/shard_map/attend/pallas_call | solution.py:478
  259.3 6.8 %out_norm.1 = (f32[512,1024]{1,0:T(8,128)}, bf16[512,1024]{1,0:T(8,128)(2,1)}) custom-call(bf16[512,1024]{1,0:T(8,128)(2,1)} %bitcast.58, bf16[512,1024]{1,0:T(8,128)(2,1)} %get-tuple-element.70.o_ref.o0, bf16[8,4,256,128]{3,2,1,0:T(8,128)(2,1)} %get-tuple-element.71.w_ref.wo_ref, f32[8,2,128]{2,1,0:T(2,128)} %get-tuple-element.61.gn_ref), custom_call_target="tpu_custom_call" | custom-call | tf_op jit(solution)/shard_map/out_norm/pallas_call | solution.py:562
  266.1 47.8 %feed.1 = (bf16[4,512,704]{2,1,0:T(8,128)(2,1)}, bf16[4,512,704]{2,1,0:T(8,128)(2,1)}, bf16[4,512,704]{2,1,0:T(8,128)(2,1)}, f32[512,1024]{1,0:T(8,128)}, f32[51...) custom-call(f32[512,1024]{1,0:T(8,128)} %get-tuple-element.72.h_ref, ...), custom_call_target="tpu_custom_call" | custom-call | tf_op jit(solution)/shard_map/feed/pallas_call | solution.py:632
  313.9 2.3 copy.89
  316.2 21.4 %attend_back.1 = (bf16[512,1024]{1,0:T(8,128)(2,1)}, bf16[1024,1024]{1,0:T(8,128)(2,1)}, bf16[1024,1024]{1,0:T(8,128)(2,1)}) custom-call(bf16[512,1024]{1,0:T(8,128)(2,1)} %get-tuple-element.65.q_ref, bf16[1024,1024]{1,0:T(8,128)(2,1)} %get-tuple-element.66.k_ref, bf16[1024,1024]{1,0:T(8,128)(2,1)} %get-tuple-element.67.v_ref, ...), custom_call_target="tpu_custom_call" | custom-call | tf_op jit(solution)/shard_map/attend_back/pallas_call | solution.py:525
  338.1 3.2 reshape.299
  341.3 14.2 %dynamic-slice_reduce_fusion = (bf16[1024,4,128]{2,1,0:T(4,128)(2,1)S(1)}, bf16[1024,4,128]{2,1,0:T(4,128)(2,1)}) fusion(bf16[1024,4,2,128]{3,2,1,0:T(2,128)(2,1)S(1)} %reshape.299, s32[]{:T(128)S(6)} %select_n.98, s32[]{:T(128)S(6)} %select_n.97), kind=kLoop, calls=%fused_computation | loop fusion | bytes 4194312 | tf_op jit(solution)/shard_map/jit(dynamic_index_in_dim)/dynamic_slice | solution.py:1390
  357.2 1.9 reshape.296
  359.1 9.1 %dynamic-slice_reduce_fusion.2 = (bf16[512,4,128]{2,1,0:T(4,128)(2,1)S(1)}, bf16[512,4,128]{2,1,0:T(4,128)(2,1)}) fusion(bf16[512,4,2,128]{3,2,1,0:T(2,128)(2,1)} %reshape.296, s32[]{:T(128)S(6)} %select_n.98, s32[]{:T(128)S(6)} %select_n.97), kind=kLoop, calls=%fused_computation.4 | loop fusion | bytes 2097160 | tf_op jit(solution)/shard_map/jit(dynamic_index_in_dim)/dynamic_slice | solution.py:1390
  369.2 2.7 copy.67
  372.3 4.7 copy.68
  377.1 2.8 copy.69
  383.6 7.3 %dynamic-slice_reduce_fusion.6 = (bf16[512,4,128]{2,1,0:T(4,128)(2,1)S(1)}, bf16[512,4,128]{2,1,0:T(4,128)(2,1)}) fusion(bf16[512,4,2,128]{3,2,1,0:T(2,128)(2,1)S(1)} %reshape.291, s32[]{:T(128)S(6)} %select_n.98, s32[]{:T(128)S(6)} %select_n.97), kind=kLoop, calls=%fused_computation.8 | loop fusion | bytes 2097160 | tf_op jit(solution)/shard_map/jit(dynamic_index_in_dim)/dynamic_slice | solution.py:1390
  391.0 6.8 %dynamic-slice_reduce_fusion.4 = (bf16[512,4,128]{2,1,0:T(4,128)(2,1)S(1)}, bf16[512,4,128]{2,1,0:T(4,128)(2,1)S(1)}) fusion(bf16[512,4,2,128]{3,2,1,0:T(2,128)(2,1)S(1)} %reshape_squeeze.7, s32[]{:T(128)S(6)} %select_n.98, s32[]{:T(128)S(6)} %select_n.97), kind=kLoop, calls=%fused_computation.6 | loop fusion | bytes 2097160 | tf_op jit(solution)/shard_map/jit(dynamic_index_in_dim)/dynamic_slice | solution.py:1390
  399.2 16.5 %project_back.1 = (f32[512,1024]{1,0:T(8,128)}, bf16[512,1024]{1,0:T(8,128)(2,1)}, f32[1,1024]{1,0:T(1,128)}) custom-call(bf16[512,1024]{1,0:T(8,128)(2,1)} %bitcast.59, bf16[1,512,1024]{2,1,0:T(8,128)(2,1)} %get-tuple-element.60.xh_ref, bf16[512,1024]{1,0:T(8,128)(2,1)} %get-tuple-element.80.dq_ref.q0, bf16[1024,1024]{1,0:T(8,128)(2,1)} %get-tuple-element.81.dk_ref.k0, ...), custom_call_target="tpu_custom_call" | custom-call | tf_op jit(solution)/shard_map/project_back/pallas_call | solution.py:690
  420.1 12.1 %attn_grads.1 = (bf16[4,4,256,128]{3,2,1,0:T(8,128)(2,1)}, bf16[4,4,128,256]{3,2,1,0:T(8,128)(2,1)}, bf16[4,4,128,256]{3,2,1,0:T(8,128)(2,1)}, bf16[4,4,128,256]{3,2,1,0:T(8,128)(2,1)}) custom-call(bf16[512,1024]{1,0:T(8,128)(2,1)} %get-tuple-element.70.o_ref.o0, bf16[512,1024]{1,0:T(8,128)(2,1)} %collective-permute-done.5.o1, bf16[512,512]{1,0:T(8,128)(2,1)} %bitcast.71, ...), custom_call_target="tpu_custom_call" | custom-call | tf_op jit(solution)/shard_map/attn_grads/pallas_call | solution.py:754
  432.2 4.6 copy.74.h1
  436.8 4.6 copy.75.g1
  441.4 4.6 copy.76.u1
  447.1 15.3 %feed_grads.1 = (bf16[4,4,704,128]{3,2,1,0:T(8,128)(2,1)}, bf16[4,4,704,128]{3,2,1,0:T(8,128)(2,1)}, bf16[4,4,704,128]{3,2,1,0:T(8,128)(2,1)}) custom-call(bf16[4,512,704]{2,1,0:T(8,128)(2,1)} %get-tuple-element.87.h0, bf16[4,512,704]{2,1,0:T(8,128)(2,1)} %copy.74.h1, bf16[4,512,704]{2,1,0:T(8,128)(2,1)} %get-tuple-element.88.g0, ...), custom_call_target="tpu_custom_call" | custom-call | tf_op jit(solution)/shard_map/feed_grads/pallas_call | solution.py:720
  462.4 147.4 %bwd_exchange.1 = (f32[2,128]{1,0:T(2,128)}, bf16[1,512,1024]{2,1,0:T(8,128)(2,1)}, f32[704,128]{1,0:T(8,128)}, f32[704,128]{1,0:T(8,128)}, f32[704,128]{1,0:T(8...) custom-call(f32[2,1024]{1,0:T(2,128)} %pad_maximum_fusion.2.refs_0_, ...), custom_call_target="tpu_custom_call" | custom-call | tf_op jit(solution)/shard_map/bwd_exchange/pallas_call | solution.py:1014
  611.1 4.4 input_grad.1
  (95 shorter events, 28.8 us)
Async XLA Ops:
  3.7 5.5 copy-start.16
  337.6 42.4 %collective-permute-start.8 = (bf16[512,1024]{1,0:T(8,128)(2,1)}, bf16[512,1024]{1,0:T(8,128)(2,1)}, u32[]{:S(2)}, u32[]{:S(2)}) collective-permute-start(bf16[512,1024]{1,0:T(8,128)(2,1)} %get-tuple-element.80.dq_ref.q0), channel_id=1, source_target_pairs={{0,4},{4,0},{8,12},{12,8},{16,20},{20,16},{24,28},{28,24},{1,5},{5... | collective-permute-start | bytes 3145736 | tf_op jit(solution)/shard_map/ppermute | solution.py:1385
  356.7 23.7 %collective-permute-start.7 = (bf16[1024,512]{1,0:T(8,128)(2,1)}, bf16[1024,512]{1,0:T(8,128)(2,1)}, u32[]{:S(2)}, u32[]{:S(2)}) collective-permute-start(bf16[1024,512]{1,0:T(8,128)(2,1)} %bitcast.47), channel_id=1, source_target_pairs={{0,4},{4,0},{8,12},{12,8},{16,20},{20,16},{24,28},{28,24},{1,5},{5... | collective-permute-start | bytes 3145736 | tf_op jit(solution)/shard_map/ppermute | solution.py:1385
  356.8 23.7 %collective-permute-start.5 = (bf16[512,1024]{1,0:T(8,128)(2,1)}, bf16[512,1024]{1,0:T(8,128)(2,1)}, u32[]{:S(2)}, u32[]{:S(2)}) collective-permute-start(bf16[512,1024]{1,0:T(8,128)(2,1)} %get-tuple-element.70.o_ref.o0), channel_id=1, source_target_pairs={{0,4},{4,0},{8,12},{12,8},{16,20},{20,16},{24,28},{28,24},{1,5},{5... | collective-permute-start | bytes 3145736 | tf_op jit(solution)/shard_map/ppermute | solution.py:1385
  359.1 10.1 %copy-start = (bf16[4,512,704]{2,1,0:T(8,128)(2,1)S(1)}, bf16[4,512,704]{2,1,0:T(8,128)(2,1)}, u32[]{:S(2)}) copy-start(bf16[4,512,704]{2,1,0:T(8,128)(2,1)} %get-tuple-element.87.h0) | copy-start | bytes 8650756
  369.1 10.7 %collective-permute-start.6 = (bf16[512,512]{1,0:T(8,128)(2,1)}, bf16[512,512]{1,0:T(8,128)(2,1)}, u32[]{:S(2)}, u32[]{:S(2)}) collective-permute-start(bf16[512,512]{1,0:T(8,128)(2,1)} %bitcast.49), channel_id=1, source_target_pairs={{0,4},{4,0},{8,12},{12,8},{16,20},{20,16},{24,28},{28,24},{1,5},{5... | collective-permute-start | bytes 1572872 | tf_op jit(solution)/shard_map/ppermute | solution.py:1385
  371.9 60.3 %collective-permute-start = (bf16[4,512,704]{1,2,0:T(8,128)(2,1)}, bf16[4,512,704]{1,2,0:T(8,128)(2,1)}, u32[]{:S(2)}, u32[]{:S(2)}) collective-permute-start(bf16[4,512,704]{1,2,0:T(8,128)(2,1)} %copy.67), channel_id=1, source_target_pairs={{0,4},{4,0},{8,12},{12,8},{16,20},{20,16},{24,28},{28,24},{1,5},{5... | collective-permute-start | bytes 8650760 | tf_op jit(solution)/shard_map/ppermute | solution.py:1385
  372.3 4.7 copy-start.1
  379.8 57.0 %collective-permute-start.1 = (bf16[4,512,704]{1,2,0:T(8,128)(2,1)}, bf16[4,512,704]{1,2,0:T(8,128)(2,1)}, u32[]{:S(2)}, u32[]{:S(2)}) collective-permute-start(bf16[4,512,704]{1,2,0:T(8,128)(2,1)} %copy.68), channel_id=1, source_target_pairs={{0,4},{4,0},{8,12},{12,8},{16,20},{20,16},{24,28},{28,24},{1,5},{5... | collective-permute-start | bytes 8650760 | tf_op jit(solution)/shard_map/ppermute | solution.py:1385
  380.0 61.5 %collective-permute-start.2 = (bf16[4,512,704]{1,2,0:T(8,128)(2,1)}, bf16[4,512,704]{1,2,0:T(8,128)(2,1)}, u32[]{:S(2)}, u32[]{:S(2)}) collective-permute-start(bf16[4,512,704]{1,2,0:T(8,128)(2,1)} %copy.69), channel_id=1, source_target_pairs={{0,4},{4,0},{8,12},{12,8},{16,20},{20,16},{24,28},{28,24},{1,5},{5... | collective-permute-start | bytes 8650760 | tf_op jit(solution)/shard_map/ppermute | solution.py:1385
  380.4 18.3 %collective-permute-start.10 = (bf16[1024,1024]{1,0:T(8,128)(2,1)}, bf16[1024,1024]{1,0:T(8,128)(2,1)}, u32[]{:S(2)}, u32[]{:S(2)}) collective-permute-start(bf16[1024,1024]{1,0:T(8,128)(2,1)} %get-tuple-element.82.dv_ref.v0), channel_id=1, source_target_pairs={{0,4},{4,0},{8,12},{12,8},{16,20},{20,16},{24,28},{28,24},{1,5},{5... | collective-permute-start | bytes 6291464 | tf_op jit(solution)/shard_map/ppermute | solution.py:1385
  380.5 18.3 %collective-permute-start.9 = (bf16[1024,1024]{1,0:T(8,128)(2,1)}, bf16[1024,1024]{1,0:T(8,128)(2,1)}, u32[]{:S(2)}, u32[]{:S(2)}) collective-permute-start(bf16[1024,1024]{1,0:T(8,128)(2,1)} %get-tuple-element.81.dk_ref.k0), channel_id=1, source_target_pairs={{0,4},{4,0},{8,12},{12,8},{16,20},{20,16},{24,28},{28,24},{1,5},{5... | collective-permute-start | bytes 6291464 | tf_op jit(solution)/shard_map/ppermute | solution.py:1385
  398.7 47.3 %collective-permute-start.3 = (bf16[512,512]{1,0:T(8,128)(2,1)S(1)}, bf16[512,512]{1,0:T(8,128)(2,1)S(1)}, u32[]{:S(2)}, u32[]{:S(2)}) collective-permute-start(bf16[512,512]{1,0:T(8,128)(2,1)S(1)} %bitcast.79), channel_id=1, source_target_pairs={{0,4},{4,0},{8,12},{12,8},{16,20},{20,16},{24,28},{28,24},{1,5},{5... | collective-permute-start | bytes 1572872 | tf_op jit(solution)/shard_map/ppermute | solution.py:1385
  398.8 16.9 %copy-start.4 = (bf16[512,4,128]{2,1,0:T(4,128)(2,1)S(1)}, bf16[512,4,128]{2,1,0:T(4,128)(2,1)}, u32[]{:S(2)}) copy-start(bf16[512,4,128]{2,1,0:T(4,128)(2,1)} %get-tuple-element.112) | copy-start | bytes 1572868
  398.8 17.8 %copy-start.2 = (bf16[1024,4,128]{2,1,0:T(4,128)(2,1)S(1)}, bf16[1024,4,128]{2,1,0:T(4,128)(2,1)}, u32[]{:S(2)}) copy-start(bf16[1024,4,128]{2,1,0:T(4,128)(2,1)} %get-tuple-element.110) | copy-start | bytes 3145732
  398.8 47.2 %collective-permute-start.4 = (bf16[512,512]{1,0:T(8,128)(2,1)}, bf16[512,512]{1,0:T(8,128)(2,1)S(1)}, u32[]{:S(2)}, u32[]{:S(2)}) collective-permute-start(bf16[512,512]{1,0:T(8,128)(2,1)} %bitcast.51), channel_id=1, source_target_pairs={{0,4},{4,0},{8,12},{12,8},{16,20},{20,16},{24,28},{28,24},{1,5},{5... | collective-permute-start | bytes 1572872 | tf_op jit(solution)/shard_map/ppermute | solution.py:1385
  416.6 2.9 copy-start.18
  611.0 4.4 copy-start.15
  611.0 5.1 copy-start.14
  611.0 5.7 copy-start.13
  611.0 6.4 %copy-start.12 = (f32[256,128]{1,0:T(8,128)S(1)}, f32[256,128]{1,0:T(8,128)}, u32[]{:S(2)}) copy-start(f32[256,128]{1,0:T(8,128)} %get-tuple-element.143) | copy-start | bytes 393220
  611.0 7.0 %copy-start.11 = (f32[704,128]{1,0:T(8,128)S(1)}, f32[704,128]{1,0:T(8,128)}, u32[]{:S(2)}) copy-start(f32[704,128]{1,0:T(8,128)} %get-tuple-element.106) | copy-start | bytes 1081348
  611.0 7.8 %copy-start.10 = (f32[704,128]{1,0:T(8,128)S(1)}, f32[704,128]{1,0:T(8,128)}, u32[]{:S(2)}) copy-start(f32[704,128]{1,0:T(8,128)} %get-tuple-element.107) | copy-start | bytes 1081348
  615.4 4.1 copy-start.9
  (6 other events, 11.4 us)

commit v2 on v1

--- a/solution.py
+++ b/solution.py
@@ -143,172 +143,6 @@
 
 def gather_sems(g):
     return g.nz + (g.na - 1) + g.na * (g.na - 1) + g.na * g.nb
-
-
-def k1_kernel(g, cap, nq, ksel, halo, units, n_w, *refs):
-    refs = list(refs)
-    take = lambda n: [refs.pop(0) for _ in range(n)]
-    requests, sel = take(2)
-    x, gains, mem_k, mem_v = take(4)
-    shards = take(n_w)
-    bufs = take(n_w)
-    xh, gains_all, mk, mv = take(4)
-    loc_k, loc_v, stage_k, stage_v, rec_k, rec_v, zst_k, zst_v = take(8)
-    req_in, req_s = take(2)
-    ss, rs, msl, mss, mrs, zss, zrs, xss, xrs, qss, qrs, gss, grs = take(13)
-    a, b, c, t, me = coords(g)
-    greet(g, me, t)
-    rq, gn = [], []
-    for k in range(1, g.dp):
-        to = (me + k) % g.dp
-        d = send(requests.at[to], req_in.at[me], qss.at[k], qrs.at[k], to, t)
-        d.start()
-        rq.append(d)
-    for k in range(1, g.dp):
-        to = (me + k) % g.dp
-        d = send(gains, gains_all.at[me], gss.at[k], grs.at[k], to, t)
-        d.start()
-        gn.append(d)
-    own_r = pltpu.make_async_copy(requests.at[me], req_in.at[me], qss.at[0])
-    own_r.start()
-    own_g = pltpu.make_async_copy(gains, gains_all.at[me], gss.at[0])
-    own_g.start()
-    lk = pltpu.make_async_copy(mem_k, loc_k, msl.at[0])
-    lv = pltpu.make_async_copy(mem_v, loc_v, msl.at[1])
-    lk.start()
-    lv.start()
-    per = gather_sems(g)
-    gs = [Gather(g, shards[w], bufs[w], rows, bf, (ss, rs), i * per) for i, (w, rows, bf) in enumerate(units)]
-    for u in gs[:4]:
-        u.start_z()
-    xs = []
-    for k in range(1, halo + 1):
-        d = send(x, xh.at[k - 1], xss.at[k - 1], xrs.at[k - 1], me, (t + k) % g.nz)
-        xs.append(d)
-
-        @pl.when(t + k < g.nz)
-        def _():
-            d.start()
-
-    own_r.wait()
-    own_g.wait()
-    for d in rq:
-        d.wait()
-    cp = pltpu.make_async_copy(req_in, req_s, qrs.at[0])
-    cp.start()
-    cp.wait()
-
-    def exchange(loc, stage, rec, i, load):
-        load.wait()
-
-        @pl.loop(0, g.dp)
-        def _(s):
-            for k in range(cap):
-                stage[s, k] = loc[req_s[s, 0, k]]
-
-        out = []
-        for k in range(1, g.dp):
-            to = (me + k) % g.dp
-            d = send(stage.at[to], rec.at[me], mss.at[i, k], mrs.at[i, k], to, t)
-            d.start()
-            out.append(d)
-        own = pltpu.make_async_copy(stage.at[me], rec.at[me], mss.at[i, 0])
-        own.start()
-        return out + [own]
-
-    ek = exchange(loc_k, stage_k, rec_k, 0, lk)
-    for u in gs[:4]:
-        u.start_first()
-    ev = exchange(loc_v, stage_v, rec_v, 1, lv)
-    for u in gs[4:]:
-        u.start_z()
-    for u in gs[:4]:
-        u.start_second()
-    for u in gs[:4]:
-        u.start_core()
-
-    def spread(moves, rec, zst, out, i):
-        for d in moves:
-            d.wait()
-
-        @pl.loop(0, nq)
-        def _(q):
-            for j in range(ksel):
-                zst[q, j] = rec[sel[q * ksel + j] // cap, sel[q * ksel + j] % cap]
-
-        res = []
-        for k in range(1, g.nz):
-            to = (t + k) % g.nz
-            d = send(zst.at[to], out.at[t], zss.at[i, k], zrs.at[i, k], me, to)
-            d.start()
-            res.append(d)
-        own = pltpu.make_async_copy(zst.at[t], out.at[t], zss.at[i, 0])
-        own.start()
-        return res + [own]
-
-    zk = spread(ek, rec_k, zst_k, mk, 0)
-    for u in gs[4:]:
-        u.start_first()
-    zv = spread(ev, rec_v, zst_v, mv, 1)
-    for u in gs[4:]:
-        u.start_second()
-    for u in gs[4:]:
-        u.start_core()
-    for d in zk + zv + gn:
-        d.wait()
-    for u in gs:
-        u.finish()
-    for k, d in enumerate(xs):
-
-        @pl.when(t + k + 1 < g.nz)
-        def _():
-            d.wait_send()
-
-        @pl.when(t >= k + 1)
-        def _():
-            d.wait_recv()
-
-
-def k1(g, cap, halo, requests, sel, x, gains, mem_k, mem_v, shards, nq, ksel):
-    bf = jnp.bfloat16
-    blk = mem_k.shape[1:]
-    units = []
-    for w, s in enumerate(shards):
-        r = s.shape[0]
-        kind = w % 7
-        if w in (0, 4):
-            units.append((w, (0, r), True))
-        elif w in (1, 5):
-            units.append((w, (0, r), False))
-        else:
-            units.append((w, (0, r // 2), True))
-            units.append((w, (r // 2, r - r // 2), False))
-    n_w = len(shards)
-    any_ = pl.BlockSpec(memory_space=pl.ANY)
-    nsem = len(units) * gather_sems(g)
-    dma = lambda *n: pltpu.SemaphoreType.DMA(n)
-    out_shape = (
-        [jax.ShapeDtypeStruct((g.dp, g.nz) + s.shape, bf) for s in shards]
-        + [jax.ShapeDtypeStruct((halo,) + x.shape, bf), jax.ShapeDtypeStruct((g.dp,) + gains.shape, gains.dtype)]
-        + [jax.ShapeDtypeStruct((g.nz, ksel) + blk, bf)] * 2
-    )
-    scratch = (
-        [pltpu.VMEM(mem_k.shape, bf)] * 2
-        + [pltpu.VMEM((g.dp, cap) + blk, bf)] * 4
-        + [pltpu.VMEM((nq, ksel) + blk, bf)] * 2
-        + [pltpu.VMEM((g.dp, 8, 128), jnp.int32), pltpu.SMEM((g.dp, 8, 128), jnp.int32)]
-        + [dma(nsem), dma(nsem), dma(2), dma(2, g.dp), dma(2, g.dp), dma(2, g.nz), dma(2, g.nz)]
-        + [dma(halo), dma(halo), dma(g.dp), dma(g.dp), dma(g.dp), dma(g.dp)]
-    )
-    return pl.pallas_call(
-        functools.partial(k1_kernel, g, cap, nq, ksel, halo, units, n_w),
-        out_shape=out_shape,
-        in_specs=[pl.BlockSpec(memory_space=pltpu.VMEM), pl.BlockSpec(memory_space=pltpu.SMEM)] + [any_] * (4 + n_w),
-        out_specs=[any_] * len(out_shape),
-        scratch_shapes=scratch,
-        compiler_params=pltpu.CompilerParams(collective_id=0, has_side_effects=True, vmem_limit_bytes=60 * 2**20),
-        name="fwd_exchange",
-    )(requests, sel, x, gains, mem_k, mem_v, *shards)
 
 
 def plan_requests(retrieved, partner, dp_size, blocks_dev, cap):
@@ -789,6 +623,311 @@
         compiler_params=pltpu.CompilerParams(vmem_limit_bytes=VL, dimension_semantics=("arbitrary",)),
         name="input_grad",
     )(x, gains, dn1, more, dh)
+
+
+def fwd_kernel(g, cap, nq, ksel, halo, window, units, n_w, *refs):
+    refs = list(refs)
+    take = lambda n: [refs.pop(0) for _ in range(n)]
+    requests, sel, seg_q, seg_k = take(4)
+    x, gains, mem_k, mem_v, cos, sin = take(6)
+    shards = take(n_w)
+    bufs = take(n_w)
+    xh, gains_all, mk, mv = take(4)
+    n1_o, q_o, k_o, v_o, o_o, l_o, h_o, n2_o = take(8)
+    loc, stage_k, stage_v, rec_k, rec_v = take(5)
+    req_in, req_s = take(2)
+    x_v, xh_v, n_v, n2_v, h_v, cos_v, sin_v, gn_v, wqkv = take(9)
+    ss, rs, msl, mss, mrs, zss, zrs, xss, xrs, qss, qrs, gss, grs, cs = take(14)
+    a, b, c, t, me = coords(g)
+    r, d = x_v.shape
+    greet(g, me, t)
+    rq, gn = [], []
+    for k in range(1, g.dp):
+        to = (me + k) % g.dp
+        m = send(requests.at[to], req_in.at[me], qss.at[k], qrs.at[k], to, t)
+        m.start()
+        rq.append(m)
+    for k in range(1, g.dp):
+        to = (me + k) % g.dp
+        m = send(gains, gains_all.at[me], gss.at[k], grs.at[k], to, t)
+        m.start()
+        gn.append(m)
+    own_r = pltpu.make_async_copy(requests.at[me], req_in.at[me], qss.at[0])
+    own_r.start()
+    own_g = pltpu.make_async_copy(gains, gains_all.at[me], gss.at[0])
+    own_g.start()
+    load_k = pltpu.make_async_copy(mem_k, loc, msl.at[0])
+    load_v = pltpu.make_async_copy(mem_v, loc, msl.at[1])
+    load_k.start()
+    per = gather_sems(g)
+    gs = [Gather(g, shards[w], bufs[w], rows_, bf, (ss, rs), i * per) for i, (w, rows_, bf) in enumerate(units)]
+    proj, out_, gate_up, down = gs[:4], gs[4:6], gs[6:8], gs[8:]
+    for u in proj + out_:
+        u.start_z()
+    xs = []
+    for k in range(1, halo + 1):
+        m = send(x, xh.at[k - 1], xss.at[k - 1], xrs.at[k - 1], me, (t + k) % g.nz)
+        xs.append(m)
+
+        @pl.when(t + k < g.nz)
+        def _():
+            m.start()
+
+    lx = [
+        pltpu.make_async_copy(x, x_v, cs.at[0]),
+        pltpu.make_async_copy(cos, cos_v, cs.at[1]),
+        pltpu.make_async_copy(sin, sin_v, cs.at[2]),
+    ]
+    for m in lx:
+        m.start()
+    own_r.wait()
+    own_g.wait()
+    for m in rq:
+        m.wait()
+    cp = pltpu.make_async_copy(req_in, req_s, qrs.at[0])
+    cp.start()
+    cp.wait()
+
+    def exchange(stage, rec, i, load):
+        load.wait()
+
+        @pl.loop(0, g.dp)
+        def _(s):
+            for k in range(cap):
+                stage[s, k] = loc[req_s[s, 0, k]]
+
+        out = []
+        for k in range(1, g.dp):
+            to = (me + k) % g.dp
+            m = send(stage.at[to], rec.at[me], mss.at[i, k], mrs.at[i, k], to, t)
+            m.start()
+            out.append(m)
+        own = pltpu.make_async_copy(stage.at[me], rec.at[me], mss.at[i, 0])
+        own.start()
+        return out + [own]
+
+    ek = exchange(stage_k, rec_k, 0, load_k)
+    load_v.start()
+    for u in proj + out_:
+        u.start_first()
+    for u in gate_up + down:
+        u.start_z()
+    ev = exchange(stage_v, rec_v, 1, load_v)
+    for u in proj + out_:
+        u.start_second()
+
+    def spread(moves, rec, zst, out, i):
+        for m in moves:
+            m.wait()
+
+        @pl.loop(0, nq)
+        def _(q):
+            for j in range(ksel):
+                zst[q, j] = rec[sel[q * ksel + j] // cap, sel[q * ksel + j] % cap]
+
+        res = []
+        for k in range(1, g.nz):
+            to = (t + k) % g.nz
+            m = send(zst.at[to], out.at[t], zss.at[i, k], zrs.at[i, k], me, to)
+            m.start()
+            res.append(m)
+        own = pltpu.make_async_copy(zst.at[t], out.at[t], zss.at[i, 0])
+        own.start()
+        return res + [own]
+
+    zk = spread(ek, rec_k, stage_k, mk, 0)
+    for u in gate_up + down:
+        u.start_first()
+    for m in gn:
+        m.wait()
+    cg = pltpu.make_async_copy(gains_all, gn_v, cs.at[3])
+    cg.start()
+    cg.wait()
+    for m in lx:
+        m.wait()
+    gain1, gain2 = gain_row(gn_v, 0), gain_row(gn_v, 1)
+    v = x_v[...].astype(F32)
+    n_v[halo * r :, :] = (v * inv_rms(v) * gain1).astype(BF16)
+    for k, m in enumerate(xs):
+
+        @pl.when(t >= k + 1)
+        def _():
+            m.wait_recv()
+
+        lo = (halo - 1 - k) * r
+
+        @pl.when(t >= k + 1)
+        def _():
+            ch = pltpu.make_async_copy(xh.at[k], xh_v, cs.at[4])
+            ch.start()
+            ch.wait()
+            v = xh_v[...].astype(F32)
+            n_v[lo : lo + r, :] = (v * inv_rms(v) * gain1).astype(BF16)
+
+        @pl.when(t < k + 1)
+        def _():
+            n_v[lo : lo + r, :] = jnp.zeros((r, d), BF16)
+
+    cn = pltpu.make_async_copy(n_v, n1_o, cs.at[5])
+    cn.start()
+    for u in proj + out_:
+        u.start_core()
+    zv = spread(ev, rec_v, stage_v, mv, 1)
+    for u in proj:
+        u.finish()
+
+    dp, nz, kd, cols = bufs[0].shape
+    rt = (halo + 1) * r
+    tile = 512
+    wq, wk, wv, wo = bufs[:4]
+
+    def project(wq_ref, wk_ref, wv_ref, q_ref, k_ref, v_ref):
+        for e in range(dp):
+            wqkv[e * kd : (e + 1) * kd, 0:cols] = wq_ref[e, 0]
+            wqkv[e * kd : (e + 1) * kd, cols : 2 * cols] = wk_ref[e, 0]
+            wqkv[e * kd : (e + 1) * kd, 2 * cols :] = wv_ref[e, 0]
+
+        def turned(y, cs_, sn_):
+            return jnp.concatenate(
+                [turn(y[:, h * HD : (h + 1) * HD], cs_, sn_).astype(BF16) for h in range(cols // HD)], axis=1
+            )
+
+        @pl.loop(0, rt // tile)
+        def _(i):
+            at = pl.ds(pl.multiple_of(i * tile, tile), tile)
+            n = n_v[at, :]
+            cs_, sn_ = cos_v[at, :], sin_v[at, :]
+            k_ref[at, :] = turned(dot_nn(n, wqkv[:, cols : 2 * cols]), cs_, sn_)
+            v_ref[at, :] = dot_nn(n, wqkv[:, 2 * cols :]).astype(BF16)
+
+            @pl.when(i >= halo * r // tile)
+            def _():
+                to = pl.ds(pl.multiple_of(i * tile - halo * r, tile), tile)
+                q_ref[to, :] = turned(dot_nn(n, wqkv[:, 0:cols]), cs_, sn_)
+
+    wspec = pl.BlockSpec((dp, 1, kd, cols), lambda u: (0, u, 0, 0))
+    col = lambda n: pl.BlockSpec((n, cols), lambda u: (0, u))
+    pltpu.emit_pipeline(project, grid=(nz,), in_specs=[wspec] * 3, out_specs=[col(r), col(rt), col(rt)])(
+        wq, wk, wv, q_o, k_o, v_o
+    )
+    for u in gate_up:
+        u.start_second()
+    for m in zk + zv:
+        m.wait()
+
+    blk = mk.shape[2]
+    nm, per_t = ksel * blk, cols // HD
+
+    def attend(q_ref, k_ref, v_ref, mk_ref, mv_ref, o_ref, l_ref):
+        km = mk_ref[0].reshape(nm, HD)
+        vm = mv_ref[0].reshape(nm, HD)
+        for i in range(r // QT):
+            at = slice(i * QT, (i + 1) * QT)
+            k0 = halo * r - window + i * QT
+            ks = slice(k0, k0 + window + QT)
+            qq = q_ref[at, :]
+            ok = allowed_of(seg_q[at, :], seg_k[:, ks], halo * r + i * QT, k0)
+            sl = jnp.where(ok, dot_nt(qq, k_ref[ks, :]), MASKED)
+            sm = dot_nt(qq, km)
+            mx = jnp.maximum(jnp.max(sl, axis=1, keepdims=True), jnp.max(sm, axis=1, keepdims=True))
+            mc = mx * C2
+            el = jnp.exp2(sl * C2 - mc)
+            em = jnp.exp2(sm * C2 - mc)
+            tot = jnp.sum(el, axis=1, keepdims=True) + jnp.sum(em, axis=1, keepdims=True)
+            acc = dot_nn(el.astype(BF16), v_ref[ks, :]) + dot_nn(em.astype(BF16), vm)
+            o_ref[at, :] = (acc / tot).astype(BF16)
+            l_ref[0, at, :] = mc + jnp.log2(tot)
+
+    head = lambda n: pl.BlockSpec((n, HD), lambda h: (0, h))
+    mem = pl.BlockSpec((1, ksel, blk, HD), lambda h: (h // per_t, 0, 0, h % per_t))
+    pltpu.emit_pipeline(
+        attend,
+        grid=(d // HD,),
+        in_specs=[head(r), head(rt), head(rt), mem, mem],
+        out_specs=[head(r), pl.BlockSpec((1, r, 1), lambda h: (h, 0, 0))],
+    )(q_o, k_o, v_o, mk, mv, o_o, l_o)
+    for u in down:
+        u.start_second()
+    for u in gate_up:
+        u.start_core()
+    for u in out_:
+        u.finish()
+
+    h_v[...] = x_v[...].astype(F32)
+    kk = wo.shape[2]
+
+    def out_proj(o_ref, w_ref):
+        h_v[...] += dot_nn(o_ref[...], jnp.concatenate([w_ref[e, 0] for e in range(dp)], axis=1))
+
+    pltpu.emit_pipeline(
+        out_proj,
+        grid=(nz,),
+        in_specs=[pl.BlockSpec((r, kk), lambda u: (0, u)), pl.BlockSpec((dp, 1, kk, wo.shape[3]), lambda u: (0, u, 0, 0))],
+    )(o_o, wo)
+    h = h_v[...]
+    n2_v[...] = (h * inv_rms(h) * gain2).astype(BF16)
+    ch = pltpu.make_async_copy(h_v, h_o, cs.at[6])
+    ch.start()
+    c2 = pltpu.make_async_copy(n2_v, n2_o, cs.at[7])
+    c2.start()
+    for u in down:
+        u.start_core()
+    for u in gate_up + down:
+        u.finish()
+    for m in (cn, ch, c2):
+        m.wait()
+    for k, m in enumerate(xs):
+
+        @pl.when(t + k + 1 < g.nz)
+        def _():
+            m.wait_send()
+
+
+def fwd(g, cap, halo, window, requests, sel, seg_q, seg_k, x, gains, mem_k, mem_v, cos, sin, shards, nq, ksel):
+    blk = mem_k.shape[1:]
+    r, d = x.shape
+    rt = (halo + 1) * r
+    units = []
+    for w, s in enumerate(shards):
+        n = s.shape[0]
+        if w in (0, 4):
+            units.append((w, (0, n), True))
+        elif w in (1, 5):
+            units.append((w, (0, n), False))
+        else:
+            units.append((w, (0, n // 2), True))
+            units.append((w, (n // 2, n - n // 2), False))
+    n_w = len(shards)
+    any_ = pl.BlockSpec(memory_space=pl.ANY)
+    vm = pl.BlockSpec(memory_space=pltpu.VMEM)
+    nsem = len(units) * gather_sems(g)
+    dma = lambda *n: pltpu.SemaphoreType.DMA(n)
+    st = lambda s, dt=BF16: jax.ShapeDtypeStruct(s, dt)
+    out_shape = (
+        [st((g.dp, g.nz) + s.shape) for s in shards]
+        + [st((halo,) + x.shape), st((g.dp,) + gains.shape, F32)]
+        + [st((g.nz, ksel) + blk)] * 2
+        + [st((rt, d)), st((r, d)), st((rt, d)), st((rt, d)), st((r, d)), st((d // HD, r, 1), F32), st((r, d), F32), st((r, d))]
+    )
+    scratch = (
+        [pltpu.VMEM(mem_k.shape, BF16)]
+        + [pltpu.VMEM((g.dp, cap) + blk, BF16)] * 4
+        + [pltpu.VMEM((g.dp, 8, 128), jnp.int32), pltpu.SMEM((g.dp, 8, 128), jnp.int32)]
+        + [pltpu.VMEM((r, d), BF16), pltpu.VMEM((r, d), BF16), pltpu.VMEM((rt, d), BF16), pltpu.VMEM((r, d), BF16)]
+        + [pltpu.VMEM((r, d), F32), pltpu.VMEM((rt, HD), F32), pltpu.VMEM((rt, HD), F32)]
+        + [pltpu.VMEM((g.dp,) + gains.shape, F32), pltpu.VMEM((d, 3 * shards[0].shape[1]), BF16)]
+        + [dma(nsem), dma(nsem), dma(2), dma(2, g.dp), dma(2, g.dp), dma(2, g.nz), dma(2, g.nz)]
+        + [dma(halo), dma(halo), dma(g.dp), dma(g.dp), dma(g.dp), dma(g.dp), dma(8)]
+    )
+    return pl.pallas_call(
+        functools.partial(fwd_kernel, g, cap, nq, ksel, halo, window, units, n_w),
+        out_shape=out_shape,
+        in_specs=[vm, pl.BlockSpec(memory_space=pltpu.SMEM), vm, vm] + [any_] * (6 + n_w),
+        out_specs=[any_] * len(out_shape),
+        scratch_shapes=scratch,
+        compiler_params=pltpu.CompilerParams(collective_id=0, has_side_effects=True, vmem_limit_bytes=63 * 2**20),
+        name="forward",
+    )(requests, sel, seg_q, seg_k, x, gains, mem_k, mem_v, cos, sin, *shards)
 
 
 class Scatter:
@@ -1364,17 +1503,14 @@
     gains = jnp.stack([gain_attn, gain_ffn]).astype(F32)
     flat = lambda m: m.reshape((-1,) + m.shape[2:])
     shards = [w_query, w_key, w_value, w_out, w_gate.T, w_up.T, w_down]
-    wq, wk, wv, wo, wg, wu, wd, xh, gn, mk, mv = k1(
-        g, cap, halo, req, sel, x, gains, flat(memory_keys), flat(memory_values), shards, nq, ksel
-    )
     cos, sin = cover(halo, r, t)
     padded = jnp.concatenate([jnp.full((halo * r,), -1, jnp.int32), segments[0]])
     seg = lax.dynamic_slice(padded, (t * r,), ((halo + 1) * r,))
     seg_k, seg_q = seg[None, :], seg[halo * r :, None]
-
-    n1, q, k, v = project(halo, None, x, xh, gn, cos, sin, wq, wk, wv)
-    o, lse = attend(halo, window, q, k, v, mk, mv, seg_q, seg_k)
-    h, n2 = out_norm(x, o, wo, gn)
+    (wq, wk, wv, wo, wg, wu, wd, xh, gn, mk, mv, n1, q, k, v, o, lse, h, n2) = fwd(
+        g, cap, halo, window, req, sel, seg_q, seg_k, x, gains, flat(memory_keys), flat(memory_values), cos, sin,
+        shards, nq, ksel,
+    )
     hid, dg, du, block_out, dh, dhb, do, gg_ffn = feed(h, n2, c, gn, wg, wu, wd, wo)
     do = jnp.transpose(do, (1, 0, 2)).reshape(r, d)
     dq, dk, dv = attend_back(halo, window, q, k, v, mk, mv, seg_q, seg_k, o, lse, do, cos, sin)

time: 624 us -> 589 us (0.944)
  Pallas kernels: 521 us -> 485 us
    pallas_call x4 -> x1, Pallas kernels: 256 us -> 213 us  [fwd(): pl.pallas_call(functools.partial(fwd_kernel, g, cap, nq, ksel, halo, wind...]
    pallas_call x1, Pallas kernels: 147 us -> 156 us  [k2(): pl.pallas_call(functools.partial(k2_kernel, g, halo, units, n_w), out_sha...]
    unnamed x53 -> x49, local copies, waits for them, and re-layouts: 12.7 us -> 11.9 us
  transfers between devices with their start and end apart: 11 -> 11, of which waited for: 0 -> 0; matrix products, arithmetic and copies ran while one was open for 12% -> 13% of each run, Pallas kernels for 5% -> 5%
where the time goes in v2:
time: 589 us; the launch traced here: 584 us
  Pallas kernels  485 us (82%)
  local copies, waits for them, and re-layouts  87.1 us (15%)
  other arithmetic  6.7 us (1%)
    pallas_call x1, Pallas kernels, fwd(): pl.pallas_call(functools.partial(fwd_kernel, g, cap, nq, ksel, halo, wind...  213 us
    pallas_call x1, Pallas kernels, k2(): pl.pallas_call(functools.partial(k2_kernel, g, halo, units, n_w), out_sha...  156 us
    pallas_call x1, Pallas kernels, feed(): pl.pallas_call(kern, grid=(nz,), in_specs=[one((r, d)), one((r, d)), one(...  47.8 us
    dynamic_slice x4, local copies, waits for them, and re-layouts, cut(): lax.dynamic_index_in_dim(z, 1 - core, 2, False).reshape(y.shape[0], d // 2)  36.5 us
    pallas_call x1, Pallas kernels, attend_back(): pl.pallas_call(kern, grid=(d // HD,), in_specs=[head(r), head(rt), head(r...  21.1 us
    pallas_call x1, Pallas kernels, project_back(): pl.pallas_call(kern, grid=(nz,), in_specs=[full((r, d)), full((halo, r, d...  16.3 us
    pallas_call x1, Pallas kernels, feed_grads(): pl.pallas_call(kern, grid=(nz,), in_specs=[piece] * 6 + [full((r, half))]...  15.4 us
    ppermute x3, local copies, waits for them, and re-layouts, on_device_rows(): other = lambda y: lax.ppermute(y, 'dp', pairs)  13.9 us
  transfers between devices with their start and end apart: 11, of which 0 were waited for; matrix products, arithmetic and copies ran while one was open for 13% of the time, Pallas kernels for 5%

profile of v2, /device:TPU:0, one launch (start us, length us, event | category | flops | bytes accessed | tf_op | source)
XLA Modules:
  0.0 583.9 jit_solution(954403883639377999)
XLA Ops:
  4.5 1.9 fusion
  7.7 1.3 pad_maximum_fusion
  9.8 212.6 %forward.1 = (bf16[8,4,128,256]{3,2,1,0:T(8,128)(2,1)}, bf16[8,4,128,256]{3,2,1,0:T(8,128)(2,1)}, bf16[8,4,128,256]{3,2,1,0:T(8,128)(2,1)}, bf16[8,4,256,128]{3,...) custom-call(s32[8,8,128]{2,1,0:T(8,128)} %broadcast_in_dim.54.refs_0, ...), custom_call_target="tpu_custom_call" | custom-call | tf_op jit(solution)/shard_map/forward/pallas_call | solution.py:922
  222.3 47.8 %feed.1 = (bf16[4,512,704]{2,1,0:T(8,128)(2,1)}, bf16[4,512,704]{2,1,0:T(8,128)(2,1)}, bf16[4,512,704]{2,1,0:T(8,128)(2,1)}, f32[512,1024]{1,0:T(8,128)}, f32[51...) custom-call(f32[512,1024]{1,0:T(8,128)} %get-tuple-element.60.h_ref, ...), custom_call_target="tpu_custom_call" | custom-call | tf_op jit(solution)/shard_map/feed/pallas_call | solution.py:466
  270.1 2.3 copy.89
  272.5 21.1 %attend_back.1 = (bf16[512,1024]{1,0:T(8,128)(2,1)}, bf16[1024,1024]{1,0:T(8,128)(2,1)}, bf16[1024,1024]{1,0:T(8,128)(2,1)}) custom-call(bf16[512,1024]{1,0:T(8,128)(2,1)} %get-tuple-element.69.q_ref, bf16[1024,1024]{1,0:T(8,128)(2,1)} %get-tuple-element.70.k_ref, bf16[1024,1024]{1,0:T(8,128)(2,1)} %get-tuple-element.71.v_ref, ...), custom_call_target="tpu_custom_call" | custom-call | tf_op jit(solution)/shard_map/attend_back/pallas_call | solution.py:359
  294.0 3.6 reshape.299
  297.7 14.2 %dynamic-slice_reduce_fusion = (bf16[1024,4,128]{2,1,0:T(4,128)(2,1)S(1)}, bf16[1024,4,128]{2,1,0:T(4,128)(2,1)}) fusion(bf16[1024,4,2,128]{3,2,1,0:T(2,128)(2,1)S(1)} %reshape.299, s32[]{:T(128)S(6)} %select_n.98, s32[]{:T(128)S(6)} %select_n.97), kind=kLoop, calls=%fused_computation | loop fusion | bytes 4194312 | tf_op jit(solution)/shard_map/jit(dynamic_index_in_dim)/dynamic_slice | solution.py:1526
  313.5 1.5 reshape.296
  315.1 9.1 %dynamic-slice_reduce_fusion.2 = (bf16[512,4,128]{2,1,0:T(4,128)(2,1)S(1)}, bf16[512,4,128]{2,1,0:T(4,128)(2,1)}) fusion(bf16[512,4,2,128]{3,2,1,0:T(2,128)(2,1)} %reshape.296, s32[]{:T(128)S(6)} %select_n.98, s32[]{:T(128)S(6)} %select_n.97), kind=kLoop, calls=%fused_computation.4 | loop fusion | bytes 2097160 | tf_op jit(solution)/shard_map/jit(dynamic_index_in_dim)/dynamic_slice | solution.py:1526
  325.1 2.7 copy.67
  328.2 4.7 copy.68
  333.0 2.8 copy.69
  336.8 1.8 reshape.291
  339.6 6.5 %dynamic-slice_reduce_fusion.6 = (bf16[512,4,128]{2,1,0:T(4,128)(2,1)S(1)}, bf16[512,4,128]{2,1,0:T(4,128)(2,1)S(1)}) fusion(bf16[512,4,2,128]{3,2,1,0:T(2,128)(2,1)S(1)} %reshape.291, s32[]{:T(128)S(6)} %select_n.98, s32[]{:T(128)S(6)} %select_n.97), kind=kLoop, calls=%fused_computation.8 | loop fusion | bytes 2097160 | tf_op jit(solution)/shard_map/jit(dynamic_index_in_dim)/dynamic_slice | solution.py:1526
  346.2 6.8 %dynamic-slice_reduce_fusion.4 = (bf16[512,4,128]{2,1,0:T(4,128)(2,1)S(1)}, bf16[512,4,128]{2,1,0:T(4,128)(2,1)S(1)}) fusion(bf16[512,4,2,128]{3,2,1,0:T(2,128)(2,1)S(1)} %reshape_squeeze.7, s32[]{:T(128)S(6)} %select_n.98, s32[]{:T(128)S(6)} %select_n.97), kind=kLoop, calls=%fused_computation.6 | loop fusion | bytes 2097160 | tf_op jit(solution)/shard_map/jit(dynamic_index_in_dim)/dynamic_slice | solution.py:1526
  357.5 16.3 %project_back.1 = (f32[512,1024]{1,0:T(8,128)}, bf16[512,1024]{1,0:T(8,128)(2,1)}, f32[1,1024]{1,0:T(1,128)}) custom-call(bf16[512,1024]{1,0:T(8,128)(2,1)} %bitcast.57, bf16[1,512,1024]{2,1,0:T(8,128)(2,1)} %get-tuple-element.68.xh_ref, bf16[512,1024]{1,0:T(8,128)(2,1)} %get-tuple-element.77.dq_ref.q0, bf16[1024,1024]{1,0:T(8,128)(2,1)} %get-tuple-element.78.dk_ref.k0, ...), custom_call_target="tpu_custom_call" | custom-call | tf_op jit(solution)/shard_map/project_back/pallas_call | solution.py:524
  375.1 12.1 %attn_grads.1 = (bf16[4,4,256,128]{3,2,1,0:T(8,128)(2,1)}, bf16[4,4,128,256]{3,2,1,0:T(8,128)(2,1)}, bf16[4,4,128,256]{3,2,1,0:T(8,128)(2,1)}, bf16[4,4,128,256]{3,2,1,0:T(8,128)(2,1)}) custom-call(bf16[512,1024]{1,0:T(8,128)(2,1)} %get-tuple-element.74.o_ref.o0, bf16[512,1024]{1,0:T(8,128)(2,1)} %collective-permute-done.5.o1, bf16[512,512]{1,0:T(8,128)(2,1)} %bitcast.69, ...), custom_call_target="tpu_custom_call" | custom-call | tf_op jit(solution)/shard_map/attn_grads/pallas_call | solution.py:588
  387.2 4.6 copy.74.h1
  391.8 4.6 copy.75.g1
  396.4 4.7 copy.76.u1
  402.1 15.4 %feed_grads.1 = (bf16[4,4,704,128]{3,2,1,0:T(8,128)(2,1)}, bf16[4,4,704,128]{3,2,1,0:T(8,128)(2,1)}, bf16[4,4,704,128]{3,2,1,0:T(8,128)(2,1)}) custom-call(bf16[4,512,704]{2,1,0:T(8,128)(2,1)} %get-tuple-element.87.h0, bf16[4,512,704]{2,1,0:T(8,128)(2,1)} %copy.74.h1, bf16[4,512,704]{2,1,0:T(8,128)(2,1)} %get-tuple-element.88.g0, ...), custom_call_target="tpu_custom_call" | custom-call | tf_op jit(solution)/shard_map/feed_grads/pallas_call | solution.py:554
  417.5 155.7 %bwd_exchange.1 = (f32[2,128]{1,0:T(2,128)}, bf16[1,512,1024]{2,1,0:T(8,128)(2,1)}, f32[704,128]{1,0:T(8,128)}, f32[704,128]{1,0:T(8,128)}, f32[704,128]{1,0:T(8...) custom-call(f32[2,1024]{1,0:T(2,128)} %pad_maximum_fusion.2.refs_0_, ...), custom_call_target="tpu_custom_call" | custom-call | tf_op jit(solution)/shard_map/bwd_exchange/pallas_call | solution.py:1153
  574.4 4.4 input_grad.1
  (88 shorter events, 23.7 us)
Async XLA Ops:
  3.7 5.4 copy-start.15
  293.6 42.4 %collective-permute-start.8 = (bf16[512,1024]{1,0:T(8,128)(2,1)}, bf16[512,1024]{1,0:T(8,128)(2,1)}, u32[]{:S(2)}, u32[]{:S(2)}) collective-permute-start(bf16[512,1024]{1,0:T(8,128)(2,1)} %get-tuple-element.77.dq_ref.q0), channel_id=1, source_target_pairs={{0,4},{4,0},{8,12},{12,8},{16,20},{20,16},{24,28},{28,24},{1,5},{5... | collective-permute-start | bytes 3145736 | tf_op jit(solution)/shard_map/ppermute | solution.py:1521
  313.0 23.3 %collective-permute-start.7 = (bf16[1024,512]{1,0:T(8,128)(2,1)}, bf16[1024,512]{1,0:T(8,128)(2,1)}, u32[]{:S(2)}, u32[]{:S(2)}) collective-permute-start(bf16[1024,512]{1,0:T(8,128)(2,1)} %bitcast.47), channel_id=1, source_target_pairs={{0,4},{4,0},{8,12},{12,8},{16,20},{20,16},{24,28},{28,24},{1,5},{5... | collective-permute-start | bytes 3145736 | tf_op jit(solution)/shard_map/ppermute | solution.py:1521
  313.1 23.3 %collective-permute-start.5 = (bf16[512,1024]{1,0:T(8,128)(2,1)}, bf16[512,1024]{1,0:T(8,128)(2,1)}, u32[]{:S(2)}, u32[]{:S(2)}) collective-permute-start(bf16[512,1024]{1,0:T(8,128)(2,1)} %get-tuple-element.74.o_ref.o0), channel_id=1, source_target_pairs={{0,4},{4,0},{8,12},{12,8},{16,20},{20,16},{24,28},{28,24},{1,5},{5... | collective-permute-start | bytes 3145736 | tf_op jit(solution)/shard_map/ppermute | solution.py:1521
  315.1 10.1 %copy-start = (bf16[4,512,704]{2,1,0:T(8,128)(2,1)S(1)}, bf16[4,512,704]{2,1,0:T(8,128)(2,1)}, u32[]{:S(2)}) copy-start(bf16[4,512,704]{2,1,0:T(8,128)(2,1)} %get-tuple-element.87.h0) | copy-start | bytes 8650756
  325.0 10.8 %collective-permute-start.6 = (bf16[512,512]{1,0:T(8,128)(2,1)}, bf16[512,512]{1,0:T(8,128)(2,1)}, u32[]{:S(2)}, u32[]{:S(2)}) collective-permute-start(bf16[512,512]{1,0:T(8,128)(2,1)} %bitcast.49), channel_id=1, source_target_pairs={{0,4},{4,0},{8,12},{12,8},{16,20},{20,16},{24,28},{28,24},{1,5},{5... | collective-permute-start | bytes 1572872 | tf_op jit(solution)/shard_map/ppermute | solution.py:1521
  327.9 59.3 %collective-permute-start = (bf16[4,512,704]{1,2,0:T(8,128)(2,1)}, bf16[4,512,704]{1,2,0:T(8,128)(2,1)}, u32[]{:S(2)}, u32[]{:S(2)}) collective-permute-start(bf16[4,512,704]{1,2,0:T(8,128)(2,1)} %copy.67), channel_id=1, source_target_pairs={{0,4},{4,0},{8,12},{12,8},{16,20},{20,16},{24,28},{28,24},{1,5},{5... | collective-permute-start | bytes 8650760 | tf_op jit(solution)/shard_map/ppermute | solution.py:1521
  328.2 4.8 copy-start.1
  335.8 56.0 %collective-permute-start.1 = (bf16[4,512,704]{1,2,0:T(8,128)(2,1)}, bf16[4,512,704]{1,2,0:T(8,128)(2,1)}, u32[]{:S(2)}, u32[]{:S(2)}) collective-permute-start(bf16[4,512,704]{1,2,0:T(8,128)(2,1)} %copy.68), channel_id=1, source_target_pairs={{0,4},{4,0},{8,12},{12,8},{16,20},{20,16},{24,28},{28,24},{1,5},{5... | collective-permute-start | bytes 8650760 | tf_op jit(solution)/shard_map/ppermute | solution.py:1521
  335.9 60.5 %collective-permute-start.2 = (bf16[4,512,704]{1,2,0:T(8,128)(2,1)}, bf16[4,512,704]{1,2,0:T(8,128)(2,1)}, u32[]{:S(2)}, u32[]{:S(2)}) collective-permute-start(bf16[4,512,704]{1,2,0:T(8,128)(2,1)} %copy.69), channel_id=1, source_target_pairs={{0,4},{4,0},{8,12},{12,8},{16,20},{20,16},{24,28},{28,24},{1,5},{5... | collective-permute-start | bytes 8650760 | tf_op jit(solution)/shard_map/ppermute | solution.py:1521
  336.3 16.8 %collective-permute-start.10 = (bf16[1024,1024]{1,0:T(8,128)(2,1)}, bf16[1024,1024]{1,0:T(8,128)(2,1)}, u32[]{:S(2)}, u32[]{:S(2)}) collective-permute-start(bf16[1024,1024]{1,0:T(8,128)(2,1)} %get-tuple-element.79.dv_ref.v0), channel_id=1, source_target_pairs={{0,4},{4,0},{8,12},{12,8},{16,20},{20,16},{24,28},{28,24},{1,5},{5... | collective-permute-start | bytes 6291464 | tf_op jit(solution)/shard_map/ppermute | solution.py:1521
  336.4 16.9 %collective-permute-start.9 = (bf16[1024,1024]{1,0:T(8,128)(2,1)}, bf16[1024,1024]{1,0:T(8,128)(2,1)}, u32[]{:S(2)}, u32[]{:S(2)}) collective-permute-start(bf16[1024,1024]{1,0:T(8,128)(2,1)} %get-tuple-element.78.dk_ref.k0), channel_id=1, source_target_pairs={{0,4},{4,0},{8,12},{12,8},{16,20},{20,16},{24,28},{28,24},{1,5},{5... | collective-permute-start | bytes 6291464 | tf_op jit(solution)/shard_map/ppermute | solution.py:1521
  346.2 7.5 %copy-start.4 = (bf16[512,4,128]{2,1,0:T(4,128)(2,1)S(1)}, bf16[512,4,128]{2,1,0:T(4,128)(2,1)}, u32[]{:S(2)}) copy-start(bf16[512,4,128]{2,1,0:T(4,128)(2,1)} %get-tuple-element.112) | copy-start | bytes 1572868
  346.2 8.4 %copy-start.2 = (bf16[1024,4,128]{2,1,0:T(4,128)(2,1)S(1)}, bf16[1024,4,128]{2,1,0:T(4,128)(2,1)}, u32[]{:S(2)}) copy-start(bf16[1024,4,128]{2,1,0:T(4,128)(2,1)} %get-tuple-element.110) | copy-start | bytes 3145732
  353.1 48.0 %collective-permute-start.3 = (bf16[512,512]{1,0:T(8,128)(2,1)S(1)}, bf16[512,512]{1,0:T(8,128)(2,1)S(1)}, u32[]{:S(2)}, u32[]{:S(2)}) collective-permute-start(bf16[512,512]{1,0:T(8,128)(2,1)S(1)} %bitcast.77), channel_id=1, source_target_pairs={{0,4},{4,0},{8,12},{12,8},{16,20},{20,16},{24,28},{28,24},{1,5},{5... | collective-permute-start | bytes 1572872 | tf_op jit(solution)/shard_map/ppermute | solution.py:1521
  353.3 47.8 %collective-permute-start.4 = (bf16[512,512]{1,0:T(8,128)(2,1)S(1)}, bf16[512,512]{1,0:T(8,128)(2,1)S(1)}, u32[]{:S(2)}, u32[]{:S(2)}) collective-permute-start(bf16[512,512]{1,0:T(8,128)(2,1)S(1)} %bitcast.78), channel_id=1, source_target_pairs={{0,4},{4,0},{8,12},{12,8},{16,20},{20,16},{24,28},{28,24},{1,5},{5... | collective-permute-start | bytes 1572872 | tf_op jit(solution)/shard_map/ppermute | solution.py:1521
  357.5 16.3 %copy-start.16 = (f32[1,1024]{1,0:T(1,128)S(1)}, f32[1,1024]{1,0:T(1,128)}, u32[]{:S(2)}) copy-start(f32[1,1024]{1,0:T(1,128)} %get-tuple-element.85) | copy-start | bytes 12292
  574.4 4.4 copy-start.14
  574.4 5.1 copy-start.13
  574.4 5.7 copy-start.12
  574.4 6.4 %copy-start.11 = (f32[256,128]{1,0:T(8,128)S(1)}, f32[256,128]{1,0:T(8,128)}, u32[]{:S(2)}) copy-start(f32[256,128]{1,0:T(8,128)} %get-tuple-element.143) | copy-start | bytes 393220
  574.4 7.0 %copy-start.10 = (f32[704,128]{1,0:T(8,128)S(1)}, f32[704,128]{1,0:T(8,128)}, u32[]{:S(2)}) copy-start(f32[704,128]{1,0:T(8,128)} %get-tuple-element.106) | copy-start | bytes 1081348
  574.4 7.8 %copy-start.9 = (f32[704,128]{1,0:T(8,128)S(1)}, f32[704,128]{1,0:T(8,128)}, u32[]{:S(2)}) copy-start(f32[704,128]{1,0:T(8,128)} %get-tuple-element.107) | copy-start | bytes 1081348
  578.8 4.1 copy-start.8
  (4 other events, 6.3 us)

commit v3 on v2

--- a/solution.py
+++ b/solution.py
@@ -7,7 +7,6 @@
 from jax.experimental import pallas as pl
 from jax.experimental.pallas import tpu as pltpu
 from jax.sharding import PartitionSpec as P
-
 MESH = pl.DeviceIdType.MESH
 MEMB = 128
 
@@ -162,6 +161,7 @@
     req = jnp.sum(jnp.where(hit, flat[None, None, :], 0), axis=2)
     return jnp.broadcast_to(req[:, None, :], (dp_size, 8, 128)).astype(jnp.int32), (owner * cap + slot).astype(jnp.int32)
 
+
 HD = 128
 EPSILON = 1e-05
 MASKED = -1e30
@@ -208,65 +208,6 @@
     n = len(shape)
     kw = {} if buffers is None else dict(pipeline_mode=pl.Buffered(buffers))
     return pl.BlockSpec(shape, lambda *i: (0,) * n, **kw)
-
-
-def project(halo, first, x, xh, gains, cos, sin, wq, wk, wv):
-    r, d = x.shape
-    dp, nz, _, cols = wq.shape
-    rt = (halo + 1) * r
-
-    def kern(x_ref, xh_ref, gn_ref, cos_ref, sin_ref, wq_ref, wk_ref, wv_ref, n_ref, q_ref, k_ref, v_ref, w_s):
-        @pl.when(pl.program_id(0) == 0)
-        def _():
-            g = gain_row(gn_ref, 0)
-            t = lax.axis_index("tensor")
-            for j in range(halo):
-                v = xh_ref[j].astype(F32)
-                n = (v * inv_rms(v) * g).astype(BF16)
-                n_ref[pl.ds((halo - 1 - j) * r, r), :] = jnp.where(t >= j + 1, n, jnp.zeros_like(n))
-            v = x_ref[...].astype(F32)
-            n_ref[pl.ds(halo * r, r), :] = (v * inv_rms(v) * g).astype(BF16)
-
-        w_s[:, 0:cols] = rows(wq_ref)
-        w_s[:, cols : 2 * cols] = rows(wk_ref)
-        w_s[:, 2 * cols :] = rows(wv_ref)
-
-        tile = 256
-
-        @pl.loop(0, rt // tile)
-        def _(i):
-            at = pl.ds(pl.multiple_of(i * tile, tile), tile)
-            n = n_ref[at, :]
-            y = dot_nn(n, w_s[:, cols:])
-            cs, sn = cos_ref[at, :], sin_ref[at, :]
-            for h in range(cols // HD):
-                k_ref[at, h * HD : (h + 1) * HD] = turn(y[:, h * HD : (h + 1) * HD], cs, sn).astype(BF16)
-            v_ref[at, :] = y[:, cols:].astype(BF16)
-
-            @pl.when(i >= halo * r // tile)
-            def _():
-                z = dot_nn(n, w_s[:, 0:cols])
-                to = pl.ds(pl.multiple_of(i * tile - halo * r, tile), tile)
-                for h in range(cols // HD):
-                    q_ref[to, h * HD : (h + 1) * HD] = turn(z[:, h * HD : (h + 1) * HD], cs, sn).astype(BF16)
-
-    wspec = pl.BlockSpec((dp, 1, wq.shape[2], cols), lambda t: (0, t, 0, 0))
-    col = lambda n: pl.BlockSpec((n, cols), lambda t: (0, t))
-    return pl.pallas_call(
-        kern,
-        grid=(nz,),
-        in_specs=[full((r, d)), full((halo, r, d)), full(gains.shape), full((rt, HD)), full((rt, HD))] + [wspec] * 3,
-        out_specs=[full((rt, d)), col(r), col(rt), col(rt)],
-        out_shape=[
-            jax.ShapeDtypeStruct((rt, d), BF16),
-            jax.ShapeDtypeStruct((r, d), BF16),
-            jax.ShapeDtypeStruct((rt, d), BF16),
-            jax.ShapeDtypeStruct((rt, d), BF16),
-        ],
-        scratch_shapes=[pltpu.VMEM((d, 3 * cols), BF16)],
-        compiler_params=pltpu.CompilerParams(vmem_limit_bytes=VL, dimension_semantics=("arbitrary",)),
-        name="project",
-    )(x, xh, gains, cos, sin, wq, wk, wv)
 
 
 def allowed_of(seg_q, seg_k, q0, k0):
@@ -278,351 +219,6 @@
 
 QT = 256
 C2 = HD**-0.5 * math.log2(math.e)
-
-
-def attend(halo, window, q, k, v, mk, mv, seg_q, seg_k):
-    r, d = q.shape
-    rt = k.shape[0]
-    nz, ksel, blk, cols = mk.shape
-    per = cols // HD
-    nm = ksel * blk
-
-    def kern(q_ref, k_ref, v_ref, mk_ref, mv_ref, sq_ref, sk_ref, o_ref, l_ref):
-        km = mk_ref[0].reshape(nm, HD)
-        vm = mv_ref[0].reshape(nm, HD)
-        for i in range(r // QT):
-            at = slice(i * QT, (i + 1) * QT)
-            k0 = halo * r - window + i * QT
-            ks = slice(k0, k0 + window + QT)
-            qq = q_ref[at, :]
-            ok = allowed_of(sq_ref[at, :], sk_ref[:, ks], halo * r + i * QT, k0)
-            sl = jnp.where(ok, dot_nt(qq, k_ref[ks, :]), MASKED)
-            sm = dot_nt(qq, km)
-            m = jnp.maximum(jnp.max(sl, axis=1, keepdims=True), jnp.max(sm, axis=1, keepdims=True))
-            mc = m * C2
-            el = jnp.exp2(sl * C2 - mc)
-            em = jnp.exp2(sm * C2 - mc)
-            tot = jnp.sum(el, axis=1, keepdims=True) + jnp.sum(em, axis=1, keepdims=True)
-            acc = dot_nn(el.astype(BF16), v_ref[ks, :]) + dot_nn(em.astype(BF16), vm)
-            o_ref[at, :] = (acc / tot).astype(BF16)
-            l_ref[0, at, :] = mc + jnp.log2(tot)
-
-    head = lambda n: pl.BlockSpec((n, HD), lambda h: (0, h))
-    mem = pl.BlockSpec((1, ksel, blk, HD), lambda h: (h // per, 0, 0, h % per))
-    return pl.pallas_call(
-        kern,
-        grid=(d // HD,),
-        in_specs=[head(r), head(rt), head(rt), mem, mem, full((r, 1)), full((1, rt))],
-        out_specs=[head(r), pl.BlockSpec((1, r, 1), lambda h: (h, 0, 0))],
-        out_shape=[jax.ShapeDtypeStruct((r, d), BF16), jax.ShapeDtypeStruct((d // HD, r, 1), F32)],
-        compiler_params=pltpu.CompilerParams(vmem_limit_bytes=VL, dimension_semantics=("arbitrary",)),
-        name="attend",
-    )(q, k, v, mk, mv, seg_q, seg_k)
-
-
-def attend_back(halo, window, q, k, v, mk, mv, seg_q, seg_k, o, lse, do, cos, sin):
-    r, d = q.shape
-    rt = k.shape[0]
-    nz, ksel, blk, cols = mk.shape
-    per = cols // HD
-    nm = ksel * blk
-    scale = HD**-0.5
-
-    def kern(q_ref, k_ref, v_ref, mk_ref, mv_ref, sq_ref, sk_ref, o_ref, l_ref, do_ref, cos_ref, sin_ref,
-             dq_ref, dk_ref, dv_ref, sdk, sdv):
-        km = mk_ref[0].reshape(nm, HD)
-        vm = mv_ref[0].reshape(nm, HD)
-        sdk[...] = jnp.zeros_like(sdk)
-        sdv[...] = jnp.zeros_like(sdv)
-        for i in range(r // QT):
-            at = slice(i * QT, (i + 1) * QT)
-            k0 = halo * r - window + i * QT
-            ks = slice(k0, k0 + window + QT)
-            own = slice(halo * r + i * QT, halo * r + (i + 1) * QT)
-            qq, dd = q_ref[at, :], do_ref[at, :]
-            lse_c = l_ref[0, at, :]
-            delta = jnp.sum(dd.astype(F32) * o_ref[at, :].astype(F32), axis=1, keepdims=True)
-            ok = allowed_of(sq_ref[at, :], sk_ref[:, ks], halo * r + i * QT, k0)
-            pm = jnp.exp2(dot_nt(qq, km) * C2 - lse_c)
-            dsm = (pm * (dot_nt(dd, vm) - delta)).astype(BF16)
-            plo = jnp.where(ok, jnp.exp2(dot_nt(qq, k_ref[ks, :]) * C2 - lse_c), 0.0)
-            dsl = (plo * (dot_nt(dd, v_ref[ks, :]) - delta)).astype(BF16)
-            dq = (dot_nn(dsm, km) + dot_nn(dsl, k_ref[ks, :])) * scale
-            dq_ref[at, :] = turn(dq, cos_ref[own, :], -sin_ref[own, :]).astype(BF16)
-            sdk[ks, :] += dot_tn(dsl, qq)
-            sdv[ks, :] += dot_tn(plo.astype(BF16), dd)
-        dk_ref[...] = turn(sdk[...] * scale, cos_ref[...], -sin_ref[...]).astype(BF16)
-        dv_ref[...] = sdv[...].astype(BF16)
-
-    head = lambda n: pl.BlockSpec((n, HD), lambda h: (0, h))
-    mem = pl.BlockSpec((1, ksel, blk, HD), lambda h: (h // per, 0, 0, h % per))
-    return pl.pallas_call(
-        kern,
-        grid=(d // HD,),
-        in_specs=[head(r), head(rt), head(rt), mem, mem, full((r, 1)), full((1, rt)), head(r),
-                  pl.BlockSpec((1, r, 1), lambda h: (h, 0, 0)), head(r), full((rt, HD)), full((rt, HD))],
-        out_specs=[head(r), head(rt), head(rt)],
-        out_shape=[jax.ShapeDtypeStruct((n, d), BF16) for n in (r, rt, rt)],
-        scratch_shapes=[pltpu.VMEM((rt, HD), F32)] * 2,
-        compiler_params=pltpu.CompilerParams(vmem_limit_bytes=VL, dimension_semantics=("arbitrary",)),
-        name="attend_back",
-    )(q, k, v, mk, mv, seg_q, seg_k, o, lse, do, cos, sin)
-
-
-def out_norm(x, o, wo, gains):
-    r, d = x.shape
-    dp, nz, kk, _ = wo.shape
-
-    def kern(x_ref, o_ref, w_ref, gn_ref, h_ref, n_ref):
-        t = pl.program_id(0)
-
-        @pl.when(t == 0)
-        def _():
-            h_ref[...] = x_ref[...].astype(F32)
-
-        w = lanes(w_ref)
-        tile = 256
-
-        @pl.loop(0, r // tile)
-        def _(i):
-            at = pl.ds(pl.multiple_of(i * tile, tile), tile)
-            h_ref[at, :] += dot_nn(o_ref[at, :], w)
-
-        @pl.when(t == pl.num_programs(0) - 1)
-        def _():
-            h = h_ref[...]
-            n_ref[...] = (h * inv_rms(h) * gain_row(gn_ref, 1)).astype(BF16)
-
-    return pl.pallas_call(
-        kern,
-        grid=(nz,),
-        in_specs=[full((r, d)), pl.BlockSpec((r, kk), lambda t: (0, t)),
-                  pl.BlockSpec((dp, 1, kk, wo.shape[3]), lambda t: (0, t, 0, 0)), full(gains.shape)],
-        out_specs=[full((r, d)), full((r, d))],
-        out_shape=[jax.ShapeDtypeStruct((r, d), F32), jax.ShapeDtypeStruct((r, d), BF16)],
-        compiler_params=pltpu.CompilerParams(vmem_limit_bytes=VL, dimension_semantics=("arbitrary",)),
-        name="out_norm",
-    )(x, o, wo, gains)
-
-
-def feed(h, n2, c, gains, wg, wu, wd, wo):
-    r, d = h.shape
-    dp, nz, ff, _ = wg.shape
-    kk = wo.shape[2]
-
-    def kern(h_ref, n_ref, c_ref, gn_ref, wg_ref, wu_ref, wd_ref, wo_ref,
-             hid_ref, dg_ref, du_ref, out_ref, dh_ref, dhb_ref, do_ref, gg_ref, sg, su, sd, acc):
-        t = pl.program_id(0)
-        last = pl.num_programs(0) - 1
-        sg[...] = lanes(wg_ref)
-        su[...] = lanes(wu_ref)
-        sd[...] = lanes(wd_ref)
-
-        @pl.when(t == 0)
-        def _():
-            out_ref[...] = h_ref[...]
-            acc[...] = jnp.zeros_like(acc)
-
-        tile = 128
-
-        @pl.loop(0, r // tile)
-        def _(i):
-            at = pl.ds(pl.multiple_of(i * tile, tile), tile)
-            n = n_ref[at, :]
-            gate = dot_nt(n, sg[...])
-            up = dot_nt(n, su[...])
-            dhid = dot_nt(c_ref[at, :], sd[...])
-            sig = 1.0 / (1.0 + jnp.exp(-gate))
-            act = gate * sig
-            hid = (act * up).astype(BF16)
-            hid_ref[0, at, :] = hid
-            dg = (dhid * up * (sig * (1.0 + gate * (1.0 - sig)))).astype(BF16)
-            du = (dhid * act).astype(BF16)
-            dg_ref[0, at, :] = dg
-            du_ref[0, at, :] = du
-            out_ref[at, :] += dot_nn(hid, sd[...])
-            acc[at, :] += dot_nn(dg, sg[...]) + dot_nn(du, su[...])
-
-        @pl.when(t == last)
-        def _():
-            g = gain_row(gn_ref, 1)
-            h = h_ref[...]
-            dn = acc[...]
-            iv = inv_rms(h)
-            gg_ref[...] = jnp.sum(dn * h * iv, axis=0, keepdims=True)
-            gd = dn * g
-            dh = c_ref[...].astype(F32) + iv * gd - h * (iv * iv * iv * jnp.mean(h * gd, axis=1, keepdims=True))
-            dh_ref[...] = dh
-            dhb_ref[...] = dh.astype(BF16)
-
-            @pl.loop(0, nz)
-            def _(u):
-                w = jnp.concatenate([wo_ref[e, u] for e in range(dp)], axis=1)
-                do_ref[u] = dot_nt(dhb_ref[...], w).astype(BF16)
-
-    wspec = pl.BlockSpec((dp, 1, ff, wg.shape[3]), lambda t: (0, t, 0, 0))
-    piece = pl.BlockSpec((1, r, ff), lambda t: (t, 0, 0))
-    one = lambda s: full(s, 1)
-    return pl.pallas_call(
-        kern,
-        grid=(nz,),
-        in_specs=[one((r, d)), one((r, d)), one((r, d)), one(gains.shape), wspec, wspec, wspec, one(wo.shape)],
-        out_specs=[piece, piece, piece, full((r, d)), full((r, d)), full((r, d)), full((nz, r, kk)), full((1, d))],
-        out_shape=[jax.ShapeDtypeStruct((nz, r, ff), BF16)] * 3
-        + [jax.ShapeDtypeStruct((r, d), F32), jax.ShapeDtypeStruct((r, d), F32), jax.ShapeDtypeStruct((r, d), BF16),
-           jax.ShapeDtypeStruct((nz, r, kk), BF16), jax.ShapeDtypeStruct((1, d), F32)],
-        scratch_shapes=[pltpu.VMEM((ff, d), BF16)] * 3 + [pltpu.VMEM((r, d), F32)],
-        compiler_params=pltpu.CompilerParams(vmem_limit_bytes=VL, dimension_semantics=("arbitrary",)),
-        name="feed",
-    )(h, n2, c, gains, wg, wu, wd, wo)
-
-
-def project_back(halo, x, xh, dq, dk, dv, wq, wk, wv):
-    r, d = x.shape
-    dp, nz, _, cols = wq.shape
-    rt = (halo + 1) * r
-
-    def kern(x_ref, xh_ref, dq_ref, dk_ref, dv_ref, wq_ref, wk_ref, wv_ref, own_ref, hb_ref, gg_ref, acc, w_s):
-        t = pl.program_id(0)
-        w_s[:, 0:cols] = rows(wk_ref)
-        w_s[:, cols : 2 * cols] = rows(wv_ref)
-        w_s[:, 2 * cols :] = rows(wq_ref)
-
-        @pl.when(t == 0)
-        def _():
-            acc[...] = jnp.zeros_like(acc)
-
-        tile = 256
-
-        @pl.loop(0, rt // tile)
-        def _(i):
-            at = pl.ds(pl.multiple_of(i * tile, tile), tile)
-            acc[at, :] += dot_nt(jnp.concatenate([dk_ref[at, :], dv_ref[at, :]], axis=1), w_s[:, 0 : 2 * cols])
-
-        @pl.loop(0, r // tile)
-        def _(i):
-            at = pl.ds(pl.multiple_of(i * tile, tile), tile)
-            to = pl.ds(pl.multiple_of(i * tile + halo * r, tile), tile)
-            acc[to, :] += dot_nt(dq_ref[at, :], w_s[:, 2 * cols :])
-
-        @pl.when(t == pl.num_programs(0) - 1)
-        def _():
-            me = lax.axis_index("tensor")
-            own_ref[...] = acc[halo * r :, :]
-            hb_ref[...] = acc[: halo * r, :].astype(BF16)
-            v = x_ref[...].astype(F32)
-            g = jnp.sum(acc[halo * r :, :] * v * inv_rms(v), axis=0, keepdims=True)
-            for j in range(halo):
-                v = xh_ref[j].astype(F32)
-                lo = (halo - 1 - j) * r
-                more = jnp.sum(acc[lo : lo + r, :] * v * inv_rms(v), axis=0, keepdims=True)
-                g = g + jnp.where(me >= j + 1, more, jnp.zeros_like(more))
-            gg_ref[...] = g
-
-    wspec = pl.BlockSpec((dp, 1, wq.shape[2], cols), lambda t: (0, t, 0, 0))
-    col = lambda n: pl.BlockSpec((n, cols), lambda t: (0, t))
-    return pl.pallas_call(
-        kern,
-        grid=(nz,),
-        in_specs=[full((r, d)), full((halo, r, d)), col(r), col(rt), col(rt)] + [wspec] * 3,
-        out_specs=[full((r, d)), full((halo * r, d)), full((1, d))],
-        out_shape=[jax.ShapeDtypeStruct((r, d), F32), jax.ShapeDtypeStruct((halo * r, d), BF16),
-                   jax.ShapeDtypeStruct((1, d), F32)],
-        scratch_shapes=[pltpu.VMEM((rt, d), F32), pltpu.VMEM((d, 3 * cols), BF16)],
-        compiler_params=pltpu.CompilerParams(vmem_limit_bytes=VL, dimension_semantics=("arbitrary",)),
-        name="project_back",
-    )(x, xh, dq, dk, dv, wq, wk, wv)
-
-
-def feed_grads(hid, dg, du, n2, c):
-    nz, r, ff = hid[0].shape
-    half = n2[0].shape[1]
-    nb = half // 128
-
-    def kern(h0, h1, g0, g1, u0, u1, n0, n1, c0, c1, gg, gu, gd):
-        def put(out, a0, a1, b0, b1):
-            y = (dot_tn(a0[0], b0[...]) + dot_tn(a1[0], b1[...])).astype(BF16)
-            for e in range(nb):
-                out[e, 0] = y[:, e * 128 : (e + 1) * 128]
-
-        put(gg, g0, g1, n0, n1)
-        put(gu, u0, u1, n0, n1)
-        put(gd, h0, h1, c0, c1)
-
-    piece = pl.BlockSpec((1, r, ff), lambda t: (t, 0, 0))
-    out = pl.BlockSpec((nb, 1, ff, 128), lambda t: (0, t, 0, 0))
-    return pl.pallas_call(
-        kern,
-        grid=(nz,),
-        in_specs=[piece] * 6 + [full((r, half))] * 4,
-        out_specs=[out] * 3,
-        out_shape=[jax.ShapeDtypeStruct((nb, nz, ff, 128), BF16)] * 3,
-        compiler_params=pltpu.CompilerParams(vmem_limit_bytes=VL, dimension_semantics=("arbitrary",)),
-        name="feed_grads",
-    )(*hid, *dg, *du, *n2, *c)
-
-
-def attn_grads(halo, nz, o, dhb, n1, dq, dk, dv):
-    r, d = o[0].shape
-    half = dhb[0].shape[1]
-    rt = (halo + 1) * r
-    nb, cols = half // 128, d // nz
-
-    def kern(o0, o1, b0, b1, n0, m1, q0, q1, k0, k1, v0, v1, go, gq, gk, gv):
-        y = (dot_tn(o0[...], b0[...]) + dot_tn(o1[...], b1[...])).astype(BF16)
-        for e in range(nb):
-            go[e, 0] = y[:, e * 128 : (e + 1) * 128]
-        own = pl.ds(halo * r, r)
-        for out, p0, p1, a0, a1 in (
-            (gq, q0, q1, n0.at[own], m1.at[own]),
-            (gk, k0, k1, n0, m1),
-            (gv, v0, v1, n0, m1),
-        ):
-            y = (dot_tn(a0[...], p0[...]) + dot_tn(a1[...], p1[...])).astype(BF16)
-            for e in range(nb):
-                out[e, 0] = y[e * 128 : (e + 1) * 128, :]
-
-    col = lambda n: pl.BlockSpec((n, cols), lambda t: (0, t))
-    out1 = pl.BlockSpec((nb, 1, cols, 128), lambda t: (0, t, 0, 0))
-    out2 = pl.BlockSpec((nb, 1, 128, cols), lambda t: (0, t, 0, 0))
-    return pl.pallas_call(
-        kern,
-        grid=(nz,),
-        in_specs=[col(r)] * 2 + [full((r, half))] * 2 + [full((rt, half))] * 2 + [col(r)] * 2 + [col(rt)] * 4,
-        out_specs=[out1, out2, out2, out2],
-        out_shape=[jax.ShapeDtypeStruct((nb, nz, cols, 128), BF16)]
-        + [jax.ShapeDtypeStruct((nb, nz, 128, cols), BF16)] * 3,
-        compiler_params=pltpu.CompilerParams(vmem_limit_bytes=VL, dimension_semantics=("arbitrary",)),
-        name="attn_grads",
-    )(*o, *dhb, *n1, *dq, *dk, *dv)
-
-
-def input_grad(halo, x, gains, dn1, more, dh):
-    r, d = x.shape
-    tile = 256
-
-    def kern(x_ref, gn_ref, dn_ref, m_ref, dh_ref, out_ref):
-        t = lax.axis_index("tensor")
-        nz = lax.axis_size("tensor")
-        dn = dn_ref[...]
-        for j in range(halo):
-            v = m_ref[j].astype(F32)
-            dn = dn + jnp.where(t + j + 1 < nz, v, jnp.zeros_like(v))
-        v = x_ref[...].astype(F32)
-        iv = inv_rms(v)
-        gd = dn * gain_row(gn_ref, 0)
-        out_ref[...] = dh_ref[...] + iv * gd - v * (iv * iv * iv * jnp.mean(v * gd, axis=1, keepdims=True))
-
-    row = pl.BlockSpec((tile, d), lambda i: (i, 0))
-    return pl.pallas_call(
-        kern,
-        grid=(r // tile,),
-        in_specs=[row, full(gains.shape), row, pl.BlockSpec((halo, tile, d), lambda i: (0, i, 0)), row],
-        out_specs=row,
-        out_shape=jax.ShapeDtypeStruct((r, d), F32),
-        compiler_params=pltpu.CompilerParams(vmem_limit_bytes=VL, dimension_semantics=("arbitrary",)),
-        name="input_grad",
-    )(x, gains, dn1, more, dh)
 
 
 def fwd_kernel(g, cap, nq, ksel, halo, window, units, n_w, *refs):
@@ -930,10 +526,119 @@
     )(requests, sel, seg_q, seg_k, x, gains, mem_k, mem_v, cos, sin, *shards)
 
 
+def feed(g, h, n2, c, gains, wg, wu, wd, wo):
+    r, d = h.shape
+    dp, nz, ff, _ = wg.shape
+    kk = wo.shape[2]
+    half = d // 2
+
+    def kern(h_ref, n_ref, c_ref, gn_ref, wg_ref, wu_ref, wd_ref, wo_ref,
+             hid_ref, dg_ref, du_ref, out_ref, dh_ref, dhb_ref, do_ref, gg_ref, phid, pdg, pdu, pn, pc,
+             sg, su, sd, acc, ss, rs, hs, hr):
+        t = pl.program_id(0)
+        last = pl.num_programs(0) - 1
+        _, _, core, tz, me = coords(g)
+        peer = me + 1 - 2 * core
+
+        def half_copies():
+            res = []
+            for i, (src, dst) in enumerate(((n_ref, pn), (c_ref, pc))):
+                for e in range(dp // 2):
+                    col = pl.multiple_of((2 * e + 1 - core) * 128, 128)
+                    res.append(send(src.at[:, pl.ds(col, 128)], dst.at[:, pl.ds(e * 128, 128)],
+                                    hs.at[i, e], hr.at[i, e], peer, tz))
+            return res
+
+        def hidden_copies(u):
+            return [send(src.at[0], dst.at[u], ss.at[i, u], rs.at[i, u], peer, tz)
+                    for i, (src, dst) in enumerate(((hid_ref, phid), (dg_ref, pdg), (du_ref, pdu)))]
+
+        @pl.when(t == 0)
+        def _():
+            bar = pltpu.get_barrier_semaphore()
+            pl.semaphore_signal(bar, inc=1, device_id=(peer, tz), device_id_type=MESH)
+            pl.semaphore_wait(bar, 1)
+            for m in half_copies():
+                m.start()
+            out_ref[...] = h_ref[...]
+            acc[...] = jnp.zeros_like(acc)
+
+        for e in range(dp):
+            at = slice(e * 128, (e + 1) * 128)
+            sg[:, at] = wg_ref[e, 0]
+            su[:, at] = wu_ref[e, 0]
+            sd[:, at] = wd_ref[e, 0]
+        tile = ff // 2
+
+        @pl.loop(0, 2)
+        def _(i):
+            at = pl.ds(pl.multiple_of(i * tile, 16), tile)
+            gate = dot_nt(sg[at, :], n_ref[...])
+            up = dot_nt(su[at, :], n_ref[...])
+            dhid = dot_nt(sd[at, :], c_ref[...])
+            sig = 1.0 / (1.0 + jnp.exp(-gate))
+            act = gate * sig
+            hid_ref[0, at, :] = (act * up).astype(BF16)
+            dg_ref[0, at, :] = (dhid * up * (sig * (1.0 + gate * (1.0 - sig)))).astype(BF16)
+            du_ref[0, at, :] = (dhid * act).astype(BF16)
+
+        for m in hidden_copies(t):
+            m.start()
+        out_ref[...] += dot_tn(hid_ref[0], sd[...])
+        acc[...] += dot_tn(dg_ref[0], sg[...]) + dot_tn(du_ref[0], su[...])
+        for m in hidden_copies(t):
+            m.wait_send()
+
+        @pl.when(t == last)
+        def _():
+            gn = gain_row(gn_ref, 1)
+            h = h_ref[...]
+            dn = acc[...]
+            iv = inv_rms(h)
+            gg_ref[...] = jnp.sum(dn * h * iv, axis=0, keepdims=True)
+            gd = dn * gn
+            dh = c_ref[...].astype(F32) + iv * gd - h * (iv * iv * iv * jnp.mean(h * gd, axis=1, keepdims=True))
+            dh_ref[...] = dh
+            dhb_ref[...] = dh.astype(BF16)
+
+            @pl.loop(0, nz)
+            def _(u):
+                w = jnp.concatenate([wo_ref[e, u] for e in range(dp)], axis=1)
+                do_ref[u] = dot_nt(dhb_ref[...], w).astype(BF16)
+
+            for m in half_copies():
+                m.wait()
+            for u in range(nz):
+                for m in hidden_copies(u):
+                    m.wait_recv()
+
+    wspec = pl.BlockSpec((dp, 1, ff, wg.shape[3]), lambda t: (0, t, 0, 0))
+    piece = pl.BlockSpec((1, ff, r), lambda t: (t, 0, 0))
+    one = lambda s: full(s, 1)
+    any_ = pl.BlockSpec(memory_space=pl.ANY)
+    st = lambda s, dt=BF16: jax.ShapeDtypeStruct(s, dt)
+    dma = lambda *n: pltpu.SemaphoreType.DMA(n)
+    return pl.pallas_call(
+        kern,
+        grid=(nz,),
+        in_specs=[one((r, d)), one((r, d)), one((r, d)), one(gains.shape), wspec, wspec, wspec, one(wo.shape)],
+        out_specs=[piece, piece, piece, full((r, d)), full((r, d)), full((r, d)), full((nz, r, kk)), full((1, d))]
+        + [any_] * 5,
+        out_shape=[st((nz, ff, r))] * 3
+        + [st((r, d), F32), st((r, d), F32), st((r, d)), st((nz, r, kk)), st((1, d), F32)]
+        + [st((nz, ff, r))] * 3 + [st((r, half))] * 2,
+        scratch_shapes=[pltpu.VMEM((ff, d), BF16)] * 3 + [pltpu.VMEM((r, d), F32)]
+        + [dma(3, nz)] * 2 + [dma(2, dp // 2)] * 2,
+        compiler_params=pltpu.CompilerParams(vmem_limit_bytes=VL, dimension_semantics=("arbitrary",),
+                                             collective_id=2, has_side_effects=True),
+        name="feed",
+    )(h, n2, c, gains, wg, wu, wd, wo)
+
+
 class Scatter:
-    def __init__(self, g, src, rows, b_first, bufs, sems, out):
-        self.g, self.src, self.rows, self.b_first, self.out = g, src, rows, b_first, out
-        self.acc, self.r1, self.r2, self.r3 = bufs
+    def __init__(self, g, src, rows_, b_first, bufs, sems, out):
+        self.g, self.src, self.rows, self.b_first, self.out = g, src, rows_, b_first, out
+        self.r1, self.r2, self.r3 = bufs
         self.sems, self.next = sems, 0
         self.sent = []
 
@@ -944,9 +649,6 @@
 
     def _e(self, f, s):
         return s * self.g.nb + f if self.b_first else f * self.g.nb + s
-
-    def _dp(self, f, s, c):
-        return self._e(f, s) * 2 + c
 
     def _mine(self):
         a, b, c, t, me = coords(self.g)
@@ -957,208 +659,395 @@
     def start_first(self):
         f, s, c, t, me, n1, n2 = self._mine()
         lo, n = self.rows
-        self.own, self.first = [], []
+        self.first = []
         for k in range(1, n1):
             to = (f + k) % n1
             for j in range(n2):
                 x, y = self._sem()
-                d = send(self.src.at[self._e(to, j), :, pl.ds(lo, n), :], self.r1.at[k - 1, j], x, y, self._dp(to, s, c), t)
-                d.start()
-                self.first.append(d)
-        for j in range(n2):
-            x, _ = self._sem()
-            d = pltpu.make_async_copy(self.src.at[self._e(f, j), :, pl.ds(lo, n), :], self.acc.at[j], x)
-            d.start()
-            self.own.append(d)
+                m = send(self.src.at[self._e(to, j), :, pl.ds(lo, n), :], self.r1.at[k - 1, j], x, y,
+                         self._e(to, s) * 2 + c, t)
+                m.start()
+                self.first.append(m)
         self.sent += self.first
 
     def start_second(self):
         f, s, c, t, me, n1, n2 = self._mine()
-        for d in self.own:
-            d.wait()
-        for d in self.first:
-            d.wait_recv()
+        lo, n = self.rows
+        for m in self.first:
+            m.wait_recv()
         for j in range(n2):
+            e = self._e(f, j)
 
             @pl.loop(0, self.g.nz)
             def _(u):
-                v = self.acc[j, u].astype(F32)
+                v = self.src[e, u, lo : lo + n, :].astype(F32)
                 for k in range(n1 - 1):
                     v = v + self.r1[k, j, u].astype(F32)
-                self.acc[j, u] = v.astype(BF16)
+                self.src[e, u, lo : lo + n, :] = v.astype(BF16)
 
         self.second = []
         for k in range(1, n2):
             to = (s + k) % n2
             x, y = self._sem()
-            d = send(self.acc.at[to], self.r2.at[k - 1], x, y, self._dp(f, to, c), t)
-            d.start()
-            self.second.append(d)
+            m = send(self.src.at[self._e(f, to), :, pl.ds(lo, n), :], self.r2.at[k - 1], x, y, self._e(f, to) * 2 + c, t)
+            m.start()
+            self.second.append(m)
         self.sent += self.second
 
     def start_z(self):
         f, s, c, t, me, n1, n2 = self._mine()
-        for d in self.second:
-            d.wait_recv()
+        lo, n = self.rows
+        e = self._e(f, s)
+        for m in self.second:
+            m.wait_recv()
 
         @pl.loop(0, self.g.nz)
         def _(u):
-            v = self.acc[s, u].astype(F32)
+            v = self.src[e, u, lo : lo + n, :].astype(F32)
             for k in range(n2 - 1):
                 v = v + self.r2[k, u].astype(F32)
-            self.acc[s, u] = v.astype(BF16)
+            self.src[e, u, lo : lo + n, :] = v.astype(BF16)
 
         self.third = []
         for k in range(1, self.g.nz):
             to = (t + k) % self.g.nz
             x, y = self._sem()
-            d = send(self.acc.at[s, to], self.r3.at[k - 1], x, y, me, to)
-            d.start()
-            self.third.append(d)
+            m = send(self.src.at[e, to, pl.ds(lo, n), :], self.r3.at[k - 1], x, y, me, to)
+            m.start()
+            self.third.append(m)
         self.sent += self.third
 
     def finish(self):
         f, s, c, t, me, n1, n2 = self._mine()
         lo, n = self.rows
-        for d in self.third:
-            d.wait_recv()
-        v = self.acc[s, t].astype(F32)
+        for m in self.third:
+            m.wait_recv()
+        v = self.src[self._e(f, s), t, lo : lo + n, :].astype(F32)
         for k in range(self.g.nz - 1):
             v = v + self.r3[k].astype(F32)
         self.out[pl.ds(lo, n), :] = v
-        for d in self.sent:
-            d.wait_send()
+        for m in self.sent:
+            m.wait_send()
 
 
 def scatter_sems(g):
-    return (g.na - 1) * g.na + g.na + (g.na - 1) + (g.nz - 1)
-
-
-def k2_kernel(g, halo, units, n_w, *refs):
+    return (g.na - 1) * g.na + (g.na - 1) + (g.nz - 1)
+
+
+def back_kernel(g, halo, window, units, *refs):
     refs = list(refs)
     take = lambda n: [refs.pop(0) for _ in range(n)]
-    gains, hb = take(2)
-    srcs = take(n_w)
-    gout, more = take(2)
-    outs = take(n_w)
-    bufs = [take(4) for _ in units]
+    seg_q, seg_k, gg_ffn, gn_ref = take(4)
+    hid, dg, du, phid, pdg, pdu, n2, c_in, pn, pc = take(10)
+    q, k, v, mk, mv, o, lse, do, dhb, n1 = take(10)
+    x, xh, dh, wq, wk, wv, cos, sin = take(8)
+    gout, grad_in = take(2)
+    outs = take(7)
+    dq, dk, dv, pdq, pdk, pdv, po = take(7)
+    G = take(7)
+    bufs = [take(3) for _ in units]
     sems = [take(2) for _ in units]
-    gz, gs, gd = take(3)
-    zss, zrs, dss, drs, hss, hrs = take(6)
-    a, b, c, t, me = coords(g)
+    n2_v, pn_v, c_v, pc_v, n1_v, pn1_v, dhb_v, pdhb_v = take(8)
+    x_v, xh_v, dh_v, acc, hb_v, more, cos_v, sin_v, sdk, sdv, w_s = take(11)
+    gz, gs, gd, gp = take(4)
+    zss, zrs, dss, drs, hss, hrs, ls, css, crs = take(9)
+    a, b, core, t, me = coords(g)
+    peer = me + 1 - 2 * core
+    r, d = x_v.shape
+    rt = (halo + 1) * r
+    nz, ff, _ = hid.shape
+    dp, _, kd, cols = wq.shape
+    nb = dp // 2
+    half = d // 2
+    ksel, blk = mk.shape[1:3]
+    nm, per_t = ksel * blk, cols // HD
     greet(g, me, t)
-    us = [
-        Scatter(g, srcs[w], rows, bf, bufs[i], sems[i], outs[w]) for i, (w, rows, bf) in enumerate(units)
-    ]
-    pairs = [us[i : i + 2] for i in range(0, len(us), 2)]
-    np_ = len(pairs)
-    r = more.shape[1]
+    us = [Scatter(g, G[w], rows_, bf, bufs[i], sems[i], outs[w]) for i, (w, rows_, bf) in enumerate(units)]
+    of = lambda *ws: [u for u, (w, _, _) in zip(us, units) if w in ws]
+
+    loads = []
+
+    def load(src, dst):
+        m = pltpu.make_async_copy(src, dst, ls.at[len(loads)])
+        m.start()
+        loads.append(m)
+        return m
+
+    def mine(src, dst):
+        return [load(src.at[:, pl.ds(pl.multiple_of((2 * e + core) * 128, 128), 128)], dst.at[:, pl.ds(e * 128, 128)])
+                for e in range(nb)]
+
+    l_ffn = mine(n2, n2_v) + mine(c_in, c_v) + [load(pn, pn_v), load(pc, pc_v)]
+    l_rest = mine(n1, n1_v) + mine(dhb, dhb_v)
+    l_x = [load(x, x_v), load(dh, dh_v), load(cos, cos_v), load(sin, sin_v)]
+    cores = []
+
+    def to_peer(src, dst):
+        i = len(cores)
+        m = send(src, dst, css.at[i], crs.at[i], peer, t)
+        m.start()
+        cores.append(m)
+        return m
+
+    def theirs(src, dst):
+        return [to_peer(src.at[:, pl.ds(pl.multiple_of((2 * e + 1 - core) * 128, 128), 128)], dst.at[:, pl.ds(e * 128, 128)])
+                for e in range(nb)]
+
+    p_rest = theirs(n1, pn1_v) + theirs(dhb, pdhb_v) + [to_peer(o, po)]
+    for m in l_ffn:
+        m.wait()
+
+    def ffn_grads(A, B, mine_v, peer_v, out):
+        def body(a_ref, b_ref):
+            u = pl.program_id(0)
+            y = (dot_nn(a_ref[0], mine_v[...]) + dot_nn(b_ref[0], peer_v[...])).astype(BF16)
+            for e in range(nb):
+                out[e, u] = y[:, e * 128 : (e + 1) * 128]
+
+        piece = pl.BlockSpec((1, ff, r), lambda u: (u, 0, 0))
+        pltpu.emit_pipeline(body, grid=(nz,), in_specs=[piece] * 2)(A, B)
+
+    ffn_grads(hid, phid, c_v, pc_v, G[2])
+    for u in of(2):
+        u.start_first()
+    ffn_grads(dg, pdg, n2_v, pn_v, G[0])
+    for u in of(0):
+        u.start_first()
+    ffn_grads(du, pdu, n2_v, pn_v, G[1])
+    for u in of(1):
+        u.start_first()
+    for m in l_rest + p_rest + l_x:
+        m.wait()
+
+    col = lambda n: pl.BlockSpec((n, cols), lambda u: (0, u))
+
+    def out_grads(a_ref, b_ref):
+        u = pl.program_id(0)
+        y = (dot_tn(a_ref[...], dhb_v[...]) + dot_tn(b_ref[...], pdhb_v[...])).astype(BF16)
+        for e in range(nb):
+            G[3][e, u] = y[:, e * 128 : (e + 1) * 128]
+
+    pltpu.emit_pipeline(out_grads, grid=(nz,), in_specs=[col(r)] * 2)(o, po)
+    for u in of(2):
+        u.start_second()
+
+    scale = HD**-0.5
+
+    def attend_back(q_ref, k_ref, v_ref, mk_ref, mv_ref, o_ref, l_ref, do_ref, dq_ref, dk_ref, dv_ref):
+        km = mk_ref[0].reshape(nm, HD)
+        vm = mv_ref[0].reshape(nm, HD)
+        sdk[...] = jnp.zeros_like(sdk)
+        sdv[...] = jnp.zeros_like(sdv)
+        for i in range(r // QT):
+            at = slice(i * QT, (i + 1) * QT)
+            k0 = halo * r - window + i * QT
+            ks = slice(k0, k0 + window + QT)
+            own = slice(halo * r + i * QT, halo * r + (i + 1) * QT)
+            qq, dd = q_ref[at, :], do_ref[0, at, :]
+            lse_c = l_ref[0, at, :]
+            delta = jnp.sum(dd.astype(F32) * o_ref[at, :].astype(F32), axis=1, keepdims=True)
+            ok = allowed_of(seg_q[at, :], seg_k[:, ks], halo * r + i * QT, k0)
+            pm = jnp.exp2(dot_nt(qq, km) * C2 - lse_c)
+            dsm = (pm * (dot_nt(dd, vm) - delta)).astype(BF16)
+            plo = jnp.where(ok, jnp.exp2(dot_nt(qq, k_ref[ks, :]) * C2 - lse_c), 0.0)
+            dsl = (plo * (dot_nt(dd, v_ref[ks, :]) - delta)).astype(BF16)
+            dqv = (dot_nn(dsm, km) + dot_nn(dsl, k_ref[ks, :])) * scale
+            dq_ref[at, :] = turn(dqv, cos_v[own, :], -sin_v[own, :]).astype(BF16)
+            sdk[ks, :] += dot_tn(dsl, qq)
+            sdv[ks, :] += dot_tn(plo.astype(BF16), dd)
+        dk_ref[...] = turn(sdk[...] * scale, cos_v[...], -sin_v[...]).astype(BF16)
+        dv_ref[...] = sdv[...].astype(BF16)
+
+    head = lambda n: pl.BlockSpec((n, HD), lambda h: (0, h))
+    mem = pl.BlockSpec((1, ksel, blk, HD), lambda h: (h // per_t, 0, 0, h % per_t))
+    pltpu.emit_pipeline(
+        attend_back,
+        grid=(d // HD,),
+        in_specs=[head(r), head(rt), head(rt), mem, mem, head(r), pl.BlockSpec((1, r, 1), lambda h: (h, 0, 0)),
+                  pl.BlockSpec((1, r, HD), lambda h: (h // per_t, 0, h % per_t))],
+        out_specs=[head(r), head(rt), head(rt)],
+    )(q, k, v, mk, mv, o, lse, do, dq, dk, dv)
+    p_att = [to_peer(dq, pdq), to_peer(dk, pdk), to_peer(dv, pdv)]
+    for u in of(0):
+        u.start_second()
+    for u in of(3):
+        u.start_first()
+    for u in of(2):
+        u.start_z()
+
+    acc[...] = jnp.zeros_like(acc)
+
+    def project_back(dq_ref, dk_ref, dv_ref, wq_ref, wk_ref, wv_ref):
+        for e in range(dp):
+            at = slice(e * kd, (e + 1) * kd)
+            w_s[at, 0:cols] = wk_ref[e, 0]
+            w_s[at, cols : 2 * cols] = wv_ref[e, 0]
+            w_s[at, 2 * cols :] = wq_ref[e, 0]
+        tile = 512
+
+        @pl.loop(0, rt // tile)
+        def _(i):
+            at = pl.ds(pl.multiple_of(i * tile, tile), tile)
+            acc[at, :] += dot_nt(jnp.concatenate([dk_ref[at, :], dv_ref[at, :]], axis=1), w_s[:, 0 : 2 * cols])
+
+        acc[halo * r :, :] += dot_nt(dq_ref[...], w_s[:, 2 * cols :])
+
+    wspec = pl.BlockSpec((dp, 1, kd, cols), lambda u: (0, u, 0, 0))
+    pltpu.emit_pipeline(project_back, grid=(nz,), in_specs=[col(r), col(rt), col(rt)] + [wspec] * 3)(
+        dq, dk, dv, wq, wk, wv
+    )
+    hb_v[...] = acc[: halo * r, :].astype(BF16)
     hd = []
     for j in range(halo):
-        d = send(hb.at[pl.ds((halo - 1 - j) * r, r), :], more.at[j], hss.at[j], hrs.at[j], me, (t + g.nz - 1 - j) % g.nz)
-        hd.append(d)
+        m = send(hb_v.at[pl.ds((halo - 1 - j) * r, r), :], more.at[j], hss.at[j], hrs.at[j], me, (t + g.nz - 1 - j) % g.nz)
+        hd.append(m)
 
         @pl.when(t >= j + 1)
         def _():
-            d.start()
+            m.start()
+
+    vx = x_v[...].astype(F32)
+    gp[0:1, :] = jnp.sum(acc[halo * r :, :] * vx * inv_rms(vx), axis=0, keepdims=True)
+    gp[1:2, :] = gg_ffn[...]
+    for j in range(halo):
+
+        @pl.when(t >= j + 1)
+        def _():
+            cx = pltpu.make_async_copy(xh.at[j], xh_v, zss.at[g.nz - 1])
+            cx.start()
+            cx.wait()
+            vh = xh_v[...].astype(F32)
+            lo = (halo - 1 - j) * r
+            gp[0:1, :] = gp[0:1, :] + jnp.sum(acc[lo : lo + r, :] * vh * inv_rms(vh), axis=0, keepdims=True)
 
     zg = []
-    for k in range(1, g.nz):
-        d = send(gains, gz.at[k - 1], zss.at[k - 1], zrs.at[k - 1], me, (t + k) % g.nz)
-        d.start()
-        zg.append(d)
-    for p in range(min(2, np_)):
-        for u in pairs[p]:
-            u.start_first()
-    for d in zg:
-        d.wait()
-    tot = gains[...]
-    for k in range(g.nz - 1):
-        tot = tot + gz[k]
+    for i in range(1, g.nz):
+        m = send(gp, gz.at[i - 1], zss.at[i - 1], zrs.at[i - 1], me, (t + i) % g.nz)
+        m.start()
+        zg.append(m)
+    for u in of(1):
+        u.start_second()
+    for u in of(0):
+        u.start_z()
+    for m in p_att:
+        m.wait()
+
+    own = pl.ds(halo * r, r)
+
+    def proj_grads(q0, q1, k0, k1, v0, v1):
+        u = pl.program_id(0)
+        for out, p0, p1, a0, a1 in (
+            (G[4], q0, q1, n1_v.at[own], pn1_v.at[own]),
+            (G[5], k0, k1, n1_v, pn1_v),
+            (G[6], v0, v1, n1_v, pn1_v),
+        ):
+            y = (dot_tn(a0[...], p0[...]) + dot_tn(a1[...], p1[...])).astype(BF16)
+            for e in range(nb):
+                out[e, u] = y[e * 128 : (e + 1) * 128, :]
+
+    pltpu.emit_pipeline(proj_grads, grid=(nz,), in_specs=[col(r)] * 2 + [col(rt)] * 4)(dq, pdq, dk, pdk, dv, pdv)
+    for u in of(4, 5, 6):
+        u.start_first()
+    for m in zg:
+        m.wait()
+    tot = gp[...]
+    for i in range(g.nz - 1):
+        tot = tot + gz[i]
     for e in range(g.dp):
         gs[e] = tot[:, e * 128 : (e + 1) * 128]
-    dg = []
-    for k in range(1, g.dp):
-        to = (me + k) % g.dp
-        d = send(gs.at[to], gd.at[me], dss.at[k], drs.at[k], to, t)
-        d.start()
-        dg.append(d)
-    own = pltpu.make_async_copy(gs.at[me], gd.at[me], dss.at[0])
-    own.start()
-    for p in range(np_):
-        for u in pairs[p]:
-            u.start_second()
-        if p + 2 < np_:
-            for u in pairs[p + 2]:
-                u.start_first()
-        if p >= 1:
-            for u in pairs[p - 1]:
-                u.start_z()
-    for u in pairs[-1]:
+    ds_ = []
+    for i in range(1, g.dp):
+        to = (me + i) % g.dp
+        m = send(gs.at[to], gd.at[me], dss.at[i], drs.at[i], to, t)
+        m.start()
+        ds_.append(m)
+    og = pltpu.make_async_copy(gs.at[me], gd.at[me], dss.at[0])
+    og.start()
+    for u in of(3):
+        u.start_second()
+    for u in of(1):
         u.start_z()
-    own.wait()
-    for d in dg:
-        d.wait()
-    v = gd[0]
+    for u in of(4, 5, 6):
+        u.start_second()
+    for u in of(3):
+        u.start_z()
+
+    for j, m in enumerate(hd):
+
+        @pl.when(t + j + 1 < g.nz)
+        def _():
+            m.wait_recv()
+            acc[halo * r :, :] = acc[halo * r :, :] + more[j].astype(F32)
+
+        @pl.when(t >= j + 1)
+        def _():
+            m.wait_send()
+
+    vx = x_v[...].astype(F32)
+    iv = inv_rms(vx)
+    gd_ = acc[halo * r :, :] * gain_row(gn_ref, 0)
+    grad_in[...] = dh_v[...] + iv * gd_ - vx * (iv * iv * iv * jnp.mean(vx * gd_, axis=1, keepdims=True))
+    for u in of(4, 5, 6):
+        u.start_z()
+    og.wait()
+    for m in ds_:
+        m.wait()
+    s = gd[0]
     for e in range(1, g.dp):
-        v = v + gd[e]
-    gout[...] = v
+        s = s + gd[e]
+    gout[...] = s
     for u in us:
         u.finish()
-    for j, d in enumerate(hd):
-
-        @pl.when(t >= j + 1)
-        def _():
-            d.wait_send()
-
-        @pl.when(t + j + 1 < g.nz)
-        def _():
-            d.wait_recv()
-
-
-def halves(srcs_rows):
-    units = []
-    for item in srcs_rows:
-        if len(item) == 2:
-            (w0, n0), (w1, n1) = item
-            units += [(w0, (0, n0), True), (w1, (0, n1), False)]
-        else:
-            ((w, n),) = item
-            units += [(w, (0, n // 2), True), (w, (n // 2, n - n // 2), False)]
-    return units
-
-
-def k2(g, halo, gains, hb, srcs, units, r):
+
+
+def back(g, halo, window, seg_q, seg_k, gg_ffn, gains, hid, dg, du, phid, pdg, pdu, n2, c, pn, pc,
+         q, k, v, mk, mv, o, lse, do, dhb, n1, x, xh, dh, wq, wk, wv, cos, sin):
+    r, d = x.shape
+    rt = (halo + 1) * r
+    nz, ff, _ = hid.shape
+    dp, _, kd, cols = wq.shape
+    nb, half = dp // 2, d // 2
     any_ = pl.BlockSpec(memory_space=pl.ANY)
     vm = pl.BlockSpec(memory_space=pltpu.VMEM)
     dma = lambda *n: pltpu.SemaphoreType.DMA(n)
-    d = hb.shape[1]
-    n_w = len(srcs)
-    scratch = []
+    st = lambda s, dt=BF16: jax.ShapeDtypeStruct(s, dt)
+    pieces = [(ff, 128)] * 3 + [(cols, 128)] + [(kd, cols)] * 3
+    units = []
+    for w in (2, 0, 1, 3):
+        n = pieces[w][0]
+        units += [(w, (0, n // 2), True), (w, (n // 2, n - n // 2), False)]
+    units += [(4, (0, kd), True), (5, (0, kd), False), (6, (0, kd // 2), True), (6, (kd // 2, kd - kd // 2), False)]
+    scratch = [pltpu.VMEM((nb, nz) + p, BF16) for p in pieces]
     for w, (lo, n), bf in units:
-        cols = srcs[w].shape[3]
-        n1, n2 = (g.nb, g.na) if bf else (g.na, g.nb)
+        cc = pieces[w][1]
+        n1_, n2_ = (g.nb, g.na) if bf else (g.na, g.nb)
         scratch += [
-            pltpu.VMEM((n2, g.nz, n, cols), BF16),
-            pltpu.VMEM((n1 - 1, n2, g.nz, n, cols), BF16),
-            pltpu.VMEM((n2 - 1, g.nz, n, cols), BF16),
-            pltpu.VMEM((g.nz - 1, n, cols), BF16),
+            pltpu.VMEM((n1_ - 1, n2_, nz, n, cc), BF16),
+            pltpu.VMEM((n2_ - 1, nz, n, cc), BF16),
+            pltpu.VMEM((nz - 1, n, cc), BF16),
         ]
     scratch += [dma(scatter_sems(g))] * (2 * len(units))
-    scratch += [pltpu.VMEM((g.nz - 1,) + gains.shape, F32), pltpu.VMEM((g.dp, 2, 128), F32), pltpu.VMEM((g.dp, 2, 128), F32)]
-    scratch += [dma(g.nz), dma(g.nz), dma(g.dp), dma(g.dp), dma(halo), dma(halo)]
-    out_shape = [jax.ShapeDtypeStruct((2, 128), F32), jax.ShapeDtypeStruct((halo, r, d), BF16)] + [
-        jax.ShapeDtypeStruct(s.shape[2:], F32) for s in srcs
-    ]
+    scratch += [pltpu.VMEM((r, half), BF16)] * 4 + [pltpu.VMEM((rt, half), BF16)] * 2 + [pltpu.VMEM((r, half), BF16)] * 2
+    scratch += [pltpu.VMEM((r, d), BF16)] * 2 + [pltpu.VMEM((r, d), F32), pltpu.VMEM((rt, d), F32)]
+    scratch += [pltpu.VMEM((halo * r, d), BF16), pltpu.VMEM((halo, r, d), BF16)]
+    scratch += [pltpu.VMEM((rt, HD), F32)] * 4 + [pltpu.VMEM((d, 3 * cols), BF16)]
+    scratch += [pltpu.VMEM((nz - 1, 2, d), F32), pltpu.VMEM((dp, 2, 128), F32), pltpu.VMEM((dp, 2, 128), F32), pltpu.VMEM((2, d), F32)]
+    scratch += [dma(nz), dma(nz), dma(dp), dma(dp), dma(halo), dma(halo), dma(4 * nb + 6), dma(2 * nb + 4), dma(2 * nb + 4)]
+    out_shape = (
+        [st((2, 128), F32), st((r, d), F32)]
+        + [st(p, F32) for p in pieces]
+        + [st((r, d)), st((rt, d)), st((rt, d)), st((r, d)), st((rt, d)), st((rt, d)), st((r, d))]
+    )
     return pl.pallas_call(
-        functools.partial(k2_kernel, g, halo, units, n_w),
+        functools.partial(back_kernel, g, halo, window, units),
         out_shape=out_shape,
-        in_specs=[vm, any_] + [any_] * n_w,
-        out_specs=[vm, any_] + [vm] * n_w,
+        in_specs=[vm] * 4 + [any_] * 28,
+        out_specs=[vm] * 9 + [any_] * 7,
         scratch_shapes=scratch,
-        compiler_params=pltpu.CompilerParams(collective_id=1, has_side_effects=True, vmem_limit_bytes=60 * 2**20),
-        name="bwd_exchange",
-    )(gains, hb, *srcs)
+        compiler_params=pltpu.CompilerParams(collective_id=1, has_side_effects=True, vmem_limit_bytes=63 * 2**20),
+        name="backward",
+    )(seg_q, seg_k, gg_ffn, gains, hid, dg, du, phid, pdg, pdu, n2, c, pn, pc, q, k, v, mk, mv, o, lse, do, dhb, n1,
+      x, xh, dh, wq, wk, wv, cos, sin)
 
 
 HEADS = 8
@@ -1511,30 +1400,11 @@
         g, cap, halo, window, req, sel, seg_q, seg_k, x, gains, flat(memory_keys), flat(memory_values), cos, sin,
         shards, nq, ksel,
     )
-    hid, dg, du, block_out, dh, dhb, do, gg_ffn = feed(h, n2, c, gn, wg, wu, wd, wo)
-    do = jnp.transpose(do, (1, 0, 2)).reshape(r, d)
-    dq, dk, dv = attend_back(halo, window, q, k, v, mk, mv, seg_q, seg_k, o, lse, do, cos, sin)
-    dn1, hb, gg_attn = project_back(halo, x, xh, dq, dk, dv, wq, wk, wv)
-
-    core = me % 2
-    pairs = [(i, i ^ 1) for i in range(g.dp)]
-    other = lambda y: lax.ppermute(y, "dp", pairs)
-
-    def cut(y):
-        z = y.reshape(y.shape[0], d // 256, 2, 128)
-        mine = lax.dynamic_index_in_dim(z, core, 2, False).reshape(y.shape[0], d // 2)
-        theirs = lax.dynamic_index_in_dim(z, 1 - core, 2, False).reshape(y.shape[0], d // 2)
-        return mine, other(theirs)
-
-    both = lambda y: (y, other(y))
-    ggt, gut, gdn = feed_grads(both(hid), both(dg), both(du), cut(n2), cut(c))
-    go, gq, gk, gv = attn_grads(halo, g.nz, both(o), cut(dhb), cut(n1), both(dq), both(dk), both(dv))
-    srcs = [ggt, gut, gdn, go, gq, gk, gv]
-    n = lambda w: (w, srcs[w].shape[2])
-    units = halves([(n(0), n(1)), (n(2),), (n(3),), (n(4), n(5)), (n(6),)])
-    gains_part = jnp.concatenate([gg_attn, gg_ffn], axis=0)
-    gout, more, o_gate, o_up, o_down, o_out, o_q, o_k, o_v = k2(g, halo, gains_part, hb, srcs, units, r)
-    grad_in = input_grad(halo, x, gn, dn1, more, dh)
+    (hid, dg, du, block_out, dh, dhb, do, gg_ffn, phid, pdg, pdu, pn, pc) = feed(g, h, n2, c, gn, wg, wu, wd, wo)
+    gout, grad_in, o_gate, o_up, o_down, o_out, o_q, o_k, o_v = back(
+        g, halo, window, seg_q, seg_k, gg_ffn, gn, hid, dg, du, phid, pdg, pdu, n2, c, pn, pc,
+        q, k, v, mk, mv, o, lse, do, dhb, n1, x, xh, dh, wq, wk, wv, cos, sin,
+    )[:9]
     return (
         block_out[None], grad_in[None], gout[0], o_q, o_k, o_v, o_out, gout[1], o_gate.T, o_up.T, o_down,
     )

time: 589 us -> 458 us (0.78)
  local copies, waits for them, and re-layouts: 87.1 us -> 13.8 us
  Pallas kernels: 485 us -> 437 us
    pallas_call x6 -> x1, Pallas kernels: 225 us -> 180 us  [back(): pl.pallas_call(functools.partial(back_kernel, g, halo, window, units), ou...]
    dynamic_slice x4 -> x0, local copies, waits for them, and re-layouts: 36.5 us -> none  [cut(): lax.dynamic_index_in_dim(z, 1 - core, 2, False).reshape(y.shape[0], d // 2)]
    ppermute x3 -> x0, local copies, waits for them, and re-layouts: 13.9 us -> none  [on_device_rows(): other = lambda y: lax.ppermute(y, 'dp', pairs)]
    pallas_call x3 -> x0, local copies, waits for them, and re-layouts: 10.2 us -> none  [feed(): pl.pallas_call(kern, grid=(nz,), in_specs=[one((r, d)), one((r, d)), one(...]
    reshape x4 -> x0, local copies, waits for them, and re-layouts: 9.31 us -> none  [the longest x3 6.96 us: cut(): z = y.reshape(y.shape[0], d // 256, 2, 128)]
    unnamed x49 -> x27, local copies, waits for them, and re-layouts: 11.9 us -> 9.49 us
  transfers between devices with their start and end apart: 11 -> 0, of which waited for: 0 -> 0; matrix products, arithmetic and copies ran while one was open for 13% -> 0% of each run, Pallas kernels for 5% -> 0%
where the time goes in v3:
time: 458 us
  Pallas kernels  437 us (95%)
  local copies, waits for them, and re-layouts  13.8 us (3%)
  other arithmetic  5.39 us (1%)
    pallas_call x1, Pallas kernels, fwd(): pl.pallas_call(functools.partial(fwd_kernel, g, cap, nq, ksel, halo, wind...  213 us
    pallas_call x1, Pallas kernels, back(): pl.pallas_call(functools.partial(back_kernel, g, halo, window, units), ou...  180 us
    pallas_call x1, Pallas kernels, feed(): pl.pallas_call(kern, grid=(nz,), in_specs=[one((r, d)), one((r, d)), one(...  44.3 us
    unnamed x27, local copies, waits for them, and re-layouts  9.49 us

profile of v3, /device:TPU:0, one launch (start us, length us, event | category | flops | bytes accessed | tf_op | source)
XLA Modules:
  0.0 457.6 jit_solution(10994447081705417523)
XLA Ops:
  1.3 0.8 reshape_squeeze.3
  2.1 0.2 convert_reduce_fusion
  2.3 0.5 multiply_add_fusion.refs_1_
  2.8 1.2 maximum_convert_fusion.refs_5_
  4.0 0.8 pad_dynamic-slice_fusion
  4.8 0.1 iota_compare_fusion
  4.9 0.1 select_reduce_fusion
  5.0 0.6 broadcast_in_dim.54.refs_0_
  5.7 0.9 copy.29.refs_2_.refs_0_
  6.5 1.9 fusion
  8.4 1.3 pad_maximum_fusion
  9.7 212.8 %forward.1 = (bf16[8,4,128,256]{3,2,1,0:T(8,128)(2,1)}, bf16[8,4,128,256]{3,2,1,0:T(8,128)(2,1)}, bf16[8,4,128,256]{3,2,1,0:T(8,128)(2,1)}, bf16[8,4,256,128]{3,...) custom-call(s32[8,8,128]{2,1,0:T(8,128)} %broadcast_in_dim.54.refs_0, ...), custom_call_target="tpu_custom_call" | custom-call | tf_op jit(solution)/shard_map/forward/pallas_call | solution.py:518
  222.5 44.3 %feed.1 = (bf16[4,704,512]{2,1,0:T(8,128)(2,1)}, bf16[4,704,512]{2,1,0:T(8,128)(2,1)}, bf16[4,704,512]{2,1,0:T(8,128)(2,1)}, f32[512,1024]{1,0:T(8,128)}, f32[51...) custom-call(f32[512,1024]{1,0:T(8,128)} %get-tuple-element.52.h_ref,, ...), custom_call_target="tpu_custom_call" | custom-call | tf_op jit(solution)/shard_map/feed/pallas_call | solution.py:621
  266.8 180.0 %backward.1 = (f32[2,128]{1,0:T(2,128)}, f32[512,1024]{1,0:T(8,128)}, f32[704,128]{1,0:T(8,128)}, f32[704,128]{1,0:T(8,128)}, f32[704,128]{1,0:T(8,128)}, /*inde...) custom-call(s32[512,1]{1,0:T(8,128)} %copy.29.refs_2_.refs_0_, ...), custom_call_target="tpu_custom_call" | custom-call | tf_op jit(solution)/shard_map/backward/pallas_call | solution.py:1041
  446.8 1.3 slice_bitcast_fusion
  448.1 3.3 copy.41
  451.4 1.3 copy.42
  452.8 0.7 copy.43
  453.4 0.7 copy.44
  454.1 0.7 copy.45
  454.7 0.7 copy.46
  455.4 0.7 copy.47
  456.1 0.7 copy.48
  456.9 0.7 copy.49
  (23 shorter events, 0.1 us)
Async XLA Ops:
  4.8 4.9 %copy-start.8 = (s32[1024]{0:T(1024)}, s32[1024]{0:T(1024)S(1)}, u32[]{:S(2)}) copy-start(s32[1024]{0:T(1024)S(1)} %pad_dynamic-slice_fusion) | copy-start | bytes 12292
  448.1 3.3 copy-start
  451.4 1.4 copy-start.7
  451.4 2.0 copy-start.6
  451.4 2.7 copy-start.5
  451.4 3.3 copy-start.4
  451.4 4.0 copy-start.3
  451.4 4.7 %copy-start.2 = (f32[704,128]{1,0:T(8,128)S(1)}, f32[704,128]{1,0:T(8,128)}, u32[]{:S(2)}) copy-start(f32[704,128]{1,0:T(8,128)} %get-tuple-element.91) | copy-start | bytes 1081348
  452.8 4.1 copy-start.1

commit v4 on v0

--- a/solution.py
+++ b/solution.py
@@ -1,16 +1,1059 @@
+import functools
+import math
+
 import jax
 import jax.numpy as jnp
+import numpy as np
 from jax import lax
+from jax.experimental import pallas as pl
+from jax.experimental.pallas import tpu as pltpu
 from jax.sharding import PartitionSpec as P
-
-HEADS = 8
+MESH = pl.DeviceIdType.MESH
+MEMB = 128
+
+
+class Grid:
+    def __init__(self, dp, tensor):
+        side = math.isqrt(dp // 2)
+        assert side * side * 2 == dp
+        self.na, self.nb, self.nc, self.nz, self.dp = side, side, 2, tensor, dp
+
+
+def coords(g):
+    me = lax.axis_index("dp")
+    t = lax.axis_index("tensor")
+    return me // (2 * g.nb), (me // 2) % g.nb, me % 2, t, me
+
+
+def send(src, dst, ssem, rsem, dp, t):
+    return pltpu.make_async_remote_copy(
+        src_ref=src, dst_ref=dst, send_sem=ssem, recv_sem=rsem, device_id=(dp, t), device_id_type=MESH
+    )
+
+
+class Copy:
+    def __init__(self, make):
+        self.make = make
+
+    def start(self):
+        self.make().start()
+
+    def wait(self):
+        self.make().wait()
+
+    def wait_send(self):
+        self.make().wait_send()
+
+    def wait_recv(self):
+        self.make().wait_recv()
+
+
+def greet(g, me, t):
+    bar = pltpu.get_barrier_semaphore()
+    for k in range(1, g.dp):
+        pl.semaphore_signal(bar, inc=1, device_id=((me + k) % g.dp, t), device_id_type=MESH)
+    for k in range(1, g.nz):
+        pl.semaphore_signal(bar, inc=1, device_id=(me, (t + k) % g.nz), device_id_type=MESH)
+    pl.semaphore_wait(bar, g.dp - 1 + g.nz - 1)
+
+
+class Gather:
+    def __init__(self, g, shard, buf, rows, b_first, lanes, sems, base):
+        self.g, self.shard, self.buf, self.rows, self.b_first, self.lanes = g, shard, buf, rows, b_first, lanes
+        self.sems, self.next = sems, base
+        self.sent = []
+
+    def at(self, dp, t=None):
+        lo, n = self.rows
+        if self.lanes:
+            width = self.shard.shape[1]
+            col = pl.ds(pl.multiple_of(dp * width, 128), width)
+            return self.buf.at[slice(None) if t is None else t, pl.ds(lo, n), col]
+        depth, width = self.shard.shape
+        row = pl.ds(pl.multiple_of(dp * depth + lo, 16), n)
+        return self.buf.at[row, slice(None) if t is None else pl.ds(pl.multiple_of(t * width, 128), width)]
+
+    def _sem(self):
+        i = self.next
+        self.next += 1
+        return i
+
+    def _push(self, src, dst, to):
+        i = self._sem()
+        m = Copy(lambda: send(src(), dst(), self.sems[0].at[i], self.sems[1].at[i], *to()))
+        m.start()
+        self.sent.append(m)
+        return m
+
+    def _slot(self, k1, k2):
+        g = self.g
+        a, b, c, t, me = coords(g)
+        if self.b_first:
+            return (((a + g.na - k2) % g.na) * g.nb + (b + g.nb - k1) % g.nb) * 2 + c
+        return (((a + g.na - k1) % g.na) * g.nb + (b + g.nb - k2) % g.nb) * 2 + c
+
+    def _sizes(self):
+        return (self.g.nb, self.g.na) if self.b_first else (self.g.na, self.g.nb)
+
+    def start_z(self):
+        g = self.g
+        lo, n = self.rows
+        src = lambda: self.shard.at[pl.ds(lo, n), :]
+
+        def here():
+            a, b, c, t, me = coords(g)
+            return self.at(me, t)
+
+        def to(k):
+            a, b, c, t, me = coords(g)
+            return me, (t + k) % g.nz
+
+        self.z = [self._push(src, here, functools.partial(to, k)) for k in range(1, g.nz)]
+        i = self._sem()
+        self.own = Copy(lambda: pltpu.make_async_copy(src(), here(), self.sems[0].at[i]))
+        self.own.start()
+
+    def _slab(self, k1, k2):
+        return lambda: self.at(self._slot(k1, k2))
+
+    def _core(self, k1, k2):
+        def to():
+            a, b, c, t, me = coords(self.g)
+            return me + 1 - 2 * c, t
+
+        self.core.append(self._push(self._slab(k1, k2), self._slab(k1, k2), to))
+
+    def start_first(self):
+        n1, n2 = self._sizes()
+        self.own.wait()
+        for m in self.z:
+            m.wait_recv()
+        self.core = []
+        to = lambda k: (self._slot(n1 - k, 0), lax.axis_index("tensor"))
+        self.first = [
+            self._push(self._slab(0, 0), self._slab(0, 0), functools.partial(to, k)) for k in range(1, n1)
+        ]
+        self._core(0, 0)
+
+    def start_second(self):
+        n1, n2 = self._sizes()
+        for m in self.first:
+            m.wait_recv()
+        to = lambda k: (self._slot(0, n2 - k), lax.axis_index("tensor"))
+        self.second = [
+            self._push(self._slab(k1, 0), self._slab(k1, 0), functools.partial(to, k))
+            for k1 in range(n1)
+            for k in range(1, n2)
+        ]
+        for k1 in range(1, n1):
+            self._core(k1, 0)
+
+    def start_core(self):
+        n1, n2 = self._sizes()
+        for m in self.second:
+            m.wait_recv()
+        for k1 in range(n1):
+            for k2 in range(1, n2):
+                self._core(k1, k2)
+
+    def finish(self):
+        for m in self.core:
+            m.wait_recv()
+        for m in self.sent:
+            m.wait_send()
+
+
+def gather_sems(g):
+    return g.nz + (g.na - 1) + g.na * (g.na - 1) + g.na * g.nb
+
+
+def plan_requests(retrieved, partner, dp_size, blocks_dev, cap):
+    wanted = retrieved.reshape(-1)
+    n = wanted.shape[0]
+    from_partner = wanted // MEMB
+    block_index = wanted % MEMB
+    owner = block_index // blocks_dev
+    local = block_index % blocks_dev
+    seq = jnp.where(from_partner == 0, lax.axis_index("dp"), partner)
+    flat = seq * blocks_dev + local
+    i = jnp.arange(n)
+    slot = jnp.sum(((owner[:, None] == owner[None, :]) & (i[None, :] < i[:, None])).astype(jnp.int32), axis=1)
+    hit = (owner[None, None, :] == jnp.arange(dp_size)[:, None, None]) & (
+        slot[None, None, :] == jnp.arange(128)[None, :, None]
+    )
+    req = jnp.sum(jnp.where(hit, flat[None, None, :], 0), axis=2)
+    return jnp.broadcast_to(req[:, None, :], (dp_size, 8, 128)).astype(jnp.int32), (owner * cap + slot).astype(jnp.int32)
+
+
 HD = 128
-QB = 512
-MEMB = 128
-
-
 EPSILON = 1e-05
 MASKED = -1e30
+F32, BF16 = jnp.float32, jnp.bfloat16
+
+
+def dot_nn(x, y):
+    return lax.dot_general(x, y, (((1,), (0,)), ((), ())), preferred_element_type=F32)
+
+
+def dot_nt(x, y):
+    return lax.dot_general(x, y, (((1,), (1,)), ((), ())), preferred_element_type=F32)
+
+
+def dot_tn(x, y):
+    return lax.dot_general(x, y, (((0,), (0,)), ((), ())), preferred_element_type=F32)
+
+
+def inv_rms(v):
+    return lax.rsqrt(jnp.mean(v * v, axis=-1, keepdims=True) + EPSILON)
+
+
+def gain_row(gains_ref, which):
+    n = gains_ref.shape[0]
+    return jnp.concatenate([gains_ref[d, which : which + 1, :] for d in range(n)], axis=1)
+
+
+def turn(v, cos, sin):
+    return v * cos + pltpu.roll(v, HD // 2, axis=1) * sin
+
+
+def lanes(ref):
+    return jnp.concatenate([ref[d, 0] for d in range(ref.shape[0])], axis=1)
+
+
+def rows(ref):
+    return jnp.concatenate([ref[d, 0] for d in range(ref.shape[0])], axis=0)
+
+
+VL = 60 * 2**20
+
+
+def full(shape, buffers=None):
+    n = len(shape)
+    kw = {} if buffers is None else dict(pipeline_mode=pl.Buffered(buffers))
+    return pl.BlockSpec(shape, lambda *i: (0,) * n, **kw)
+
+
+def allowed_of(seg_q, seg_k, q0, k0):
+    n, m = seg_q.shape[0], seg_k.shape[1]
+    qp = lax.broadcasted_iota(jnp.int32, (n, m), 0) + q0
+    kp = lax.broadcasted_iota(jnp.int32, (n, m), 1) + k0
+    return (seg_q == seg_k) & (kp <= qp)
+
+
+QT = 256
+C2 = HD**-0.5 * math.log2(math.e)
+
+
+class Scatter:
+    def __init__(self, g, src, rows, b_first, bufs, sems, out):
+        self.g, self.src, self.rows, self.b_first, self.out = g, src, rows, b_first, out
+        self.r1, self.r2, self.r3 = bufs
+        self.sems, self.next = sems, 0
+        self.sent = []
+
+    def _push(self, src, dst, to):
+        i = self.next
+        self.next += 1
+        m = Copy(lambda: send(src(), dst(), self.sems[0].at[i], self.sems[1].at[i], *to()))
+        m.start()
+        self.sent.append(m)
+        return m
+
+    def _e(self, f, s):
+        return s * self.g.nb + f if self.b_first else f * self.g.nb + s
+
+    def _mine(self):
+        a, b, c, t, me = coords(self.g)
+        f, s = (b, a) if self.b_first else (a, b)
+        n1, n2 = (self.g.nb, self.g.na) if self.b_first else (self.g.na, self.g.nb)
+        return f, s, c, t, me, n1, n2
+
+    def start_first(self):
+        n1, n2 = self._mine()[5:]
+        lo, n = self.rows
+
+        def src(k, j):
+            f = self._mine()[0]
+            return self.src.at[self._e((f + k) % n1, j), :, pl.ds(lo, n), :]
+
+        def dst(k, j):
+            return self.r1.at[k - 1, j]
+
+        def to(k):
+            f, s, c, t = self._mine()[:4]
+            return self._e((f + k) % n1, s) * 2 + c, t
+
+        bind = functools.partial
+        self.first = [
+            self._push(bind(src, k, j), bind(dst, k, j), bind(to, k)) for k in range(1, n1) for j in range(n2)
+        ]
+
+    def start_second(self):
+        f, s, c, t, me, n1, n2 = self._mine()
+        lo, n = self.rows
+        for m in self.first:
+            m.wait_recv()
+        for j in range(n2):
+            e = self._e(f, j)
+
+            @pl.loop(0, self.g.nz)
+            def _(u):
+                v = self.src[e, u, lo : lo + n, :].astype(F32)
+                for k in range(n1 - 1):
+                    v = v + self.r1[k, j, u].astype(F32)
+                self.src[e, u, lo : lo + n, :] = v.astype(BF16)
+
+        def src(k):
+            f, s = self._mine()[:2]
+            return self.src.at[self._e(f, (s + k) % n2), :, pl.ds(lo, n), :]
+
+        def dst(k):
+            return self.r2.at[k - 1]
+
+        def to(k):
+            f, s, c, t = self._mine()[:4]
+            return self._e(f, (s + k) % n2) * 2 + c, t
+
+        bind = functools.partial
+        self.second = [self._push(bind(src, k), bind(dst, k), bind(to, k)) for k in range(1, n2)]
+
+    def start_z(self):
+        f, s, c, t, me, n1, n2 = self._mine()
+        lo, n = self.rows
+        nz = self.g.nz
+        e = self._e(f, s)
+        for m in self.second:
+            m.wait_recv()
+
+        @pl.loop(0, nz)
+        def _(u):
+            v = self.src[e, u, lo : lo + n, :].astype(F32)
+            for k in range(n2 - 1):
+                v = v + self.r2[k, u].astype(F32)
+            self.src[e, u, lo : lo + n, :] = v.astype(BF16)
+
+        def src(k):
+            f, s, c, t = self._mine()[:4]
+            return self.src.at[self._e(f, s), (t + k) % nz, pl.ds(lo, n), :]
+
+        def dst(k):
+            return self.r3.at[k - 1]
+
+        def to(k):
+            t, me = self._mine()[3:5]
+            return me, (t + k) % nz
+
+        bind = functools.partial
+        self.third = [self._push(bind(src, k), bind(dst, k), bind(to, k)) for k in range(1, nz)]
+
+    def finish(self):
+        f, s, c, t, me, n1, n2 = self._mine()
+        lo, n = self.rows
+        for m in self.third:
+            m.wait_recv()
+        v = self.src[self._e(f, s), t, lo : lo + n, :].astype(F32)
+        for k in range(self.g.nz - 1):
+            v = v + self.r3[k].astype(F32)
+        self.out[pl.ds(lo, n), :] = v
+        for m in self.sent:
+            m.wait_send()
+
+
+def scatter_sems(g):
+    return (g.na - 1) * g.na + (g.na - 1) + (g.nz - 1)
+
+
+def rope_tables(halo, nz, r):
+    half = HD // 2
+    freq = 10000.0 ** (-np.arange(half, dtype=np.float64) * 2.0 / HD)
+    both = lambda p: np.concatenate([np.cos(p[:, None] * freq), np.sin(p[:, None] * freq)], axis=1).astype(np.float32)
+    n = nz + halo
+    starts = (np.arange(-(-n // 8) * 8) - halo) * float(r)
+    return both(np.arange(r, dtype=np.float64)), both(starts)
+
+
+def layer_kernel(g, cfg, *refs):
+    cap, nq, ksel, halo, window, gunits, sunits = cfg
+    refs = list(refs)
+    take = lambda n: [refs.pop(0) for _ in range(n)]
+    requests, sel, seg_q, seg_k, tab1, tab2 = take(6)
+    x, gains, mem_k, mem_v, cot = take(5)
+    shards = take(7)
+    gout = take(1)[0]
+    outs = take(7)
+    block_out, grad_in = take(2)
+    bufs = take(7)
+    wq, wk, wv, wo, wg, wu, wd = bufs
+    xh, mk, mv, rec_k, rec_v, n1, q, k, v, o, lse = take(11)
+    hid, sa, sb, dg, du, phid, pdg, pdu, do, dq, dk, dv, pdq, pdk, pdv, po, dh_o = take(17)
+    req_in, req_s, gn_v, cos_v, sin_v = take(5)
+    rbufs = [take(3) for _ in sunits]
+    rsems = [take(2) for _ in sunits]
+    pn_v, pc_v, pn1_v, pdhb_v, more = take(5)
+    gz, gs, gd, gp = take(4)
+    ss, rs, ms, qss, qrs, gss, grs, mss, mrs, zss, zrs, xss, xrs = take(13)
+    css, crs, hss, hrs, ass, ars, dss, drs = take(8)
+    a, b, core, t, me = coords(g)
+    peer = me + 1 - 2 * core
+    r, d = block_out.shape
+    rt = (halo + 1) * r
+    nz, ff, _ = hid.shape
+    dp = g.dp
+    nb, half = dp // 2, d // 2
+    kd, cols = shards[0].shape
+    blk = mk.shape[2]
+    nm, per_t = ksel * blk, cols // HD
+    heads = d // HD
+    any_ = pl.BlockSpec(memory_space=pl.ANY)
+
+    def local(src, dst, i):
+        m = pltpu.make_async_copy(src, dst, ms.at[i])
+        m.start()
+        return m
+
+    ncore = [0]
+
+    def to_peer(src, dst):
+        i = ncore[0]
+        ncore[0] += 1
+        m = send(src, dst, css.at[i], crs.at[i], peer, t)
+        m.start()
+        return m
+
+    def lane_block(ref, e, c_):
+        return ref.at[:, pl.ds(pl.multiple_of((2 * e + c_) * 128, 128), 128)]
+
+    def theirs(src, dst):
+        return [to_peer(lane_block(src, e, 1 - core), dst.at[:, pl.ds(e * 128, 128)]) for e in range(nb)]
+
+    def keep_half(src, dst):
+        for e in range(nb):
+            dst[:, e * 128 : (e + 1) * 128] = src[:, pl.ds(pl.multiple_of((2 * e + core) * 128, 128), 128)]
+
+    per = gather_sems(g)
+    gat = [Gather(g, shards[w], bufs[w], rows_, bf, lanes_, (ss, rs), i * per)
+           for i, (w, rows_, bf, lanes_) in enumerate(gunits)]
+    gof = lambda *ws: [u for u, s in zip(gat, gunits) if s[0] in ws]
+    proj, out_, gate_up, down = gof(0, 1, 2), gof(3), gof(4, 5), gof(6)
+
+    head = lambda n, lo: pl.BlockSpec((n, HD), lambda h: (0, h + lo))
+    mem = lambda lo: pl.BlockSpec((1, ksel, blk, HD), lambda h: ((h + lo) // per_t, 0, 0, (h + lo) % per_t))
+    col = lambda n: pl.BlockSpec((n, cols), lambda u: (0, u))
+    piece = pl.BlockSpec((1, ff, r), lambda u: (u, 0, 0))
+    wcol = pl.BlockSpec((d, cols), lambda u: (0, u))
+    wrow = lambda n: pl.BlockSpec((1, n, d), lambda u: (u, 0, 0))
+
+    greet(g, me, t)
+    def forward(loc, stage_k, stage_v, x_v, xh_v, n_v):
+        rq, gn = [], []
+        for i in range(1, dp):
+            to = (me + i) % dp
+            m = send(requests.at[to], req_in.at[me], qss.at[i], qrs.at[i], to, t)
+            m.start()
+            rq.append(m)
+        for i in range(1, dp):
+            to = (me + i) % dp
+            m = send(gains, gn_v.at[me], gss.at[i], grs.at[i], to, t)
+            m.start()
+            gn.append(m)
+        own_r = pltpu.make_async_copy(requests.at[me], req_in.at[me], qss.at[0])
+        own_r.start()
+        own_g = pltpu.make_async_copy(gains, gn_v.at[me], gss.at[0])
+        own_g.start()
+        load_k = local(mem_k, loc, 0)
+        for u in proj + out_:
+            u.start_z()
+        xs = []
+        for i in range(1, halo + 1):
+            m = send(x, xh.at[i - 1], xss.at[i - 1], xrs.at[i - 1], me, (t + i) % nz)
+            xs.append(m)
+
+            @pl.when(t + i < nz)
+            def _():
+                m.start()
+
+        lx = local(x, x_v, 1)
+        own_r.wait()
+        for m in rq:
+            m.wait()
+        cp = local(req_in, req_s, 2)
+        cp.wait()
+
+        def exchange(stage, rec, i, load):
+            load.wait()
+
+            @pl.loop(0, dp)
+            def _(s):
+                for j in range(cap):
+                    stage[s, j] = loc[req_s[s, 0, j]]
+
+            out = []
+            for j in range(1, dp):
+                to = (me + j) % dp
+                m = send(stage.at[to], rec.at[pl.ds(me * cap, cap)], mss.at[i, j], mrs.at[i, j], to, t)
+                m.start()
+                out.append(m)
+            own = pltpu.make_async_copy(stage.at[me], rec.at[pl.ds(me * cap, cap)], mss.at[i, 0])
+            own.start()
+            return out + [own]
+
+        ek = exchange(stage_k, rec_k, 0, load_k)
+        load_v = local(mem_v, loc, 3)
+        for u in gate_up:
+            u.start_z()
+        ev = exchange(stage_v, rec_v, 1, load_v)
+        for u in proj + out_:
+            u.start_first()
+
+        left = lax.broadcasted_iota(jnp.int32, (r, HD), 1) < HD // 2
+        c1 = tab1[...]
+        s1 = pltpu.roll(c1, HD // 2, axis=1)
+        cc, sc = jnp.where(left, c1, s1), jnp.where(left, s1, c1)
+        for j in range(halo + 1):
+            c2 = jnp.broadcast_to(tab2[pl.ds(t + j, 1), :], (r, HD))
+            s2 = pltpu.roll(c2, HD // 2, axis=1)
+            ce, se = jnp.where(left, c2, s2), jnp.where(left, s2, c2)
+            cos_v[j * r : (j + 1) * r, :] = cc * ce - sc * se
+            sin_ = sc * ce + cc * se
+            sin_v[j * r : (j + 1) * r, :] = jnp.where(left, -sin_, sin_)
+
+        own_g.wait()
+        for m in gn:
+            m.wait()
+        lx.wait()
+        gain1 = gain_row(gn_v, 0)
+        vx = x_v[...].astype(F32)
+        n_v[halo * r :, :] = (vx * inv_rms(vx) * gain1).astype(BF16)
+        for i, m in enumerate(xs):
+            lo = (halo - 1 - i) * r
+
+            @pl.when(t >= i + 1)
+            def _():
+                m.wait_recv()
+                ch = local(xh.at[i], xh_v, 4)
+                ch.wait()
+                vh = xh_v[...].astype(F32)
+                n_v[lo : lo + r, :] = (vh * inv_rms(vh) * gain1).astype(BF16)
+
+            @pl.when(t < i + 1)
+            def _():
+                n_v[lo : lo + r, :] = jnp.zeros((r, d), BF16)
+
+        cn = local(n_v, n1, 5)
+
+        def spread(moves, rec, zst, out, i):
+            for m in moves:
+                m.wait()
+            lr = local(rec, loc.at[pl.ds(0, dp * cap)], 6)
+            lr.wait()
+
+            @pl.loop(0, nq)
+            def _(s):
+                for j in range(ksel):
+                    zst[s, j] = loc[sel[s * ksel + j]]
+
+            res = []
+            for j in range(1, nz):
+                to = (t + j) % nz
+                m = send(zst.at[to], out.at[t], zss.at[i, j], zrs.at[i, j], me, to)
+                m.start()
+                res.append(m)
+            own = pltpu.make_async_copy(zst.at[t], out.at[t], zss.at[i, 0])
+            own.start()
+            return res + [own]
+
+        zk = spread(ek, rec_k, stage_k, mk, 0)
+        zv = spread(ev, rec_v, stage_v, mv, 1)
+        for u in down:
+            u.start_z()
+        for u in proj:
+            u.start_second()
+        for u in gate_up:
+            u.start_first()
+        for u in out_:
+            u.start_second()
+        for u in proj:
+            u.start_core()
+        for u in proj:
+            u.finish()
+
+        def turned(y, cs_, sn_):
+            return jnp.concatenate(
+                [turn(y[:, h * HD : (h + 1) * HD], cs_, sn_).astype(BF16) for h in range(cols // HD)], axis=1
+            )
+
+        def project(wq_ref, wk_ref, wv_ref, q_ref, k_ref, v_ref):
+            @pl.loop(0, halo + 1)
+            def _(i):
+                at = pl.ds(pl.multiple_of(i * r, r), r)
+                n = n_v[at, :]
+                k_ref[at, :] = turned(dot_nn(n, wk_ref[...]), cos_v[at, :], sin_v[at, :])
+                v_ref[at, :] = dot_nn(n, wv_ref[...]).astype(BF16)
+
+            q_ref[...] = turned(dot_nn(n_v[halo * r :, :], wq_ref[...]), cos_v[halo * r :, :], sin_v[halo * r :, :])
+
+        pltpu.emit_pipeline(project, grid=(nz,), in_specs=[wcol] * 3, out_specs=[col(r), col(rt), col(rt)])(
+            wq, wk, wv, q, k, v
+        )
+        for m in zk + zv:
+            m.wait()
+        cn.wait()
+        for i, m in enumerate(xs):
+
+            @pl.when(t + i + 1 < nz)
+            def _():
+                m.wait_send()
+
+    nblk = mem_k.shape[0]
+    pl.run_scoped(
+        forward,
+        pltpu.VMEM((nblk, blk, cols), BF16),
+        pltpu.VMEM((max(dp, nq), cap, blk, cols), BF16),
+        pltpu.VMEM((max(dp, nq), cap, blk, cols), BF16),
+        pltpu.VMEM((r, d), BF16),
+        pltpu.VMEM((r, d), BF16),
+        pltpu.VMEM((rt, d), BF16),
+    )
+
+    def attend(q_ref, k_ref, v_ref, mk_ref, mv_ref, o_ref, l_ref):
+        km = mk_ref[0].reshape(nm, HD)
+        vm = mv_ref[0].reshape(nm, HD)
+        for i in range(r // QT):
+            at = slice(i * QT, (i + 1) * QT)
+            k0 = halo * r - window + i * QT
+            ks = slice(k0, k0 + window + QT)
+            qq = q_ref[at, :]
+            ok = allowed_of(seg_q[at, :], seg_k[:, ks], halo * r + i * QT, k0)
+            sl = jnp.where(ok, dot_nt(qq, k_ref[ks, :]), MASKED)
+            sm = dot_nt(qq, km)
+            mx = jnp.maximum(jnp.max(sl, axis=1, keepdims=True), jnp.max(sm, axis=1, keepdims=True))
+            mc = mx * C2
+            el = jnp.exp2(sl * C2 - mc)
+            em = jnp.exp2(sm * C2 - mc)
+            tot = jnp.sum(el, axis=1, keepdims=True) + jnp.sum(em, axis=1, keepdims=True)
+            acc = dot_nn(el.astype(BF16), v_ref[ks, :]) + dot_nn(em.astype(BF16), vm)
+            o_ref[at, :] = (acc / tot).astype(BF16)
+            l_ref[0, at, :] = mc + jnp.log2(tot)
+
+    def run_attend(lo, n):
+        pltpu.emit_pipeline(
+            attend,
+            grid=(n,),
+            in_specs=[head(r, lo), head(rt, lo), head(rt, lo), mem(lo), mem(lo)],
+            out_specs=[head(r, lo), pl.BlockSpec((1, r, 1), lambda h: (h + lo, 0, 0))],
+        )(q, k, v, mk, mv, o, lse)
+
+    run_attend(0, heads // 2)
+    for u in gate_up:
+        u.start_second()
+    for u in down:
+        u.start_first()
+    run_attend(heads // 2, heads - heads // 2)
+    for u in out_:
+        u.start_core()
+    for u in out_:
+        u.finish()
+
+    us = [None] * len(sunits)
+
+    def rest(h_v, n2_v, c_v, n2h, ch, acc, *G):
+        for i, (w, rows_, bf) in enumerate(sunits):
+            us[i] = Scatter(g, G[w], rows_, bf, rbufs[i], rsems[i], outs[w])
+        of = lambda *ws: [u for u, s in zip(us, sunits) if s[0] in ws]
+        lc = local(cot, c_v, 0)
+        lx = local(x, n2_v, 1)
+        to_o = to_peer(o, po)
+        lx.wait()
+        h_v[...] = n2_v[...].astype(F32)
+
+        def out_proj(o_ref, w_ref):
+            h_v[...] += dot_nn(o_ref[...], w_ref[0])
+
+        pltpu.emit_pipeline(out_proj, grid=(nz,), in_specs=[col(r), wrow(cols)])(o, wo)
+        gain2 = gain_row(gn_v, 1)
+        hv = h_v[...]
+        n2_v[...] = (hv * inv_rms(hv) * gain2).astype(BF16)
+        lc.wait()
+        p_n = theirs(n2_v, pn_v) + theirs(c_v, pc_v)
+        keep_half(n2_v, n2h)
+        keep_half(c_v, ch)
+        for u in gate_up:
+            u.start_core()
+        for u in gate_up:
+            u.finish()
+
+        tile = ff // 2
+
+        def hidden(wg_ref, wu_ref, hid_ref, a_ref, b_ref):
+            @pl.loop(0, 2)
+            def _(i):
+                at = pl.ds(pl.multiple_of(i * tile, 16), tile)
+                gate = dot_nt(wg_ref[0, at, :], n2_v[...])
+                up = dot_nt(wu_ref[0, at, :], n2_v[...])
+                sig = 1.0 / (1.0 + jnp.exp(-gate))
+                act = gate * sig
+                hid_ref[0, at, :] = (act * up).astype(BF16)
+                a_ref[0, at, :] = (up * (sig * (1.0 + gate * (1.0 - sig)))).astype(BF16)
+                b_ref[0, at, :] = act.astype(BF16)
+
+        pltpu.emit_pipeline(hidden, grid=(nz,), in_specs=[wrow(ff)] * 2, out_specs=[piece] * 3)(wg, wu, hid, sa, sb)
+        p_h = to_peer(hid, phid)
+        for u in down:
+            u.start_second()
+        for m in p_n + [p_h, to_o]:
+            m.wait()
+
+        def ffn_grads(A, B, mine_v, peer_v, out):
+            def body(a_ref, b_ref):
+                u = pl.program_id(0)
+                y = (dot_nn(a_ref[0], mine_v[...]) + dot_nn(b_ref[0], peer_v[...])).astype(BF16)
+                for e in range(nb):
+                    out[e, u] = y[:, e * 128 : (e + 1) * 128]
+
+            pltpu.emit_pipeline(body, grid=(nz,), in_specs=[piece] * 2)(A, B)
+
+        ffn_grads(hid, phid, ch, pc_v, G[2])
+        for u in of(2):
+            u.start_first()
+        for u in down:
+            u.start_core()
+        for u in down:
+            u.finish()
+
+        def hidden_back(wd_ref, a_ref, b_ref, dg_ref, du_ref):
+            @pl.loop(0, 2)
+            def _(i):
+                at = pl.ds(pl.multiple_of(i * tile, 16), tile)
+                dhid = dot_nt(wd_ref[0, at, :], c_v[...])
+                dg_ref[0, at, :] = (dhid * a_ref[0, at, :].astype(F32)).astype(BF16)
+                du_ref[0, at, :] = (dhid * b_ref[0, at, :].astype(F32)).astype(BF16)
+
+        pltpu.emit_pipeline(hidden_back, grid=(nz,), in_specs=[wrow(ff), piece, piece], out_specs=[piece] * 2)(
+            wd, sa, sb, dg, du
+        )
+        p_g, p_u = to_peer(dg, pdg), to_peer(du, pdu)
+        acc[0:r, :] = jnp.zeros((r, d), F32)
+
+        def norm_grad(dg_ref, du_ref, wg_ref, wu_ref):
+            acc[0:r, :] += dot_tn(dg_ref[0], wg_ref[0]) + dot_tn(du_ref[0], wu_ref[0])
+
+        pltpu.emit_pipeline(norm_grad, grid=(nz,), in_specs=[piece, piece, wrow(ff), wrow(ff)])(dg, du, wg, wu)
+        for u in of(2):
+            u.start_second()
+        p_g.wait()
+        ffn_grads(dg, pdg, n2h, pn_v, G[0])
+        for u in of(0):
+            u.start_first()
+        p_u.wait()
+        ffn_grads(du, pdu, n2h, pn_v, G[1])
+        for u in of(1):
+            u.start_first()
+
+        def attention_back(dhb_v, dhbh, n1h, sdk, sdv, hb_v):
+            dn = acc[0:r, :]
+            hv = h_v[...]
+            iv = inv_rms(hv)
+            gp[1:2, :] = jnp.sum(dn * hv * iv, axis=0, keepdims=True)
+            gdn = dn * gain2
+            dh = c_v[...].astype(F32) + iv * gdn - hv * (iv * iv * iv * jnp.mean(hv * gdn, axis=1, keepdims=True))
+            acc[0:r, :] = dh
+            dhb_v[...] = dh.astype(BF16)
+            ld = local(acc.at[pl.ds(0, r)], dh_o, 2)
+            p_r = theirs(dhb_v, pdhb_v) + theirs(n1, pn1_v)
+            keep_half(dhb_v, dhbh)
+            ln = [local(lane_block(n1, e, core), n1h.at[:, pl.ds(e * 128, 128)], 8 + e) for e in range(nb)]
+
+            def mixed_grad(w_ref, do_ref):
+                do_ref[...] = dot_nt(dhb_v[...], w_ref[0]).astype(BF16)
+
+            pltpu.emit_pipeline(mixed_grad, grid=(nz,), in_specs=[wrow(cols)], out_specs=[col(r)])(wo, do)
+            for u in of(2):
+                u.start_z()
+
+            scale = HD**-0.5
+
+            def attend_back(q_ref, k_ref, v_ref, mk_ref, mv_ref, o_ref, l_ref, do_ref, dq_ref, dk_ref, dv_ref):
+                km = mk_ref[0].reshape(nm, HD)
+                vm = mv_ref[0].reshape(nm, HD)
+                sdk[...] = jnp.zeros_like(sdk)
+                sdv[...] = jnp.zeros_like(sdv)
+                for i in range(r // QT):
+                    at = slice(i * QT, (i + 1) * QT)
+                    k0 = halo * r - window + i * QT
+                    ks = slice(k0, k0 + window + QT)
+                    own = slice(halo * r + i * QT, halo * r + (i + 1) * QT)
+                    qq, dd = q_ref[at, :], do_ref[at, :]
+                    lse_c = l_ref[0, at, :]
+                    delta = jnp.sum(dd.astype(F32) * o_ref[at, :].astype(F32), axis=1, keepdims=True)
+                    ok = allowed_of(seg_q[at, :], seg_k[:, ks], halo * r + i * QT, k0)
+                    pm = jnp.exp2(dot_nt(qq, km) * C2 - lse_c)
+                    dsm = (pm * (dot_nt(dd, vm) - delta)).astype(BF16)
+                    plo = jnp.where(ok, jnp.exp2(dot_nt(qq, k_ref[ks, :]) * C2 - lse_c), 0.0)
+                    dsl = (plo * (dot_nt(dd, v_ref[ks, :]) - delta)).astype(BF16)
+                    dqv = (dot_nn(dsm, km) + dot_nn(dsl, k_ref[ks, :])) * scale
+                    dq_ref[at, :] = turn(dqv, cos_v[own, :], -sin_v[own, :]).astype(BF16)
+                    sdk[ks, :] += dot_tn(dsl, qq)
+                    sdv[ks, :] += dot_tn(plo.astype(BF16), dd)
+                dk_ref[...] = turn(sdk[...] * scale, cos_v[...], -sin_v[...]).astype(BF16)
+                dv_ref[...] = sdv[...].astype(BF16)
+
+            def run_back(lo, n):
+                pltpu.emit_pipeline(
+                    attend_back,
+                    grid=(n,),
+                    in_specs=[head(r, lo), head(rt, lo), head(rt, lo), mem(lo), mem(lo), head(r, lo),
+                              pl.BlockSpec((1, r, 1), lambda h: (h + lo, 0, 0)), head(r, lo)],
+                    out_specs=[head(r, lo), head(rt, lo), head(rt, lo)],
+                )(q, k, v, mk, mv, o, lse, do, dq, dk, dv)
+
+            run_back(0, heads // 2)
+            for m in p_r + ln:
+                m.wait()
+
+            def out_grads(a_ref, b_ref):
+                u = pl.program_id(0)
+                y = (dot_tn(a_ref[...], dhbh[...]) + dot_tn(b_ref[...], pdhb_v[...])).astype(BF16)
+                for e in range(nb):
+                    G[3][e, u] = y[:, e * 128 : (e + 1) * 128]
+
+            pltpu.emit_pipeline(out_grads, grid=(nz,), in_specs=[col(r)] * 2)(o, po)
+            for u in of(3):
+                u.start_first()
+            run_back(heads // 2, heads - heads // 2)
+            p_att = [to_peer(dq, pdq), to_peer(dk, pdk), to_peer(dv, pdv)]
+            for u in of(0):
+                u.start_second()
+            ld.wait()
+
+            acc[...] = jnp.zeros_like(acc)
+
+            def project_back(dq_ref, dk_ref, dv_ref, wq_ref, wk_ref, wv_ref):
+                @pl.loop(0, halo + 1)
+                def _(i):
+                    at = pl.ds(pl.multiple_of(i * r, r), r)
+                    acc[at, :] += dot_nt(dk_ref[at, :], wk_ref[...]) + dot_nt(dv_ref[at, :], wv_ref[...])
+
+                acc[halo * r :, :] += dot_nt(dq_ref[...], wq_ref[...])
+
+            pltpu.emit_pipeline(project_back, grid=(nz,), in_specs=[col(r), col(rt), col(rt)] + [wcol] * 3)(
+                dq, dk, dv, wq, wk, wv
+            )
+            hb_v[...] = acc[: halo * r, :].astype(BF16)
+            hd = []
+            for j in range(halo):
+                m = send(hb_v.at[pl.ds((halo - 1 - j) * r, r), :], more.at[j], hss.at[j], hrs.at[j], me,
+                         (t + nz - 1 - j) % nz)
+                hd.append(m)
+
+                @pl.when(t >= j + 1)
+                def _():
+                    m.start()
+
+            for u in of(1):
+                u.start_second()
+            for u in of(0):
+                u.start_z()
+            for u in of(3):
+                u.start_second()
+            for m in p_att:
+                m.wait()
+
+            own = pl.ds(halo * r, r)
+
+            def grads_of(out, p0, p1, a0, a1):
+                def body(x_ref, y_ref):
+                    u = pl.program_id(0)
+                    y = (dot_tn(a0[...], x_ref[...]) + dot_tn(a1[...], y_ref[...])).astype(BF16)
+                    for e in range(nb):
+                        out[e, u] = y[e * 128 : (e + 1) * 128, :]
+
+                n = p0.shape[0]
+                pltpu.emit_pipeline(body, grid=(nz,), in_specs=[col(n)] * 2)(p0, p1)
+
+            grads_of(G[4], dq, pdq, n1h.at[own], pn1_v.at[own])
+            grads_of(G[5], dk, pdk, n1h, pn1_v)
+            for u in of(4, 5):
+                u.start_first()
+            grads_of(G[6], dv, pdv, n1h, pn1_v)
+            for u in of(6):
+                u.start_first()
+
+            lx2 = local(x, c_v, 3)
+            lx2.wait()
+            vx = c_v[...].astype(F32)
+            gp[0:1, :] = jnp.sum(acc[halo * r :, :] * vx * inv_rms(vx), axis=0, keepdims=True)
+            for j in range(halo):
+
+                @pl.when(t >= j + 1)
+                def _():
+                    cx = local(xh.at[j], n2_v, 4)
+                    cx.wait()
+                    vh = n2_v[...].astype(F32)
+                    lo = (halo - 1 - j) * r
+                    gp[0:1, :] = gp[0:1, :] + jnp.sum(acc[lo : lo + r, :] * vh * inv_rms(vh), axis=0, keepdims=True)
+
+            zg = []
+            for i in range(1, nz):
+                m = send(gp, gz.at[i - 1], ass.at[i - 1], ars.at[i - 1], me, (t + i) % nz)
+                m.start()
+                zg.append(m)
+            for u in of(1):
+                u.start_z()
+            for u in of(4, 5):
+                u.start_second()
+
+            def feed_out(hid_ref, wd_ref):
+                h_v[...] += dot_tn(hid_ref[0], wd_ref[0])
+
+            pltpu.emit_pipeline(feed_out, grid=(nz,), in_specs=[piece, wrow(ff)])(hid, wd)
+            lo_ = local(h_v, block_out, 5)
+            for u in of(6):
+                u.start_second()
+            for u in of(3):
+                u.start_z()
+            for m in zg:
+                m.wait()
+            tot = gp[...]
+            for i in range(nz - 1):
+                tot = tot + gz[i]
+            for e in range(dp):
+                gs[e] = tot[:, e * 128 : (e + 1) * 128]
+            ds_ = []
+            for i in range(1, dp):
+                to = (me + i) % dp
+                m = send(gs.at[to], gd.at[me], dss.at[i], drs.at[i], to, t)
+                m.start()
+                ds_.append(m)
+            og = pltpu.make_async_copy(gs.at[me], gd.at[me], dss.at[0])
+            og.start()
+            for u in of(4, 5):
+                u.start_z()
+
+            lo_.wait()
+            ld2 = local(dh_o, h_v, 6)
+            for j, m in enumerate(hd):
+
+                @pl.when(t + j + 1 < nz)
+                def _():
+                    m.wait_recv()
+                    acc[halo * r :, :] = acc[halo * r :, :] + more[j].astype(F32)
+
+                @pl.when(t >= j + 1)
+                def _():
+                    m.wait_send()
+
+            ld2.wait()
+            vx = c_v[...].astype(F32)
+            iv = inv_rms(vx)
+            gdx = acc[halo * r :, :] * gain_row(gn_v, 0)
+            acc[halo * r :, :] = h_v[...] + iv * gdx - vx * (iv * iv * iv * jnp.mean(vx * gdx, axis=1, keepdims=True))
+            lg = local(acc.at[pl.ds(halo * r, r)], grad_in, 7)
+            for u in of(6):
+                u.start_z()
+            og.wait()
+            for m in ds_:
+                m.wait()
+            tot = gd[0]
+            for e in range(1, dp):
+                tot = tot + gd[e]
+            gout[...] = tot
+            for u in us:
+                u.finish()
+            lg.wait()
+
+        pl.run_scoped(
+            attention_back,
+            pltpu.VMEM((r, d), BF16),
+            pltpu.VMEM((r, half), BF16),
+            pltpu.VMEM((rt, half), BF16),
+            pltpu.VMEM((rt, HD), F32),
+            pltpu.VMEM((rt, HD), F32),
+            pltpu.VMEM((halo * r, d), BF16),
+        )
+
+    pieces = [o_.shape for o_ in outs]
+    pl.run_scoped(
+        rest,
+        pltpu.VMEM((r, d), F32),
+        pltpu.VMEM((r, d), BF16),
+        pltpu.VMEM((r, d), BF16),
+        pltpu.VMEM((r, half), BF16),
+        pltpu.VMEM((r, half), BF16),
+        pltpu.VMEM((rt, d), F32),
+        *[pltpu.VMEM((nb, nz) + tuple(p), BF16) for p in pieces],
+    )
+
+
+def run_layer(g, cap, halo, window, requests, sel, seg_q, seg_k, x, gains, mem_k, mem_v, cot, shards, nq, ksel):
+    blk, cols = mem_k.shape[1:]
+    r, d = x.shape
+    rt = (halo + 1) * r
+    nz, dp = g.nz, g.dp
+    half = d // 2
+    kd, ff = shards[0].shape[0], shards[4].shape[0]
+    heads = d // HD
+    tab1, tab2 = (jnp.asarray(v) for v in rope_tables(halo, nz, r))
+    gunits = []
+    for w, s in enumerate(shards):
+        n, lanes_ = s.shape[0], w >= 3
+        if w in (0, 4):
+            gunits.append((w, (0, n), True, lanes_))
+        elif w in (1, 5):
+            gunits.append((w, (0, n), False, lanes_))
+        else:
+            gunits.append((w, (0, n // 2), True, lanes_))
+            gunits.append((w, (n // 2, n - n // 2), False, lanes_))
+    pieces = [(ff, 128)] * 3 + [(cols, 128)] + [(kd, cols)] * 3
+    sunits = []
+    for w in (2, 0, 1, 3):
+        n = pieces[w][0]
+        sunits += [(w, (0, n // 2), True), (w, (n // 2, n - n // 2), False)]
+    sunits += [(4, (0, kd), True), (5, (0, kd), False), (6, (0, kd // 2), True), (6, (kd // 2, kd - kd // 2), False)]
+    any_ = pl.BlockSpec(memory_space=pl.ANY)
+    vm = pl.BlockSpec(memory_space=pltpu.VMEM)
+    dma = lambda *n: pltpu.SemaphoreType.DMA(n)
+    st = lambda s, dt=BF16: jax.ShapeDtypeStruct(s, dt)
+    nsem = len(gunits) * gather_sems(g)
+    hbm = (
+        [st((d, d))] * 3 + [st((nz, cols, d))] + [st((nz, ff, d))] * 3
+        + [st((halo, r, d))] + [st((nz, ksel, blk, cols))] * 2 + [st((dp * cap, blk, cols))] * 2
+        + [st((rt, d)), st((r, d)), st((rt, d)), st((rt, d)), st((r, d)), st((heads, r, 1), F32)]
+        + [st((nz, ff, r))] * 8 + [st((r, d)), st((r, d)), st((rt, d)), st((rt, d))]
+        + [st((r, d)), st((rt, d)), st((rt, d)), st((r, d)), st((r, d), F32)]
+    )
+    out_shape = [st((2, 128), F32)] + [st(p, F32) for p in pieces] + [st((r, d), F32)] * 2 + hbm
+    scratch = [pltpu.VMEM((dp, 8, 128), jnp.int32), pltpu.SMEM((dp, 8, 128), jnp.int32), pltpu.VMEM((dp, 2, 128), F32)]
+    scratch += [pltpu.VMEM((rt, HD), F32)] * 2
+    for w, (lo, n), bf in sunits:
+        cc = pieces[w][1]
+        n1_, n2_ = (g.nb, g.na) if bf else (g.na, g.nb)
+        scratch += [
+            pltpu.VMEM((n1_ - 1, n2_, nz, n, cc), BF16),
+            pltpu.VMEM((n2_ - 1, nz, n, cc), BF16),
+            pltpu.VMEM((nz - 1, n, cc), BF16),
+        ]
+    scratch += [dma(scatter_sems(g))] * (2 * len(sunits))
+    scratch += [pltpu.VMEM((r, half), BF16)] * 2 + [pltpu.VMEM((rt, half), BF16), pltpu.VMEM((r, half), BF16)]
+    scratch += [pltpu.VMEM((halo, r, d), BF16)]
+    scratch += [pltpu.VMEM((nz - 1, 2, d), F32), pltpu.VMEM((dp, 2, 128), F32), pltpu.VMEM((dp, 2, 128), F32), pltpu.VMEM((2, d), F32)]
+    ncore = 7 + 4 * (dp // 2)
+    scratch += [dma(nsem), dma(nsem), dma(8 + dp // 2), dma(dp), dma(dp), dma(dp), dma(dp), dma(2, dp), dma(2, dp)]
+    scratch += [dma(2, nz), dma(2, nz), dma(halo), dma(halo)]
+    scratch += [dma(ncore), dma(ncore), dma(halo), dma(halo), dma(nz), dma(nz), dma(dp), dma(dp)]
+    cfg = (cap, nq, ksel, halo, window, gunits, sunits)
+    return pl.pallas_call(
+        functools.partial(layer_kernel, g, cfg),
+        out_shape=out_shape,
+        in_specs=[vm, pl.BlockSpec(memory_space=pltpu.SMEM), vm, vm, vm, vm] + [any_] * (5 + len(shards)),
+        out_specs=[vm] * 8 + [any_] * (2 + len(hbm)),
+        scratch_shapes=scratch,
+        compiler_params=pltpu.CompilerParams(collective_id=0, has_side_effects=True, vmem_limit_bytes=67043328),
+        name="layer",
+    )(requests, sel, seg_q, seg_k, tab1, tab2, x, gains, mem_k, mem_v, cot, *shards)
+
+
+HEADS = 8
+QB = 512
 
 
 def normalize(field, gain_vec):
@@ -85,7 +1128,7 @@
     return lax.all_gather(local_grad, "tensor", axis=0, tiled=True)
 
 
-def on_device(
+def on_device_any(
     block_in,
     segments,
     retrieved,
@@ -317,40 +1360,56 @@
     return (block_out[None], grad_in[None]) + results
 
 
+def on_device(*args):
+    x, dp = args[0], lax.axis_size("dp")
+    side = math.isqrt(dp // 2)
+    if 2 * side * side == dp and x.shape[2] % (128 * dp) == 0:
+        return on_device_rows(*args)
+    return on_device_any(*args)
+
+
+def on_device_rows(
+    block_in, segments, retrieved, partner, memory_keys, memory_values,
+    gain_attn, w_query, w_key, w_value, w_out, gain_ffn, w_gate, w_up, w_down, cotangent,
+):
+    g = Grid(lax.axis_size("dp"), lax.axis_size("tensor"))
+    t, me = lax.axis_index("tensor"), lax.axis_index("dp")
+    x, c = block_in[0], cotangent[0]
+    r, d = x.shape
+    seq_len = segments.shape[1]
+    window = seq_len // 4
+    halo = -(-window // r)
+    nq, ksel = retrieved.shape[1:]
+    cap = max(2, -(-2 * nq * ksel // g.dp))
+    req, sel = plan_requests(retrieved[0], partner[0], g.dp, memory_keys.shape[1], cap)
+    gains = jnp.stack([gain_attn, gain_ffn]).astype(F32)
+    flat = lambda m: m.reshape((-1,) + m.shape[2:])
+    shards = [w_query, w_key, w_value, w_out, w_gate.T, w_up.T, w_down]
+    padded = jnp.concatenate([jnp.full((halo * r,), -1, jnp.int32), segments[0]])
+    seg = lax.dynamic_slice(padded, (t * r,), ((halo + 1) * r,))
+    seg_k, seg_q = seg[None, :], seg[halo * r :, None]
+    gout, o_gate, o_up, o_down, o_out, o_q, o_k, o_v, block_out, grad_in = run_layer(
+        g, cap, halo, window, req, sel, seg_q, seg_k, x, gains, flat(memory_keys), flat(memory_values), c, shards, nq, ksel
+    )[:10]
+    return (
+        block_out[None], grad_in[None], gout[0], o_q, o_k, o_v, o_out, gout[1], o_gate.T, o_up.T, o_down,
+    )
+
+
 def solution(mesh):
     return jax.shard_map(
         on_device,
         mesh=mesh,
         in_specs=(
-            P("dp", "tensor", None),
-            P("dp", None),
-            P("dp", None, None),
-            P("dp"),
-            P(None, "dp", None, "tensor"),
-            P(None, "dp", None, "tensor"),
-            P("dp"),
-            P("dp", "tensor"),
-            P("dp", "tensor"),
-            P("dp", "tensor"),
-            P("tensor", "dp"),
-            P("dp"),
-            P("dp", "tensor"),
-            P("dp", "tensor"),
-            P("tensor", "dp"),
-            P("dp", "tensor", None),
+            P("dp", "tensor", None), P("dp", None), P("dp", None, None), P("dp"),
+            P(None, "dp", None, "tensor"), P(None, "dp", None, "tensor"),
+            P("dp"), P("dp", "tensor"), P("dp", "tensor"), P("dp", "tensor"), P("tensor", "dp"),
+            P("dp"), P("dp", "tensor"), P("dp", "tensor"), P("tensor", "dp"), P("dp", "tensor", None),
         ),
         out_specs=(
-            P("dp", "tensor", None),
-            P("dp", "tensor", None),
-            P("dp"),
-            P("dp", "tensor"),
-            P("dp", "tensor"),
-            P("dp", "tensor"),
-            P("tensor", "dp"),
-            P("dp"),
-            P("dp", "tensor"),
-            P("dp", "tensor"),
-            P("tensor", "dp"),
+            P("dp", "tensor", None), P("dp", "tensor", None),
+            P("dp"), P("dp", "tensor"), P("dp", "tensor"), P("dp", "tensor"), P("tensor", "dp"),
+            P("dp"), P("dp", "tensor"), P("dp", "tensor"), P("tensor", "dp"),
         ),
         check_vma=False,
     )

time: 1340 us -> 432 us (0.32)
  waiting for transfers between devices: 604 us -> 0 us
  Pallas kernels: 0 us -> 413 us
  matrix products: 273 us -> 0 us
  blocking collectives: 176 us -> 0 us
  other arithmetic: 123 us -> 2.16 us
  local copies, waits for them, and re-layouts: 127 us -> 14.3 us
  between operations: 18.1 us -> 1.36 us
    pallas_call x0 -> x1, Pallas kernels: none -> 413 us  [run_layer(): pl.pallas_call(functools.partial(layer_kernel, g, cfg), out_shape=out_sha...]
    reduce_scatter x7 -> x0, waiting for transfers between devices: 350 us -> none  [the longest x2 153 us: return_rows(): lax.psum_scatter(summed.astype(jnp.bfloat16), 'tensor', scatter_dimension...]
    dot_general x57 -> x0, matrix products: 273 us -> none  [the longest x4 55.2 us: backward_block(): jnp.einsum('qhd,khd->hqk', grad_blk, values_both, preferred_element_type=...]
    all_gather x7 -> x0, waiting for transfers between devices: 250 us -> none  [the longest x2 135 us: all_rows(): return lax.all_gather(local_grad, 'tensor', axis=0, tiled=True)]
    all_gather x6 -> x0, blocking collectives: 143 us -> none  [the longest x1 52.9 us: on_device(): lax.all_gather(w_query, 'dp', axis=0, tiled=True)]
    convert_element_type x22 -> x1, other arithmetic: 55.9 us -> 1.24 us  [on_device_rows(): gains = jnp.stack([gain_attn, gain_ffn]).astype(F32)]
    unnamed x114 -> x27, local copies, waits for them, and re-layouts: 31.7 us -> 10.1 us
    gather x4 -> x0, local copies, waits for them, and re-layouts: 21.6 us -> none  [the longest x1 6.26 us: on_device(): picked_keys = memory_keys[received[..., 0], received[..., 1]]]
  transfers between devices with their start and end apart: 20 -> 0, of which waited for: 12 -> 0; matrix products, arithmetic and copies ran while one was open for 26% -> 0% of each run, Pallas kernels for 0% -> 0%
where the time goes in v4:
time: 432 us; the launch traced here: 431 us
  Pallas kernels  413 us (96%)
  local copies, waits for them, and re-layouts  14.3 us (3%)
    pallas_call x1, Pallas kernels, run_layer(): pl.pallas_call(functools.partial(layer_kernel, g, cfg), out_shape=out_sha...  413 us
    unnamed x27, local copies, waits for them, and re-layouts  10.1 us

profile of v4, /device:TPU:0, one launch (start us, length us, event | category | flops | bytes accessed | tf_op | source)
XLA Modules:
  0.0 430.6 jit_solution(5823718660385986400)
XLA Ops:
  1.3 0.8 reshape_squeeze.3
  2.1 0.2 convert_reduce_fusion
  2.3 0.5 multiply_add_fusion.refs_1_
  2.8 1.2 maximum_convert_fusion.refs_7_
  4.0 0.8 pad_dynamic-slice_fusion
  4.8 0.6 copy-done.8
  5.4 0.1 iota_compare_fusion
  5.5 0.1 select_reduce_fusion
  5.6 0.6 broadcast_in_dim.52.refs_0_
  6.2 0.9 copy.30.refs_2_
  7.1 412.7 %layer.1 = (f32[2,128]{1,0:T(2,128)}, f32[704,128]{1,0:T(8,128)}, f32[704,128]{1,0:T(8,128)}, f32[704,128]{1,0:T(8,128)}, f32[256,128]{1,0:T(8,128)}, /*index=5*...) custom-call(s32[8,8,128]{2,1,0:T(8,128)} %broadcast_in_dim.52.refs_0, ...), custom_call_target="tpu_custom_call" | custom-call | tf_op jit(solution)/shard_map/layer/pallas_call | solution.py:1044
  419.8 1.3 slice_bitcast_fusion
  421.1 3.3 copy.41
  424.4 0.0 copy-done
  424.4 0.0 copy-start.4
  424.4 0.0 copy-start.3
  424.4 1.3 copy.42
  425.7 0.7 copy.43
  426.4 0.7 copy.44
  427.1 0.7 copy.45
  427.7 0.7 copy.46
  428.4 0.7 copy.47
  429.1 0.7 copy.48
  429.8 0.7 copy.49
  (17 shorter events, 0.1 us)
Async XLA Ops:
  4.8 0.6 copy-start.8
  421.1 3.3 copy-start
  424.4 1.4 copy-start.7
  424.4 2.0 copy-start.6
  424.4 2.7 copy-start.5
  424.4 3.3 copy-start.4
  424.4 4.0 copy-start.3
  424.4 4.7 %copy-start.2 = (f32[704,128]{1,0:T(8,128)S(1)}, f32[704,128]{1,0:T(8,128)}, u32[]{:S(2)}) copy-start(f32[704,128]{1,0:T(8,128)} %get-tuple-element.29) | copy-start | bytes 1081348
  425.7 4.1 copy-start.1

commit v5 on v4

--- a/solution.py
+++ b/solution.py
@@ -60,8 +60,50 @@
 class Gather:
     def __init__(self, g, shard, buf, rows, b_first, lanes, sems, base):
         self.g, self.shard, self.buf, self.rows, self.b_first, self.lanes = g, shard, buf, rows, b_first, lanes
-        self.sems, self.next = sems, base
-        self.sent = []
+        self.sems, self.count, self.base = sems, 0, base
+        lo, n = rows
+        nz = g.nz
+        n1, n2 = (g.nb, g.na) if b_first else (g.na, g.nb)
+        bind = functools.partial
+        shard_rows = lambda: shard.at[pl.ds(lo, n), :]
+        tensor = lambda: lax.axis_index("tensor")
+
+        def here():
+            a, b, c, t, me = coords(g)
+            return self.at(me, t)
+
+        def passed(k):
+            a, b, c, t, me = coords(g)
+            return self.at(me, (t + nz - 2 * k) % nz)
+
+        def far(k):
+            a, b, c, t, me = coords(g)
+            return me, (t + 2 * k) % nz
+
+        def pair():
+            a, b, c, t, me = coords(g)
+            return me, t + 1 - 2 * (t % 2)
+
+        def other_core():
+            a, b, c, t, me = coords(g)
+            return me + 1 - 2 * c, t
+
+        slab = lambda k1, k2: bind(lambda k1, k2: self.at(self._slot(k1, k2)), k1, k2)
+        to1 = lambda k: (self._slot(n1 - k, 0), tensor())
+        to2 = lambda k: (self._slot(0, n2 - k), tensor())
+        self.far = [self._copy(shard_rows, here, bind(far, k)) for k in range(1, nz // 2)]
+        self.near = [self._copy(shard_rows, here, pair)]
+        self.relayed = [self._copy(bind(passed, k), bind(passed, k), pair) for k in range(1, nz // 2)]
+        i = self._sem()
+        self.own = Copy(lambda: pltpu.make_async_copy(shard_rows(), here(), sems[0].at[i]))
+        self.first = [self._copy(slab(0, 0), slab(0, 0), bind(to1, k)) for k in range(1, n1)]
+        self.second = [
+            self._copy(slab(k1, 0), slab(k1, 0), bind(to2, k)) for k1 in range(n1) for k in range(1, n2)
+        ]
+        core = lambda k1, k2: self._copy(slab(k1, k2), slab(k1, k2), other_core)
+        self.core0 = [core(0, 0)]
+        self.core1 = [core(k1, 0) for k1 in range(1, n1)]
+        self.core2 = [core(k1, k2) for k1 in range(n1) for k2 in range(1, n2)]
 
     def at(self, dp, t=None):
         lo, n = self.rows
@@ -74,16 +116,13 @@
         return self.buf.at[row, slice(None) if t is None else pl.ds(pl.multiple_of(t * width, 128), width)]
 
     def _sem(self):
-        i = self.next
-        self.next += 1
+        i = self.base + self.count
+        self.count += 1
         return i
 
-    def _push(self, src, dst, to):
+    def _copy(self, src, dst, to):
         i = self._sem()
-        m = Copy(lambda: send(src(), dst(), self.sems[0].at[i], self.sems[1].at[i], *to()))
-        m.start()
-        self.sent.append(m)
-        return m
+        return Copy(lambda: send(src(), dst(), self.sems[0].at[i], self.sems[1].at[i], *to()))
 
     def _slot(self, k1, k2):
         g = self.g
@@ -92,74 +131,39 @@
             return (((a + g.na - k2) % g.na) * g.nb + (b + g.nb - k1) % g.nb) * 2 + c
         return (((a + g.na - k1) % g.na) * g.nb + (b + g.nb - k2) % g.nb) * 2 + c
 
-    def _sizes(self):
-        return (self.g.nb, self.g.na) if self.b_first else (self.g.na, self.g.nb)
-
     def start_z(self):
-        g = self.g
-        lo, n = self.rows
-        src = lambda: self.shard.at[pl.ds(lo, n), :]
-
-        def here():
-            a, b, c, t, me = coords(g)
-            return self.at(me, t)
-
-        def to(k):
-            a, b, c, t, me = coords(g)
-            return me, (t + k) % g.nz
-
-        self.z = [self._push(src, here, functools.partial(to, k)) for k in range(1, g.nz)]
-        i = self._sem()
-        self.own = Copy(lambda: pltpu.make_async_copy(src(), here(), self.sems[0].at[i]))
-        self.own.start()
-
-    def _slab(self, k1, k2):
-        return lambda: self.at(self._slot(k1, k2))
-
-    def _core(self, k1, k2):
-        def to():
-            a, b, c, t, me = coords(self.g)
-            return me + 1 - 2 * c, t
-
-        self.core.append(self._push(self._slab(k1, k2), self._slab(k1, k2), to))
+        for m in self.far + self.near + [self.own]:
+            m.start()
+
+    def relay_z(self):
+        for m, n in zip(self.far, self.relayed):
+            m.wait_recv()
+            n.start()
 
     def start_first(self):
-        n1, n2 = self._sizes()
         self.own.wait()
-        for m in self.z:
+        for m in self.near + self.relayed:
             m.wait_recv()
-        self.core = []
-        to = lambda k: (self._slot(n1 - k, 0), lax.axis_index("tensor"))
-        self.first = [
-            self._push(self._slab(0, 0), self._slab(0, 0), functools.partial(to, k)) for k in range(1, n1)
-        ]
-        self._core(0, 0)
+        for m in self.first + self.core0:
+            m.start()
 
     def start_second(self):
-        n1, n2 = self._sizes()
         for m in self.first:
             m.wait_recv()
-        to = lambda k: (self._slot(0, n2 - k), lax.axis_index("tensor"))
-        self.second = [
-            self._push(self._slab(k1, 0), self._slab(k1, 0), functools.partial(to, k))
-            for k1 in range(n1)
-            for k in range(1, n2)
-        ]
-        for k1 in range(1, n1):
-            self._core(k1, 0)
+        for m in self.second + self.core1:
+            m.start()
 
     def start_core(self):
-        n1, n2 = self._sizes()
         for m in self.second:
             m.wait_recv()
-        for k1 in range(n1):
-            for k2 in range(1, n2):
-                self._core(k1, k2)
+        for m in self.core2:
+            m.start()
 
     def finish(self):
-        for m in self.core:
+        core = self.core0 + self.core1 + self.core2
+        for m in core:
             m.wait_recv()
-        for m in self.sent:
+        for m in self.far + self.near + self.relayed + self.first + self.second + core:
             m.wait_send()
 
 
@@ -248,16 +252,59 @@
     def __init__(self, g, src, rows, b_first, bufs, sems, out):
         self.g, self.src, self.rows, self.b_first, self.out = g, src, rows, b_first, out
         self.r1, self.r2, self.r3 = bufs
-        self.sems, self.next = sems, 0
-        self.sent = []
-
-    def _push(self, src, dst, to):
-        i = self.next
-        self.next += 1
-        m = Copy(lambda: send(src(), dst(), self.sems[0].at[i], self.sems[1].at[i], *to()))
-        m.start()
-        self.sent.append(m)
-        return m
+        self.sems, self.count = sems, 0
+        n1, n2 = self._mine()[5:]
+        nz = g.nz
+        lo, n = rows
+        bind = functools.partial
+        at = lambda e, t: src.at[e, t, pl.ds(lo, n), :]
+
+        def src1(k, j):
+            f = self._mine()[0]
+            return at(self._e((f + k) % n1, j), slice(None))
+
+        def to1(k):
+            f, s, c, t = self._mine()[:4]
+            return self._e((f + k) % n1, s) * 2 + c, t
+
+        def src2(k):
+            f, s = self._mine()[:2]
+            return at(self._e(f, (s + k) % n2), slice(None))
+
+        def to2(k):
+            f, s, c, t = self._mine()[:4]
+            return self._e(f, (s + k) % n2) * 2 + c, t
+
+        def src_near(k):
+            f, s, c, t = self._mine()[:4]
+            return at(self._e(f, s), (t + 1 - 2 * (t % 2) + 2 * k) % nz)
+
+        def to_near():
+            t, me = self._mine()[3:5]
+            return me, t + 1 - 2 * (t % 2)
+
+        def src_far(k):
+            f, s, c, t = self._mine()[:4]
+            return at(self._e(f, s), (t + 2 * k) % nz)
+
+        def to_far(k):
+            t, me = self._mine()[3:5]
+            return me, (t + 2 * k) % nz
+
+        land = lambda ref, *i: bind(lambda ref, i: ref.at[i], ref, i)
+        self.first = [
+            self._copy(bind(src1, k, j), land(self.r1, k - 1, j), bind(to1, k)) for k in range(1, n1) for j in range(n2)
+        ]
+        self.second = [self._copy(bind(src2, k), land(self.r2, k - 1), bind(to2, k)) for k in range(1, n2)]
+        self.near = [self._copy(bind(src_near, k), land(self.r3, k), to_near) for k in range(nz // 2)]
+        self.far = [
+            self._copy(bind(src_far, k), land(self.r3, nz // 2 + k - 1), bind(to_far, k)) for k in range(1, nz // 2)
+        ]
+
+    def _copy(self, src, dst, to):
+        i = self.count
+        self.count += 1
+        return Copy(lambda: send(src(), dst(), self.sems[0].at[i], self.sems[1].at[i], *to()))
 
     def _e(self, f, s):
         return s * self.g.nb + f if self.b_first else f * self.g.nb + s
@@ -268,99 +315,69 @@
         n1, n2 = (self.g.nb, self.g.na) if self.b_first else (self.g.na, self.g.nb)
         return f, s, c, t, me, n1, n2
 
+    def _add(self, e, u, more):
+        lo, n = self.rows
+        v = self.src[e, u, lo : lo + n, :].astype(F32)
+        for m in more:
+            v = v + m.astype(F32)
+        self.src[e, u, lo : lo + n, :] = v.astype(BF16)
+
     def start_first(self):
-        n1, n2 = self._mine()[5:]
-        lo, n = self.rows
-
-        def src(k, j):
-            f = self._mine()[0]
-            return self.src.at[self._e((f + k) % n1, j), :, pl.ds(lo, n), :]
-
-        def dst(k, j):
-            return self.r1.at[k - 1, j]
-
-        def to(k):
-            f, s, c, t = self._mine()[:4]
-            return self._e((f + k) % n1, s) * 2 + c, t
-
-        bind = functools.partial
-        self.first = [
-            self._push(bind(src, k, j), bind(dst, k, j), bind(to, k)) for k in range(1, n1) for j in range(n2)
-        ]
+        for m in self.first:
+            m.start()
 
     def start_second(self):
         f, s, c, t, me, n1, n2 = self._mine()
-        lo, n = self.rows
         for m in self.first:
             m.wait_recv()
         for j in range(n2):
-            e = self._e(f, j)
 
             @pl.loop(0, self.g.nz)
             def _(u):
-                v = self.src[e, u, lo : lo + n, :].astype(F32)
-                for k in range(n1 - 1):
-                    v = v + self.r1[k, j, u].astype(F32)
-                self.src[e, u, lo : lo + n, :] = v.astype(BF16)
-
-        def src(k):
-            f, s = self._mine()[:2]
-            return self.src.at[self._e(f, (s + k) % n2), :, pl.ds(lo, n), :]
-
-        def dst(k):
-            return self.r2.at[k - 1]
-
-        def to(k):
-            f, s, c, t = self._mine()[:4]
-            return self._e(f, (s + k) % n2) * 2 + c, t
-
-        bind = functools.partial
-        self.second = [self._push(bind(src, k), bind(dst, k), bind(to, k)) for k in range(1, n2)]
+                self._add(self._e(f, j), u, [self.r1[k, j, u] for k in range(n1 - 1)])
+
+        for m in self.second:
+            m.start()
 
     def start_z(self):
         f, s, c, t, me, n1, n2 = self._mine()
-        lo, n = self.rows
-        nz = self.g.nz
-        e = self._e(f, s)
         for m in self.second:
             m.wait_recv()
 
-        @pl.loop(0, nz)
+        @pl.loop(0, self.g.nz)
         def _(u):
-            v = self.src[e, u, lo : lo + n, :].astype(F32)
-            for k in range(n2 - 1):
-                v = v + self.r2[k, u].astype(F32)
-            self.src[e, u, lo : lo + n, :] = v.astype(BF16)
-
-        def src(k):
-            f, s, c, t = self._mine()[:4]
-            return self.src.at[self._e(f, s), (t + k) % nz, pl.ds(lo, n), :]
-
-        def dst(k):
-            return self.r3.at[k - 1]
-
-        def to(k):
-            t, me = self._mine()[3:5]
-            return me, (t + k) % nz
-
-        bind = functools.partial
-        self.third = [self._push(bind(src, k), bind(dst, k), bind(to, k)) for k in range(1, nz)]
+            self._add(self._e(f, s), u, [self.r2[k, u] for k in range(n2 - 1)])
+
+        for m in self.near:
+            m.start()
+
+    def relay_z(self):
+        f, s, c, t, me, n1, n2 = self._mine()
+        for k, m in enumerate(self.near):
+            m.wait_recv()
+            self._add(self._e(f, s), (t + 2 * k) % self.g.nz, [self.r3[k]])
+        for m in self.far:
+            m.start()
 
     def finish(self):
         f, s, c, t, me, n1, n2 = self._mine()
         lo, n = self.rows
-        for m in self.third:
+        half = self.g.nz // 2
+        for m in self.far:
             m.wait_recv()
         v = self.src[self._e(f, s), t, lo : lo + n, :].astype(F32)
-        for k in range(self.g.nz - 1):
-            v = v + self.r3[k].astype(F32)
+        for k in range(half - 1):
+            v = v + self.r3[half + k].astype(F32)
         self.out[pl.ds(lo, n), :] = v
-        for m in self.sent:
+        for m in self.first + self.second + self.near + self.far:
             m.wait_send()
 
 
 def scatter_sems(g):
     return (g.na - 1) * g.na + (g.na - 1) + (g.nz - 1)
+
+
+POLL = dict(attend=6, back_down=2, back_gate=5)
 
 
 def rope_tables(halo, nz, r):
@@ -385,14 +402,14 @@
     bufs = take(7)
     wq, wk, wv, wo, wg, wu, wd = bufs
     xh, mk, mv, rec_k, rec_v, n1, q, k, v, o, lse = take(11)
-    hid, sa, sb, dg, du, phid, pdg, pdu, do, dq, dk, dv, pdq, pdk, pdv, po, dh_o = take(17)
+    hid, phid, pdg, pdu, do, dq, dk, dv, pdq, pdk, pdv, po, dh_o = take(13)
     req_in, req_s, gn_v, cos_v, sin_v = take(5)
     rbufs = [take(3) for _ in sunits]
     rsems = [take(2) for _ in sunits]
     pn_v, pc_v, pn1_v, pdhb_v, more = take(5)
     gz, gs, gd, gp = take(4)
     ss, rs, ms, qss, qrs, gss, grs, mss, mrs, zss, zrs, xss, xrs = take(13)
-    css, crs, hss, hrs, ass, ars, dss, drs = take(8)
+    css, crs, hss, hrs, ass, ars, dss, drs, fss, frs, fls = take(11)
     a, b, core, t, me = coords(g)
     peer = me + 1 - 2 * core
     r, d = block_out.shape
@@ -436,33 +453,49 @@
     gof = lambda *ws: [u for u, s in zip(gat, gunits) if s[0] in ws]
     proj, out_, gate_up, down = gof(0, 1, 2), gof(3), gof(4, 5), gof(6)
 
-    head = lambda n, lo: pl.BlockSpec((n, HD), lambda h: (0, h + lo))
-    mem = lambda lo: pl.BlockSpec((1, ksel, blk, HD), lambda h: ((h + lo) // per_t, 0, 0, (h + lo) % per_t))
+    def piped(body, n, in_specs, out_specs=(), polls=()):
+        def step(*blocks):
+            body(*blocks)
+            for at, fns in polls:
+
+                @pl.when(pl.program_id(0) == at)
+                def _():
+                    for fn in fns:
+                        fn()
+
+        return pltpu.emit_pipeline(step, grid=(n,), in_specs=in_specs, out_specs=out_specs)
+
+    every = lambda units, *names: [getattr(u, name) for name in names for u in units]
+
+    head = lambda n: pl.BlockSpec((n, HD), lambda h: (0, h))
+    mem = pl.BlockSpec((1, ksel, blk, HD), lambda h: (h // per_t, 0, 0, h % per_t))
+    row_stat = pl.BlockSpec((1, r, 1), lambda h: (h, 0, 0))
     col = lambda n: pl.BlockSpec((n, cols), lambda u: (0, u))
     piece = pl.BlockSpec((1, ff, r), lambda u: (u, 0, 0))
     wcol = pl.BlockSpec((d, cols), lambda u: (0, u))
     wrow = lambda n: pl.BlockSpec((1, n, d), lambda u: (u, 0, 0))
 
-    greet(g, me, t)
     def forward(loc, stage_k, stage_v, x_v, xh_v, n_v):
+        load_k = local(mem_k, loc, 0)
+        lx = local(x, x_v, 1)
+        greet(g, me, t)
         rq, gn = [], []
         for i in range(1, dp):
             to = (me + i) % dp
             m = send(requests.at[to], req_in.at[me], qss.at[i], qrs.at[i], to, t)
             m.start()
             rq.append(m)
+        own_r = pltpu.make_async_copy(requests.at[me], req_in.at[me], qss.at[0])
+        own_r.start()
+        for u in proj + out_:
+            u.start_z()
         for i in range(1, dp):
             to = (me + i) % dp
             m = send(gains, gn_v.at[me], gss.at[i], grs.at[i], to, t)
             m.start()
             gn.append(m)
-        own_r = pltpu.make_async_copy(requests.at[me], req_in.at[me], qss.at[0])
-        own_r.start()
         own_g = pltpu.make_async_copy(gains, gn_v.at[me], gss.at[0])
         own_g.start()
-        load_k = local(mem_k, loc, 0)
-        for u in proj + out_:
-            u.start_z()
         xs = []
         for i in range(1, halo + 1):
             m = send(x, xh.at[i - 1], xss.at[i - 1], xrs.at[i - 1], me, (t + i) % nz)
@@ -472,38 +505,53 @@
             def _():
                 m.start()
 
-        lx = local(x, x_v, 1)
         own_r.wait()
         for m in rq:
             m.wait()
         cp = local(req_in, req_s, 2)
         cp.wait()
+        parts = cols // 128
+        lane = lambda p: pl.ds(p * 128, 128)
+
+        def pick(stage, to):
+            for j in range(cap):
+                stage[to, j] = loc[req_s[to, 0, j]]
 
         def exchange(stage, rec, i, load):
             load.wait()
-
-            @pl.loop(0, dp)
-            def _(s):
-                for j in range(cap):
-                    stage[s, j] = loc[req_s[s, 0, j]]
-
-            out = []
+            out = [[] for _ in range(parts)]
+            mine = pl.ds(me * cap, cap)
+
+            def go(p, j):
+                to = (me + j) % dp
+                m = send(stage.at[to, :, :, lane(p)], rec.at[mine, :, lane(p)], mss.at[i, p, j], mrs.at[i, p, j], to, t)
+                m.start()
+                out[p].append(m)
+
             for j in range(1, dp):
-                to = (me + j) % dp
-                m = send(stage.at[to], rec.at[pl.ds(me * cap, cap)], mss.at[i, j], mrs.at[i, j], to, t)
-                m.start()
-                out.append(m)
-            own = pltpu.make_async_copy(stage.at[me], rec.at[pl.ds(me * cap, cap)], mss.at[i, 0])
-            own.start()
-            return out + [own]
+                pick(stage, (me + j) % dp)
+                go(0, j)
+            for p in range(1, parts):
+                for j in range(1, dp):
+                    go(p, j)
+            pick(stage, me)
+            for p in range(parts):
+                own = pltpu.make_async_copy(stage.at[me, :, :, lane(p)], rec.at[mine, :, lane(p)], mss.at[i, p, 0])
+                own.start()
+                out[p].append(own)
+            return out
 
         ek = exchange(stage_k, rec_k, 0, load_k)
         load_v = local(mem_v, loc, 3)
         for u in gate_up:
             u.start_z()
+        for u in proj + out_:
+            u.relay_z()
         ev = exchange(stage_v, rec_v, 1, load_v)
         for u in proj + out_:
             u.start_first()
+        for u in gate_up:
+            u.relay_z()
 
         left = lax.broadcasted_iota(jnp.int32, (r, HD), 1) < HD // 2
         c1 = tab1[...]
@@ -541,37 +589,40 @@
 
         cn = local(n_v, n1, 5)
 
-        def spread(moves, rec, zst, out, i):
-            for m in moves:
+        def spread(moves, rec, zst, out, i, p):
+            for m in moves[p]:
                 m.wait()
-            lr = local(rec, loc.at[pl.ds(0, dp * cap)], 6)
+            lr = local(rec.at[:, :, lane(p)], loc.at[pl.ds(0, dp * cap), :, lane(p)], 6)
             lr.wait()
 
             @pl.loop(0, nq)
             def _(s):
                 for j in range(ksel):
-                    zst[s, j] = loc[sel[s * ksel + j]]
+                    zst[s, j, :, lane(p)] = loc[sel[s * ksel + j], :, lane(p)]
 
             res = []
             for j in range(1, nz):
                 to = (t + j) % nz
-                m = send(zst.at[to], out.at[t], zss.at[i, j], zrs.at[i, j], me, to)
+                m = send(zst.at[to, :, :, lane(p)], out.at[t, :, :, lane(p)], zss.at[i, p, j], zrs.at[i, p, j], me, to)
                 m.start()
                 res.append(m)
-            own = pltpu.make_async_copy(zst.at[t], out.at[t], zss.at[i, 0])
+            own = pltpu.make_async_copy(zst.at[t, :, :, lane(p)], out.at[t, :, :, lane(p)], zss.at[i, p, 0])
             own.start()
             return res + [own]
 
-        zk = spread(ek, rec_k, stage_k, mk, 0)
-        zv = spread(ev, rec_v, stage_v, mv, 1)
+        zk, zv = [], []
+        for p in range(parts):
+            zk += spread(ek, rec_k, stage_k, mk, 0, p)
+        for p in range(parts):
+            zv += spread(ev, rec_v, stage_v, mv, 1, p)
         for u in down:
             u.start_z()
         for u in proj:
             u.start_second()
+        for u in out_:
+            u.start_second()
         for u in gate_up:
             u.start_first()
-        for u in out_:
-            u.start_second()
         for u in proj:
             u.start_core()
         for u in proj:
@@ -592,9 +643,11 @@
 
             q_ref[...] = turned(dot_nn(n_v[halo * r :, :], wq_ref[...]), cos_v[halo * r :, :], sin_v[halo * r :, :])
 
-        pltpu.emit_pipeline(project, grid=(nz,), in_specs=[wcol] * 3, out_specs=[col(r), col(rt), col(rt)])(
-            wq, wk, wv, q, k, v
-        )
+        piped(project, nz, [wcol] * 3, [col(r), col(rt), col(rt)])(wq, wk, wv, q, k, v)
+        for u in out_:
+            u.start_core()
+        for u in down:
+            u.relay_z()
         for m in zk + zv:
             m.wait()
         cn.wait()
@@ -635,31 +688,29 @@
             o_ref[at, :] = (acc / tot).astype(BF16)
             l_ref[0, at, :] = mc + jnp.log2(tot)
 
-    def run_attend(lo, n):
-        pltpu.emit_pipeline(
-            attend,
-            grid=(n,),
-            in_specs=[head(r, lo), head(rt, lo), head(rt, lo), mem(lo), mem(lo)],
-            out_specs=[head(r, lo), pl.BlockSpec((1, r, 1), lambda h: (h + lo, 0, 0))],
-        )(q, k, v, mk, mv, o, lse)
-
-    run_attend(0, heads // 2)
-    for u in gate_up:
-        u.start_second()
-    for u in down:
-        u.start_first()
-    run_attend(heads // 2, heads - heads // 2)
-    for u in out_:
-        u.start_core()
+    piped(
+        attend,
+        heads,
+        [head(r), head(rt), head(rt), mem, mem],
+        [head(r), row_stat],
+        [(POLL["attend"], every(gate_up, "start_second") + every(down, "start_first"))],
+    )(q, k, v, mk, mv, o, lse)
     for u in out_:
         u.finish()
 
-    us = [None] * len(sunits)
-
-    def rest(h_v, n2_v, c_v, n2h, ch, acc, *G):
+    sof = lambda us, *ws: [u for u in us if u.which in ws]
+
+    def units(G):
+        res = []
         for i, (w, rows_, bf) in enumerate(sunits):
-            us[i] = Scatter(g, G[w], rows_, bf, rbufs[i], rsems[i], outs[w])
-        of = lambda *ws: [u for u, s in zip(us, sunits) if s[0] in ws]
+            if w in G:
+                u = Scatter(g, G[w], rows_, bf, rbufs[i], rsems[i], outs[w])
+                u.which = w
+                res.append(u)
+        return res
+
+    def rest(h_v, n2_v, c_v, n2h, ch, acc, *gf):
+        fu = units(dict(enumerate(gf)))
         lc = local(cot, c_v, 0)
         lx = local(x, n2_v, 1)
         to_o = to_peer(o, po)
@@ -669,7 +720,7 @@
         def out_proj(o_ref, w_ref):
             h_v[...] += dot_nn(o_ref[...], w_ref[0])
 
-        pltpu.emit_pipeline(out_proj, grid=(nz,), in_specs=[col(r), wrow(cols)])(o, wo)
+        piped(out_proj, nz, [col(r), wrow(cols)])(o, wo)
         gain2 = gain_row(gn_v, 1)
         hv = h_v[...]
         n2_v[...] = (hv * inv_rms(hv) * gain2).astype(BF16)
@@ -682,74 +733,88 @@
         for u in gate_up:
             u.finish()
 
-        tile = ff // 2
-
-        def hidden(wg_ref, wu_ref, hid_ref, a_ref, b_ref):
-            @pl.loop(0, 2)
-            def _(i):
-                at = pl.ds(pl.multiple_of(i * tile, 16), tile)
-                gate = dot_nt(wg_ref[0, at, :], n2_v[...])
-                up = dot_nt(wu_ref[0, at, :], n2_v[...])
-                sig = 1.0 / (1.0 + jnp.exp(-gate))
-                act = gate * sig
-                hid_ref[0, at, :] = (act * up).astype(BF16)
-                a_ref[0, at, :] = (up * (sig * (1.0 + gate * (1.0 - sig)))).astype(BF16)
-                b_ref[0, at, :] = act.astype(BF16)
-
-        pltpu.emit_pipeline(hidden, grid=(nz,), in_specs=[wrow(ff)] * 2, out_specs=[piece] * 3)(wg, wu, hid, sa, sb)
-        p_h = to_peer(hid, phid)
-        for u in down:
-            u.start_second()
-        for m in p_n + [p_h, to_o]:
-            m.wait()
-
-        def ffn_grads(A, B, mine_v, peer_v, out):
-            def body(a_ref, b_ref):
+        def feed_forward(hid_v, a_v, b_v):
+            tile = ff // 2
+            give = lambda src, dst, i, u: send(src.at[u], dst.at[u], fss.at[i, u], frs.at[i, u], peer, t)
+            keep = lambda u: pltpu.make_async_copy(hid_v.at[u], hid.at[u], fls.at[u])
+
+            def hidden(wg_ref, wu_ref):
                 u = pl.program_id(0)
-                y = (dot_nn(a_ref[0], mine_v[...]) + dot_nn(b_ref[0], peer_v[...])).astype(BF16)
-                for e in range(nb):
-                    out[e, u] = y[:, e * 128 : (e + 1) * 128]
-
-            pltpu.emit_pipeline(body, grid=(nz,), in_specs=[piece] * 2)(A, B)
-
-        ffn_grads(hid, phid, ch, pc_v, G[2])
-        for u in of(2):
-            u.start_first()
-        for u in down:
-            u.start_core()
-        for u in down:
-            u.finish()
-
-        def hidden_back(wd_ref, a_ref, b_ref, dg_ref, du_ref):
-            @pl.loop(0, 2)
-            def _(i):
-                at = pl.ds(pl.multiple_of(i * tile, 16), tile)
-                dhid = dot_nt(wd_ref[0, at, :], c_v[...])
-                dg_ref[0, at, :] = (dhid * a_ref[0, at, :].astype(F32)).astype(BF16)
-                du_ref[0, at, :] = (dhid * b_ref[0, at, :].astype(F32)).astype(BF16)
-
-        pltpu.emit_pipeline(hidden_back, grid=(nz,), in_specs=[wrow(ff), piece, piece], out_specs=[piece] * 2)(
-            wd, sa, sb, dg, du
-        )
-        p_g, p_u = to_peer(dg, pdg), to_peer(du, pdu)
-        acc[0:r, :] = jnp.zeros((r, d), F32)
-
-        def norm_grad(dg_ref, du_ref, wg_ref, wu_ref):
-            acc[0:r, :] += dot_tn(dg_ref[0], wg_ref[0]) + dot_tn(du_ref[0], wu_ref[0])
-
-        pltpu.emit_pipeline(norm_grad, grid=(nz,), in_specs=[piece, piece, wrow(ff), wrow(ff)])(dg, du, wg, wu)
-        for u in of(2):
-            u.start_second()
-        p_g.wait()
-        ffn_grads(dg, pdg, n2h, pn_v, G[0])
-        for u in of(0):
-            u.start_first()
-        p_u.wait()
-        ffn_grads(du, pdu, n2h, pn_v, G[1])
-        for u in of(1):
-            u.start_first()
-
-        def attention_back(dhb_v, dhbh, n1h, sdk, sdv, hb_v):
+
+                @pl.loop(0, 2)
+                def _(i):
+                    at = pl.ds(pl.multiple_of(i * tile, 16), tile)
+                    gate = dot_nt(wg_ref[0, at, :], n2_v[...])
+                    up = dot_nt(wu_ref[0, at, :], n2_v[...])
+                    sig = 1.0 / (1.0 + jnp.exp(-gate))
+                    act = gate * sig
+                    hid_v[u, at, :] = (act * up).astype(BF16)
+                    a_v[u, at, :] = (up * (sig * (1.0 + gate * (1.0 - sig)))).astype(BF16)
+                    b_v[u, at, :] = act.astype(BF16)
+
+                give(hid_v, phid, 0, u).start()
+                keep(u).start()
+
+            piped(hidden, nz, [wrow(ff)] * 2)(wg, wu)
+            for u in down:
+                u.start_second()
+            for m in p_n:
+                m.wait()
+
+            def ffn_grads(mine_t, B, i, mine_v, peer_v, out):
+                for u in range(nz):
+                    give(mine_t, B, i, u).wait()
+
+                def body(b_ref):
+                    u = pl.program_id(0)
+                    y = (dot_nn(mine_t[u], mine_v[...]) + dot_nn(b_ref[0], peer_v[...])).astype(BF16)
+                    for e in range(nb):
+                        out[e, u] = y[:, e * 128 : (e + 1) * 128]
+
+                piped(body, nz, [piece])(B)
+
+            ffn_grads(hid_v, phid, 0, ch, pc_v, gf[2])
+            for u in sof(fu, 2):
+                u.start_first()
+            for u in down:
+                u.start_core()
+            for u in down:
+                u.finish()
+            acc[0:r, :] = jnp.zeros((r, d), F32)
+
+            def hidden_back(wd_ref, wg_ref, wu_ref):
+                u = pl.program_id(0)
+
+                @pl.loop(0, 2)
+                def _(i):
+                    at = pl.ds(pl.multiple_of(i * tile, 16), tile)
+                    dhid = dot_nt(wd_ref[0, at, :], c_v[...])
+                    a_v[u, at, :] = (dhid * a_v[u, at, :].astype(F32)).astype(BF16)
+                    b_v[u, at, :] = (dhid * b_v[u, at, :].astype(F32)).astype(BF16)
+
+                give(a_v, pdg, 1, u).start()
+                give(b_v, pdu, 2, u).start()
+                acc[0:r, :] += dot_tn(a_v[u], wg_ref[0]) + dot_tn(b_v[u], wu_ref[0])
+
+            piped(hidden_back, nz, [wrow(ff)] * 3)(wd, wg, wu)
+            ffn_grads(a_v, pdg, 1, n2h, pn_v, gf[0])
+            for u in sof(fu, 2):
+                u.start_second()
+            for u in sof(fu, 0):
+                u.start_first()
+            ffn_grads(b_v, pdu, 2, n2h, pn_v, gf[1])
+            for u in sof(fu, 1):
+                u.start_first()
+            for u in range(nz):
+                keep(u).wait()
+
+        pl.run_scoped(feed_forward, *[pltpu.VMEM((nz, ff, r), BF16)] * 3)
+        to_o.wait()
+
+        def attention_back(dhb_v, dhbh, n1h, sdk, sdv, hb_v, *ga):
+            G = dict(zip((3, 4, 5, 6), ga))
+            us = fu + units(G)
+            of = lambda *ws: sof(us, *ws)
             dn = acc[0:r, :]
             hv = h_v[...]
             iv = inv_rms(hv)
@@ -766,7 +831,7 @@
             def mixed_grad(w_ref, do_ref):
                 do_ref[...] = dot_nt(dhb_v[...], w_ref[0]).astype(BF16)
 
-            pltpu.emit_pipeline(mixed_grad, grid=(nz,), in_specs=[wrow(cols)], out_specs=[col(r)])(wo, do)
+            piped(mixed_grad, nz, [wrow(cols)], [col(r)])(wo, do)
             for u in of(2):
                 u.start_z()
 
@@ -797,47 +862,22 @@
                 dk_ref[...] = turn(sdk[...] * scale, cos_v[...], -sin_v[...]).astype(BF16)
                 dv_ref[...] = sdv[...].astype(BF16)
 
-            def run_back(lo, n):
-                pltpu.emit_pipeline(
-                    attend_back,
-                    grid=(n,),
-                    in_specs=[head(r, lo), head(rt, lo), head(rt, lo), mem(lo), mem(lo), head(r, lo),
-                              pl.BlockSpec((1, r, 1), lambda h: (h + lo, 0, 0)), head(r, lo)],
-                    out_specs=[head(r, lo), head(rt, lo), head(rt, lo)],
-                )(q, k, v, mk, mv, o, lse, do, dq, dk, dv)
-
-            run_back(0, heads // 2)
-            for m in p_r + ln:
-                m.wait()
-
-            def out_grads(a_ref, b_ref):
-                u = pl.program_id(0)
-                y = (dot_tn(a_ref[...], dhbh[...]) + dot_tn(b_ref[...], pdhb_v[...])).astype(BF16)
-                for e in range(nb):
-                    G[3][e, u] = y[:, e * 128 : (e + 1) * 128]
-
-            pltpu.emit_pipeline(out_grads, grid=(nz,), in_specs=[col(r)] * 2)(o, po)
-            for u in of(3):
-                u.start_first()
-            run_back(heads // 2, heads - heads // 2)
+            piped(
+                attend_back,
+                heads,
+                [head(r), head(rt), head(rt), mem, mem, head(r), row_stat, head(r)],
+                [head(r), head(rt), head(rt)],
+                [(POLL["back_down"], every(of(2), "relay_z")), (POLL["back_gate"], every(of(0), "start_second"))],
+            )(q, k, v, mk, mv, o, lse, do, dq, dk, dv)
             p_att = [to_peer(dq, pdq), to_peer(dk, pdk), to_peer(dv, pdv)]
-            for u in of(0):
-                u.start_second()
             ld.wait()
 
             acc[...] = jnp.zeros_like(acc)
 
-            def project_back(dq_ref, dk_ref, dv_ref, wq_ref, wk_ref, wv_ref):
-                @pl.loop(0, halo + 1)
-                def _(i):
-                    at = pl.ds(pl.multiple_of(i * r, r), r)
-                    acc[at, :] += dot_nt(dk_ref[at, :], wk_ref[...]) + dot_nt(dv_ref[at, :], wv_ref[...])
-
-                acc[halo * r :, :] += dot_nt(dq_ref[...], wq_ref[...])
-
-            pltpu.emit_pipeline(project_back, grid=(nz,), in_specs=[col(r), col(rt), col(rt)] + [wcol] * 3)(
-                dq, dk, dv, wq, wk, wv
-            )
+            def halo_back(dk_ref, dv_ref, wk_ref, wv_ref):
+                acc[: halo * r, :] += dot_nt(dk_ref[...], wk_ref[...]) + dot_nt(dv_ref[...], wv_ref[...])
+
+            piped(halo_back, nz, [col(halo * r)] * 2 + [wcol] * 2)(dk, dv, wk, wv)
             hb_v[...] = acc[: halo * r, :].astype(BF16)
             hd = []
             for j in range(halo):
@@ -851,10 +891,28 @@
 
             for u in of(1):
                 u.start_second()
+
+            def own_back(dq_ref, dk_ref, dv_ref, wq_ref, wk_ref, wv_ref):
+                acc[halo * r :, :] += (
+                    dot_nt(dq_ref[...], wq_ref[...]) + dot_nt(dk_ref[...], wk_ref[...]) + dot_nt(dv_ref[...], wv_ref[...])
+                )
+
+            own_rows = pl.BlockSpec((r, cols), lambda u: (halo, u))
+            piped(own_back, nz, [col(r), own_rows, own_rows] + [wcol] * 3)(dq, dk, dv, wq, wk, wv)
             for u in of(0):
                 u.start_z()
+            for m in p_r + ln:
+                m.wait()
+
+            def out_grads(a_ref, b_ref):
+                u = pl.program_id(0)
+                y = (dot_tn(a_ref[...], dhbh[...]) + dot_tn(b_ref[...], pdhb_v[...])).astype(BF16)
+                for e in range(nb):
+                    G[3][e, u] = y[:, e * 128 : (e + 1) * 128]
+
+            piped(out_grads, nz, [col(r)] * 2)(o, po)
             for u in of(3):
-                u.start_second()
+                u.start_first()
             for m in p_att:
                 m.wait()
 
@@ -868,15 +926,25 @@
                         out[e, u] = y[e * 128 : (e + 1) * 128, :]
 
                 n = p0.shape[0]
-                pltpu.emit_pipeline(body, grid=(nz,), in_specs=[col(n)] * 2)(p0, p1)
+                piped(body, nz, [col(n)] * 2)(p0, p1)
 
             grads_of(G[4], dq, pdq, n1h.at[own], pn1_v.at[own])
+            for u in of(4):
+                u.start_first()
+            for u in of(1):
+                u.start_z()
             grads_of(G[5], dk, pdk, n1h, pn1_v)
-            for u in of(4, 5):
+            for u in of(5):
                 u.start_first()
+            for u in of(0):
+                u.relay_z()
+            for u in of(3):
+                u.start_second()
             grads_of(G[6], dv, pdv, n1h, pn1_v)
             for u in of(6):
                 u.start_first()
+            for u in of(1):
+                u.relay_z()
 
             lx2 = local(x, c_v, 3)
             lx2.wait()
@@ -897,20 +965,15 @@
                 m = send(gp, gz.at[i - 1], ass.at[i - 1], ars.at[i - 1], me, (t + i) % nz)
                 m.start()
                 zg.append(m)
-            for u in of(1):
+            def feed_out(hid_ref, wd_ref):
+                h_v[...] += dot_tn(hid_ref[0], wd_ref[0])
+
+            piped(feed_out, nz, [piece, wrow(ff)])(hid, wd)
+            lo_ = local(h_v, block_out, 5)
+            for u in of(3):
                 u.start_z()
             for u in of(4, 5):
                 u.start_second()
-
-            def feed_out(hid_ref, wd_ref):
-                h_v[...] += dot_tn(hid_ref[0], wd_ref[0])
-
-            pltpu.emit_pipeline(feed_out, grid=(nz,), in_specs=[piece, wrow(ff)])(hid, wd)
-            lo_ = local(h_v, block_out, 5)
-            for u in of(6):
-                u.start_second()
-            for u in of(3):
-                u.start_z()
             for m in zg:
                 m.wait()
             tot = gp[...]
@@ -926,11 +989,10 @@
                 ds_.append(m)
             og = pltpu.make_async_copy(gs.at[me], gd.at[me], dss.at[0])
             og.start()
-            for u in of(4, 5):
-                u.start_z()
-
             lo_.wait()
             ld2 = local(dh_o, h_v, 6)
+            for u in of(6):
+                u.start_second()
             for j, m in enumerate(hd):
 
                 @pl.when(t + j + 1 < nz)
@@ -948,8 +1010,12 @@
             gdx = acc[halo * r :, :] * gain_row(gn_v, 0)
             acc[halo * r :, :] = h_v[...] + iv * gdx - vx * (iv * iv * iv * jnp.mean(vx * gdx, axis=1, keepdims=True))
             lg = local(acc.at[pl.ds(halo * r, r)], grad_in, 7)
-            for u in of(6):
+            for u in of(3):
+                u.relay_z()
+            for u in of(4, 5, 6):
                 u.start_z()
+            for u in of(4, 5, 6):
+                u.relay_z()
             og.wait()
             for m in ds_:
                 m.wait()
@@ -969,9 +1035,9 @@
             pltpu.VMEM((rt, HD), F32),
             pltpu.VMEM((rt, HD), F32),
             pltpu.VMEM((halo * r, d), BF16),
+            *[pltpu.VMEM((nb, nz) + tuple(o_.shape), BF16) for o_ in outs[3:]],
         )
 
-    pieces = [o_.shape for o_ in outs]
     pl.run_scoped(
         rest,
         pltpu.VMEM((r, d), F32),
@@ -980,7 +1046,7 @@
         pltpu.VMEM((r, half), BF16),
         pltpu.VMEM((r, half), BF16),
         pltpu.VMEM((rt, d), F32),
-        *[pltpu.VMEM((nb, nz) + tuple(p), BF16) for p in pieces],
+        *[pltpu.VMEM((nb, nz) + tuple(o_.shape), BF16) for o_ in outs[:3]],
     )
 
 
@@ -1018,7 +1084,7 @@
         [st((d, d))] * 3 + [st((nz, cols, d))] + [st((nz, ff, d))] * 3
         + [st((halo, r, d))] + [st((nz, ksel, blk, cols))] * 2 + [st((dp * cap, blk, cols))] * 2
         + [st((rt, d)), st((r, d)), st((rt, d)), st((rt, d)), st((r, d)), st((heads, r, 1), F32)]
-        + [st((nz, ff, r))] * 8 + [st((r, d)), st((r, d)), st((rt, d)), st((rt, d))]
+        + [st((nz, ff, r))] * 4 + [st((r, d)), st((r, d)), st((rt, d)), st((rt, d))]
         + [st((r, d)), st((rt, d)), st((rt, d)), st((r, d)), st((r, d), F32)]
     )
     out_shape = [st((2, 128), F32)] + [st(p, F32) for p in pieces] + [st((r, d), F32)] * 2 + hbm
@@ -1036,10 +1102,12 @@
     scratch += [pltpu.VMEM((r, half), BF16)] * 2 + [pltpu.VMEM((rt, half), BF16), pltpu.VMEM((r, half), BF16)]
     scratch += [pltpu.VMEM((halo, r, d), BF16)]
     scratch += [pltpu.VMEM((nz - 1, 2, d), F32), pltpu.VMEM((dp, 2, 128), F32), pltpu.VMEM((dp, 2, 128), F32), pltpu.VMEM((2, d), F32)]
-    ncore = 7 + 4 * (dp // 2)
-    scratch += [dma(nsem), dma(nsem), dma(8 + dp // 2), dma(dp), dma(dp), dma(dp), dma(dp), dma(2, dp), dma(2, dp)]
-    scratch += [dma(2, nz), dma(2, nz), dma(halo), dma(halo)]
+    ncore = 4 + 4 * (dp // 2)
+    parts = cols // 128
+    scratch += [dma(nsem), dma(nsem), dma(8 + dp // 2), dma(dp), dma(dp), dma(dp), dma(dp), dma(2, parts, dp), dma(2, parts, dp)]
+    scratch += [dma(2, parts, nz), dma(2, parts, nz), dma(halo), dma(halo)]
     scratch += [dma(ncore), dma(ncore), dma(halo), dma(halo), dma(nz), dma(nz), dma(dp), dma(dp)]
+    scratch += [dma(3, nz), dma(3, nz), dma(nz)]
     cfg = (cap, nq, ksel, halo, window, gunits, sunits)
     return pl.pallas_call(
         functools.partial(layer_kernel, g, cfg),

time: 432 us -> 409 us (0.947)
  Pallas kernels: 413 us -> 389 us
    pallas_call x1, Pallas kernels: 413 us -> 389 us  [run_layer(): pl.pallas_call(functools.partial(layer_kernel, g, cfg), out_shape=out_sha...]
where the time goes in v5:
time: 409 us; the launch traced here: 407 us
  Pallas kernels  389 us (95%)
  local copies, waits for them, and re-layouts  14.4 us (4%)
    pallas_call x1, Pallas kernels, run_layer(): pl.pallas_call(functools.partial(layer_kernel, g, cfg), out_shape=out_sha...  389 us
    unnamed x27, local copies, waits for them, and re-layouts  10.1 us

profile of v5, /device:TPU:0, one launch (start us, length us, event | category | flops | bytes accessed | tf_op | source)
XLA Modules:
  0.0 406.6 jit_solution(10170420381320029856)
XLA Ops:
  1.3 0.8 reshape_squeeze.3
  2.1 0.2 convert_reduce_fusion
  2.3 0.5 multiply_add_fusion.refs_1_
  2.8 1.2 maximum_convert_fusion.refs_7_
  4.0 0.8 pad_dynamic-slice_fusion
  4.8 0.6 copy-done.8
  5.4 0.1 iota_compare_fusion
  5.5 0.1 select_reduce_fusion
  5.6 0.6 broadcast_in_dim.52.refs_0_
  6.2 0.9 copy.30.refs_2_
  7.1 388.8 %layer.1 = (f32[2,128]{1,0:T(2,128)}, f32[704,128]{1,0:T(8,128)}, f32[704,128]{1,0:T(8,128)}, f32[704,128]{1,0:T(8,128)}, f32[256,128]{1,0:T(8,128)}, /*index=5*...) custom-call(s32[8,8,128]{2,1,0:T(8,128)} %broadcast_in_dim.52.refs_0, ...), custom_call_target="tpu_custom_call" | custom-call | tf_op jit(solution)/shard_map/layer/pallas_call | solution.py:1112
  395.8 1.3 slice_bitcast_fusion
  397.1 3.3 copy.41
  400.4 0.0 copy-done
  400.4 0.0 copy-start.4
  400.5 1.3 copy.42
  401.8 0.0 copy-done.7
  401.8 0.7 copy.43
  402.5 0.7 copy.44
  403.1 0.7 copy.45
  403.8 0.7 copy.46
  404.4 0.7 copy.47
  405.2 0.7 copy.48
  405.9 0.7 copy.49
  (17 shorter events, 0.1 us)
Async XLA Ops:
  4.8 0.6 copy-start.8
  397.1 3.3 copy-start
  400.4 1.4 copy-start.7
  400.4 2.0 copy-start.6
  400.4 2.7 copy-start.5
  400.4 3.3 copy-start.4
  400.4 4.0 copy-start.3
  400.5 4.7 %copy-start.2 = (f32[704,128]{1,0:T(8,128)S(1)}, f32[704,128]{1,0:T(8,128)}, u32[]{:S(2)}) copy-start(f32[704,128]{1,0:T(8,128)} %get-tuple-element.29) | copy-start | bytes 1081348
  401.8 4.1 %copy-start.1 = (f32[704,128]{1,0:T(8,128)S(1)}, f32[704,128]{1,0:T(8,128)}, u32[]{:S(2)}) copy-start(f32[704,128]{1,0:T(8,128)} %get-tuple-element.56) | copy-start | bytes 1081348

commit v6 on v5

--- a/solution.py
+++ b/solution.py
@@ -377,7 +377,7 @@
     return (g.na - 1) * g.na + (g.na - 1) + (g.nz - 1)
 
 
-POLL = dict(attend=6, back_down=2, back_gate=5)
+POLL = dict(attend=0, attend_core=6, back_down=2, back_gate=5, own_out=1, own_up=3, out_z=0, out_q=3)
 
 
 def rope_tables(halo, nz, r):
@@ -393,7 +393,7 @@
     cap, nq, ksel, halo, window, gunits, sunits = cfg
     refs = list(refs)
     take = lambda n: [refs.pop(0) for _ in range(n)]
-    requests, sel, seg_q, seg_k, tab1, tab2 = take(6)
+    requests, sel, segs, tab1, tab2 = take(5)
     x, gains, mem_k, mem_v, cot = take(5)
     shards = take(7)
     gout = take(1)[0]
@@ -410,6 +410,7 @@
     gz, gs, gd, gp = take(4)
     ss, rs, ms, qss, qrs, gss, grs, mss, mrs, zss, zrs, xss, xrs = take(13)
     css, crs, hss, hrs, ass, ars, dss, drs, fss, frs, fls = take(11)
+    seg_q, seg_k = take(2)
     a, b, core, t, me = coords(g)
     peer = me + 1 - 2 * core
     r, d = block_out.shape
@@ -553,6 +554,13 @@
         for u in gate_up:
             u.relay_z()
 
+        for j in range(halo + 1):
+            lane_at = pl.multiple_of(jnp.maximum(t - halo + j, 0) * r, 128)
+            part = segs[:, pl.ds(lane_at, r)]
+            seg_k[:, j * r : (j + 1) * r] = jnp.where(t - halo + j >= 0, part, -jnp.ones_like(part))
+        own_seg = segs[:, pl.ds(pl.multiple_of(t * r, 128), r)]
+        seg_q[...] = jnp.transpose(jnp.broadcast_to(own_seg, (128, r)))
+
         left = lax.broadcasted_iota(jnp.int32, (r, HD), 1) < HD // 2
         c1 = tab1[...]
         s1 = pltpu.roll(c1, HD // 2, axis=1)
@@ -676,7 +684,7 @@
             k0 = halo * r - window + i * QT
             ks = slice(k0, k0 + window + QT)
             qq = q_ref[at, :]
-            ok = allowed_of(seg_q[at, :], seg_k[:, ks], halo * r + i * QT, k0)
+            ok = allowed_of(seg_q[at, 0:1], seg_k[:, ks], halo * r + i * QT, k0)
             sl = jnp.where(ok, dot_nt(qq, k_ref[ks, :]), MASKED)
             sm = dot_nt(qq, km)
             mx = jnp.maximum(jnp.max(sl, axis=1, keepdims=True), jnp.max(sm, axis=1, keepdims=True))
@@ -693,7 +701,8 @@
         heads,
         [head(r), head(rt), head(rt), mem, mem],
         [head(r), row_stat],
-        [(POLL["attend"], every(gate_up, "start_second") + every(down, "start_first"))],
+        [(POLL["attend"], every(gate_up, "start_second") + every(down, "start_first")),
+         (POLL["attend_core"], every(gate_up, "start_core"))],
     )(q, k, v, mk, mv, o, lse)
     for u in out_:
         u.finish()
@@ -728,8 +737,6 @@
         p_n = theirs(n2_v, pn_v) + theirs(c_v, pc_v)
         keep_half(n2_v, n2h)
         keep_half(c_v, ch)
-        for u in gate_up:
-            u.start_core()
         for u in gate_up:
             u.finish()
 
@@ -835,6 +842,19 @@
             for u in of(2):
                 u.start_z()
 
+            for m in p_r + ln:
+                m.wait()
+
+            def out_grads(a_ref, b_ref):
+                u = pl.program_id(0)
+                y = (dot_tn(a_ref[...], dhbh[...]) + dot_tn(b_ref[...], pdhb_v[...])).astype(BF16)
+                for e in range(nb):
+                    G[3][e, u] = y[:, e * 128 : (e + 1) * 128]
+
+            piped(out_grads, nz, [col(r)] * 2)(o, po)
+            for u in of(3):
+                u.start_first()
+
             scale = HD**-0.5
 
             def attend_back(q_ref, k_ref, v_ref, mk_ref, mv_ref, o_ref, l_ref, do_ref, dq_ref, dk_ref, dv_ref):
@@ -850,7 +870,7 @@
                     qq, dd = q_ref[at, :], do_ref[at, :]
                     lse_c = l_ref[0, at, :]
                     delta = jnp.sum(dd.astype(F32) * o_ref[at, :].astype(F32), axis=1, keepdims=True)
-                    ok = allowed_of(seg_q[at, :], seg_k[:, ks], halo * r + i * QT, k0)
+                    ok = allowed_of(seg_q[at, 0:1], seg_k[:, ks], halo * r + i * QT, k0)
                     pm = jnp.exp2(dot_nt(qq, km) * C2 - lse_c)
                     dsm = (pm * (dot_nt(dd, vm) - delta)).astype(BF16)
                     plo = jnp.where(ok, jnp.exp2(dot_nt(qq, k_ref[ks, :]) * C2 - lse_c), 0.0)
@@ -892,27 +912,6 @@
             for u in of(1):
                 u.start_second()
 
-            def own_back(dq_ref, dk_ref, dv_ref, wq_ref, wk_ref, wv_ref):
-                acc[halo * r :, :] += (
-                    dot_nt(dq_ref[...], wq_ref[...]) + dot_nt(dk_ref[...], wk_ref[...]) + dot_nt(dv_ref[...], wv_ref[...])
-                )
-
-            own_rows = pl.BlockSpec((r, cols), lambda u: (halo, u))
-            piped(own_back, nz, [col(r), own_rows, own_rows] + [wcol] * 3)(dq, dk, dv, wq, wk, wv)
-            for u in of(0):
-                u.start_z()
-            for m in p_r + ln:
-                m.wait()
-
-            def out_grads(a_ref, b_ref):
-                u = pl.program_id(0)
-                y = (dot_tn(a_ref[...], dhbh[...]) + dot_tn(b_ref[...], pdhb_v[...])).astype(BF16)
-                for e in range(nb):
-                    G[3][e, u] = y[:, e * 128 : (e + 1) * 128]
-
-            piped(out_grads, nz, [col(r)] * 2)(o, po)
-            for u in of(3):
-                u.start_first()
             for m in p_att:
                 m.wait()
 
@@ -931,22 +930,34 @@
             grads_of(G[4], dq, pdq, n1h.at[own], pn1_v.at[own])
             for u in of(4):
                 u.start_first()
-            for u in of(1):
-                u.start_z()
             grads_of(G[5], dk, pdk, n1h, pn1_v)
             for u in of(5):
                 u.start_first()
-            for u in of(0):
-                u.relay_z()
-            for u in of(3):
-                u.start_second()
             grads_of(G[6], dv, pdv, n1h, pn1_v)
             for u in of(6):
                 u.start_first()
-            for u in of(1):
+            for u in of(0):
+                u.start_z()
+
+            def own_back(dq_ref, dk_ref, dv_ref, wq_ref, wk_ref, wv_ref):
+                acc[halo * r :, :] += (
+                    dot_nt(dq_ref[...], wq_ref[...]) + dot_nt(dk_ref[...], wk_ref[...]) + dot_nt(dv_ref[...], wv_ref[...])
+                )
+
+            own_rows = pl.BlockSpec((r, cols), lambda u: (halo, u))
+            lx2 = local(x, c_v, 3)
+            piped(
+                own_back,
+                nz,
+                [col(r), own_rows, own_rows] + [wcol] * 3,
+                (),
+                [(POLL["own_out"], every(of(3), "start_second")), (POLL["own_up"], every(of(1), "start_z"))],
+            )(dq, dk, dv, wq, wk, wv)
+            for u in of(0):
                 u.relay_z()
-
-            lx2 = local(x, c_v, 3)
+            for u in of(2):
+                u.finish()
+
             lx2.wait()
             vx = c_v[...].astype(F32)
             gp[0:1, :] = jnp.sum(acc[halo * r :, :] * vx * inv_rms(vx), axis=0, keepdims=True)
@@ -965,15 +976,21 @@
                 m = send(gp, gz.at[i - 1], ass.at[i - 1], ars.at[i - 1], me, (t + i) % nz)
                 m.start()
                 zg.append(m)
+
             def feed_out(hid_ref, wd_ref):
                 h_v[...] += dot_tn(hid_ref[0], wd_ref[0])
 
-            piped(feed_out, nz, [piece, wrow(ff)])(hid, wd)
+            piped(
+                feed_out,
+                nz,
+                [piece, wrow(ff)],
+                (),
+                [(POLL["out_z"], every(of(1), "relay_z") + every(of(3), "start_z")),
+                 (POLL["out_q"], every(of(4, 5), "start_second"))],
+            )(hid, wd)
             lo_ = local(h_v, block_out, 5)
-            for u in of(3):
-                u.start_z()
-            for u in of(4, 5):
-                u.start_second()
+            for u in of(0):
+                u.finish()
             for m in zg:
                 m.wait()
             tot = gp[...]
@@ -993,6 +1010,11 @@
             ld2 = local(dh_o, h_v, 6)
             for u in of(6):
                 u.start_second()
+            for u in of(3):
+                u.relay_z()
+            for u in of(4, 5):
+                u.start_z()
+
             for j, m in enumerate(hd):
 
                 @pl.when(t + j + 1 < nz)
@@ -1005,17 +1027,17 @@
                     m.wait_send()
 
             ld2.wait()
+            for u in of(6):
+                u.start_z()
             vx = c_v[...].astype(F32)
             iv = inv_rms(vx)
             gdx = acc[halo * r :, :] * gain_row(gn_v, 0)
             acc[halo * r :, :] = h_v[...] + iv * gdx - vx * (iv * iv * iv * jnp.mean(vx * gdx, axis=1, keepdims=True))
             lg = local(acc.at[pl.ds(halo * r, r)], grad_in, 7)
-            for u in of(3):
-                u.relay_z()
-            for u in of(4, 5, 6):
-                u.start_z()
             for u in of(4, 5, 6):
                 u.relay_z()
+            for u in of(1, 3):
+                u.finish()
             og.wait()
             for m in ds_:
                 m.wait()
@@ -1023,7 +1045,7 @@
             for e in range(1, dp):
                 tot = tot + gd[e]
             gout[...] = tot
-            for u in us:
+            for u in of(4, 5, 6):
                 u.finish()
             lg.wait()
 
@@ -1050,7 +1072,7 @@
     )
 
 
-def run_layer(g, cap, halo, window, requests, sel, seg_q, seg_k, x, gains, mem_k, mem_v, cot, shards, nq, ksel):
+def run_layer(g, cap, halo, window, requests, sel, segs, x, gains, mem_k, mem_v, cot, shards, nq, ksel):
     blk, cols = mem_k.shape[1:]
     r, d = x.shape
     rt = (halo + 1) * r
@@ -1108,16 +1130,48 @@
     scratch += [dma(2, parts, nz), dma(2, parts, nz), dma(halo), dma(halo)]
     scratch += [dma(ncore), dma(ncore), dma(halo), dma(halo), dma(nz), dma(nz), dma(dp), dma(dp)]
     scratch += [dma(3, nz), dma(3, nz), dma(nz)]
+    scratch += [pltpu.VMEM((r, 128), jnp.int32), pltpu.VMEM((1, rt), jnp.int32)]
     cfg = (cap, nq, ksel, halo, window, gunits, sunits)
     return pl.pallas_call(
         functools.partial(layer_kernel, g, cfg),
         out_shape=out_shape,
-        in_specs=[vm, pl.BlockSpec(memory_space=pltpu.SMEM), vm, vm, vm, vm] + [any_] * (5 + len(shards)),
+        in_specs=[vm, pl.BlockSpec(memory_space=pltpu.SMEM), vm, vm, vm] + [any_] * (5 + len(shards)),
         out_specs=[vm] * 8 + [any_] * (2 + len(hbm)),
         scratch_shapes=scratch,
         compiler_params=pltpu.CompilerParams(collective_id=0, has_side_effects=True, vmem_limit_bytes=67043328),
         name="layer",
-    )(requests, sel, seg_q, seg_k, tab1, tab2, x, gains, mem_k, mem_v, cot, *shards)
+    )(requests, sel, segs, tab1, tab2, x, gains, mem_k, mem_v, cot, *shards)
+
+
+def hand_out(gout, arrays):
+    n = len(arrays)
+
+    def kern(*refs):
+        ins, outs, bufs, (ls, ss) = refs[: n + 1], refs[n + 1 : 2 * n + 3], refs[2 * n + 3 : 3 * n + 3], refs[3 * n + 3 :]
+        loads = [pltpu.make_async_copy(ins[i + 1], bufs[i], ls.at[i]) for i in range(n)]
+        stores = [pltpu.make_async_copy(bufs[i], outs[i + 2], ss.at[i]) for i in range(n)]
+        for m in loads:
+            m.start()
+        outs[0][...] = ins[0][0:1, :]
+        outs[1][...] = ins[0][1:2, :]
+        for a, b in zip(loads, stores):
+            a.wait()
+            b.start()
+        for m in stores:
+            m.wait()
+
+    any_ = pl.BlockSpec(memory_space=pl.ANY)
+    vm = pl.BlockSpec(memory_space=pltpu.VMEM)
+    gain = jax.ShapeDtypeStruct((1, 128), F32)
+    return pl.pallas_call(
+        kern,
+        in_specs=[vm] + [any_] * n,
+        out_specs=[vm] * 2 + [any_] * n,
+        out_shape=[gain, gain] + [jax.ShapeDtypeStruct(a.shape, a.dtype) for a in arrays],
+        scratch_shapes=[pltpu.VMEM(a.shape, a.dtype) for a in arrays] + [pltpu.SemaphoreType.DMA((n,))] * 2,
+        compiler_params=pltpu.CompilerParams(vmem_limit_bytes=67043328),
+        name="hand_out",
+    )(gout, *arrays)
 
 
 HEADS = 8
@@ -1453,14 +1507,14 @@
     gains = jnp.stack([gain_attn, gain_ffn]).astype(F32)
     flat = lambda m: m.reshape((-1,) + m.shape[2:])
     shards = [w_query, w_key, w_value, w_out, w_gate.T, w_up.T, w_down]
-    padded = jnp.concatenate([jnp.full((halo * r,), -1, jnp.int32), segments[0]])
-    seg = lax.dynamic_slice(padded, (t * r,), ((halo + 1) * r,))
-    seg_k, seg_q = seg[None, :], seg[halo * r :, None]
     gout, o_gate, o_up, o_down, o_out, o_q, o_k, o_v, block_out, grad_in = run_layer(
-        g, cap, halo, window, req, sel, seg_q, seg_k, x, gains, flat(memory_keys), flat(memory_values), c, shards, nq, ksel
+        g, cap, halo, window, req, sel, segments, x, gains, flat(memory_keys), flat(memory_values), c, shards, nq, ksel
     )[:10]
+    g_attn, g_ffn, block_out, grad_in, o_q, o_k, o_v, o_out, o_gate, o_up, o_down = hand_out(
+        gout, (block_out, grad_in, o_q, o_k, o_v, o_out, o_gate, o_up, o_down)
+    )
     return (
-        block_out[None], grad_in[None], gout[0], o_q, o_k, o_v, o_out, gout[1], o_gate.T, o_up.T, o_down,
+        block_out[None], grad_in[None], g_attn.reshape(-1), o_q, o_k, o_v, o_out, g_ffn.reshape(-1), o_gate.T, o_up.T, o_down,
     )
 
 

time: 409 us -> 393 us (0.961)
  local copies, waits for them, and re-layouts: 14.4 us -> 1.38 us
    unnamed x27 -> x0, local copies, waits for them, and re-layouts: 10.1 us -> none
    pallas_call x1, Pallas kernels: 389 us -> 382 us  [run_layer(): pl.pallas_call(functools.partial(layer_kernel, g, cfg), out_shape=out_sha...]
    pallas_call x0 -> x1, Pallas kernels: none -> 5.39 us  [hand_out(): pl.pallas_call(kern, in_specs=[vm] + [any_] * n, out_specs=[vm] * 2 + [an...]
where the time goes in v6:
time: 393 us; the launch traced here: 392 us
  Pallas kernels  387 us (98%)
    pallas_call x1, Pallas kernels, run_layer(): pl.pallas_call(functools.partial(layer_kernel, g, cfg), out_shape=out_sha...  382 us

profile of v6, /device:TPU:0, one launch (start us, length us, event | category | flops | bytes accessed | tf_op | source)
XLA Modules:
  0.0 392.1 jit_solution(4910828122428910479)
XLA Ops:
  1.3 0.8 reshape_squeeze.3
  2.1 0.2 convert_reduce_fusion
  2.3 0.5 multiply_add_fusion.refs_1_
  2.8 1.2 maximum_convert_fusion.refs_6_
  4.0 0.1 iota_compare_fusion
  4.1 0.1 select_reduce_fusion
  4.2 0.6 broadcast_in_dim.45.refs_0_
  4.8 381.7 %layer.1 = (f32[2,128]{1,0:T(2,128)}, f32[704,128]{1,0:T(8,128)}, f32[704,128]{1,0:T(8,128)}, f32[704,128]{1,0:T(8,128)}, f32[256,128]{1,0:T(8,128)}, /*index=5*...) custom-call(s32[8,8,128]{2,1,0:T(8,128)} %broadcast_in_dim.45.refs_0, ...), custom_call_target="tpu_custom_call" | custom-call | tf_op jit(solution)/shard_map/layer/pallas_call | solution.py:1135
  386.6 5.4 %hand_out.1 = (f32[1,128]{1,0:T(1,128)}, f32[1,128]{1,0:T(1,128)}, f32[512,1024]{1,0:T(8,128)}, f32[512,1024]{1,0:T(8,128)}, f32[128,256]{1,0:T(8,128)}, /*index...) custom-call(f32[2,128]{1,0:T(2,128)} %get-tuple-element.32.refs_0_, ...), custom_call_target="tpu_custom_call" | custom-call | tf_op jit(solution)/shard_map/hand_out/pallas_call | solution.py:1166
  (2 shorter events, 0.0 us)

commit v7 on v6

--- a/solution.py
+++ b/solution.py
@@ -377,7 +377,7 @@
     return (g.na - 1) * g.na + (g.na - 1) + (g.nz - 1)
 
 
-POLL = dict(attend=0, attend_core=6, back_down=2, back_gate=5, own_out=1, own_up=3, out_z=0, out_q=3)
+POLL = dict(hidden_back=2, attend=0, attend_core=6, back_down=2, back_gate=5, own_up=3)
 
 
 def rope_tables(halo, nz, r):
@@ -741,14 +741,14 @@
             u.finish()
 
         def feed_forward(hid_v, a_v, b_v):
-            tile = ff // 2
+            tile = ff
             give = lambda src, dst, i, u: send(src.at[u], dst.at[u], fss.at[i, u], frs.at[i, u], peer, t)
             keep = lambda u: pltpu.make_async_copy(hid_v.at[u], hid.at[u], fls.at[u])
 
             def hidden(wg_ref, wu_ref):
                 u = pl.program_id(0)
 
-                @pl.loop(0, 2)
+                @pl.loop(0, 1)
                 def _(i):
                     at = pl.ds(pl.multiple_of(i * tile, 16), tile)
                     gate = dot_nt(wg_ref[0, at, :], n2_v[...])
@@ -792,7 +792,7 @@
             def hidden_back(wd_ref, wg_ref, wu_ref):
                 u = pl.program_id(0)
 
-                @pl.loop(0, 2)
+                @pl.loop(0, 1)
                 def _(i):
                     at = pl.ds(pl.multiple_of(i * tile, 16), tile)
                     dhid = dot_nt(wd_ref[0, at, :], c_v[...])
@@ -803,10 +803,8 @@
                 give(b_v, pdu, 2, u).start()
                 acc[0:r, :] += dot_tn(a_v[u], wg_ref[0]) + dot_tn(b_v[u], wu_ref[0])
 
-            piped(hidden_back, nz, [wrow(ff)] * 3)(wd, wg, wu)
+            piped(hidden_back, nz, [wrow(ff)] * 3, (), [(POLL["hidden_back"], every(sof(fu, 2), "start_second"))])(wd, wg, wu)
             ffn_grads(a_v, pdg, 1, n2h, pn_v, gf[0])
-            for u in sof(fu, 2):
-                u.start_second()
             for u in sof(fu, 0):
                 u.start_first()
             ffn_grads(b_v, pdu, 2, n2h, pn_v, gf[1])
@@ -912,6 +910,11 @@
             for u in of(1):
                 u.start_second()
 
+            def feed_out(hid_ref, wd_ref):
+                h_v[...] += dot_tn(hid_ref[0], wd_ref[0])
+
+            piped(feed_out, nz, [piece, wrow(ff)])(hid, wd)
+            lo_ = local(h_v, block_out, 5)
             for m in p_att:
                 m.wait()
 
@@ -936,8 +939,12 @@
             grads_of(G[6], dv, pdv, n1h, pn1_v)
             for u in of(6):
                 u.start_first()
+            for u in of(3):
+                u.start_second()
             for u in of(0):
                 u.start_z()
+            lo_.wait()
+            ld2 = local(dh_o, h_v, 6)
 
             def own_back(dq_ref, dk_ref, dv_ref, wq_ref, wk_ref, wv_ref):
                 acc[halo * r :, :] += (
@@ -951,7 +958,7 @@
                 nz,
                 [col(r), own_rows, own_rows] + [wcol] * 3,
                 (),
-                [(POLL["own_out"], every(of(3), "start_second")), (POLL["own_up"], every(of(1), "start_z"))],
+                [(POLL["own_up"], every(of(1), "start_z"))],
             )(dq, dk, dv, wq, wk, wv)
             for u in of(0):
                 u.relay_z()
@@ -976,21 +983,30 @@
                 m = send(gp, gz.at[i - 1], ass.at[i - 1], ars.at[i - 1], me, (t + i) % nz)
                 m.start()
                 zg.append(m)
-
-            def feed_out(hid_ref, wd_ref):
-                h_v[...] += dot_tn(hid_ref[0], wd_ref[0])
-
-            piped(
-                feed_out,
-                nz,
-                [piece, wrow(ff)],
-                (),
-                [(POLL["out_z"], every(of(1), "relay_z") + every(of(3), "start_z")),
-                 (POLL["out_q"], every(of(4, 5), "start_second"))],
-            )(hid, wd)
-            lo_ = local(h_v, block_out, 5)
-            for u in of(0):
-                u.finish()
+            for u in of(3):
+                u.start_z()
+
+            for j, m in enumerate(hd):
+
+                @pl.when(t + j + 1 < nz)
+                def _():
+                    m.wait_recv()
+                    acc[halo * r :, :] = acc[halo * r :, :] + more[j].astype(F32)
+
+                @pl.when(t >= j + 1)
+                def _():
+                    m.wait_send()
+
+            ld2.wait()
+            vx = c_v[...].astype(F32)
+            iv = inv_rms(vx)
+            gdx = acc[halo * r :, :] * gain_row(gn_v, 0)
+            acc[halo * r :, :] = h_v[...] + iv * gdx - vx * (iv * iv * iv * jnp.mean(vx * gdx, axis=1, keepdims=True))
+            lg = local(acc.at[pl.ds(halo * r, r)], grad_in, 7)
+            for u in of(4, 5):
+                u.start_second()
+            for u in of(1):
+                u.relay_z()
             for m in zg:
                 m.wait()
             tot = gp[...]
@@ -1006,38 +1022,24 @@
                 ds_.append(m)
             og = pltpu.make_async_copy(gs.at[me], gd.at[me], dss.at[0])
             og.start()
-            lo_.wait()
-            ld2 = local(dh_o, h_v, 6)
             for u in of(6):
                 u.start_second()
             for u in of(3):
                 u.relay_z()
+            for u in of(0):
+                u.finish()
             for u in of(4, 5):
                 u.start_z()
-
-            for j, m in enumerate(hd):
-
-                @pl.when(t + j + 1 < nz)
-                def _():
-                    m.wait_recv()
-                    acc[halo * r :, :] = acc[halo * r :, :] + more[j].astype(F32)
-
-                @pl.when(t >= j + 1)
-                def _():
-                    m.wait_send()
-
-            ld2.wait()
+            for u in of(1):
+                u.finish()
             for u in of(6):
                 u.start_z()
-            vx = c_v[...].astype(F32)
-            iv = inv_rms(vx)
-            gdx = acc[halo * r :, :] * gain_row(gn_v, 0)
-            acc[halo * r :, :] = h_v[...] + iv * gdx - vx * (iv * iv * iv * jnp.mean(vx * gdx, axis=1, keepdims=True))
-            lg = local(acc.at[pl.ds(halo * r, r)], grad_in, 7)
-            for u in of(4, 5, 6):
+            for u in of(4, 5):
                 u.relay_z()
-            for u in of(1, 3):
+            for u in of(3):
                 u.finish()
+            for u in of(6):
+                u.relay_z()
             og.wait()
             for m in ds_:
                 m.wait()

time: 393 us -> 392 us (level)
  no operation moved by 1% of the time
where the time goes in v7:
time: 392 us; the launch traced here: 391 us
  Pallas kernels  386 us (98%)
    pallas_call x1, Pallas kernels, run_layer(): pl.pallas_call(functools.partial(layer_kernel, g, cfg), out_shape=out_sha...  380 us

profile of v7, /device:TPU:0, one launch (start us, length us, event | category | flops | bytes accessed | tf_op | source)
XLA Modules:
  0.0 390.8 jit_solution(13327744452419416709)
XLA Ops:
  1.3 0.8 reshape_squeeze.3
  2.1 0.2 convert_reduce_fusion
  2.3 0.5 multiply_add_fusion.refs_1_
  2.8 1.2 maximum_convert_fusion.refs_6_
  4.0 0.1 iota_compare_fusion
  4.1 0.1 select_reduce_fusion
  4.2 0.6 broadcast_in_dim.45.refs_0_
  4.8 380.4 %layer.1 = (f32[2,128]{1,0:T(2,128)}, f32[704,128]{1,0:T(8,128)}, f32[704,128]{1,0:T(8,128)}, f32[704,128]{1,0:T(8,128)}, f32[256,128]{1,0:T(8,128)}, /*index=5*...) custom-call(s32[8,8,128]{2,1,0:T(8,128)} %broadcast_in_dim.45.refs_0, ...), custom_call_target="tpu_custom_call" | custom-call | tf_op jit(solution)/shard_map/layer/pallas_call | solution.py:1137
  385.2 5.4 %hand_out.1 = (f32[1,128]{1,0:T(1,128)}, f32[1,128]{1,0:T(1,128)}, f32[512,1024]{1,0:T(8,128)}, f32[512,1024]{1,0:T(8,128)}, f32[128,256]{1,0:T(8,128)}, /*index...) custom-call(f32[2,128]{1,0:T(2,128)} %get-tuple-element.32.refs_0_, ...), custom_call_target="tpu_custom_call" | custom-call | tf_op jit(solution)/shard_map/hand_out/pallas_call | solution.py:1168
  (2 shorter events, 0.0 us)
